TPU v7x, 512 devices: a whole 4x4x16 slice. The times are simulated.
512 devices in a mesh: tm: 16 (over y, x_lo, core), expert: 32 (over x_hi, z).
Axes of the slice: x: 4 (x_hi: 2, x_lo: 2; x = x_hi * 2 + x_lo), y: 4, z: 16, core: 2. Of those that a mesh axis runs over, the one named last changes fastest.
Arguments:
- latents: bfloat16 [32, 2048, 1024], P('expert', 'tm'), may hold values from -16 to 16
- queries: bfloat16 [32, 2048, 1024], P('expert', 'tm'), may hold values from -6 to 6
- keys: bfloat16 [32, 2048, 1024], P('expert', 'tm'), may hold values from -6 to 6
- values: bfloat16 [32, 2048, 1024], P('expert', 'tm'), may hold values from -8 to 8
- inpaint_mask: int32 [32, 2048], P('expert', 'tm'), may hold values 0 or 1
- key_bias: bfloat16 [16], replicated, may hold values from -3 to 3
- out_weight: bfloat16 [1024, 1024], replicated, may hold values from -0.1875 to 0.1875
- modulation: float32 [32, 2, 1024], P('expert'), may hold values from -3 to 3
- branch_gates: float32 [32, 2, 1024], P('expert'), may hold values from 0.5 to 1.5
- expert_ids: int32 [32, 2048, 2], P('expert', 'tm'), may hold values from 0 to 31, as said below
- gate_values: float32 [32, 2048, 2], P('expert', 'tm'), may hold values from 0.2 to 1
- up_weight: bfloat16 [32, 1024, 1024], P('expert', None, 'tm'), may hold values from -0.1875 to 0.1875
- down_weight: bfloat16 [32, 1024, 1024], P('expert', 'tm'), may hold values from -0.1875 to 0.1875
Outputs:
- layer_out: bfloat16 [32, 2048, 1024], P('expert', 'tm')
Inputs may be any that keep to these rules, and one draw needn't show every extreme that they name: `expert_ids`: A token's two ids differ. Within each device's block of 128 positions of one clip, no id is named more than 16 times, and one id is named exactly 16 times; that id is the same for all clips at the same block position.
All inputs are finite; a program needn't handle non-finite values. No bound on the sum of `inpaint_mask` on one device may be relied on, other than what follows from the above.
Results may differ from a plain program's by a relative error of at most 0.01.
Values may be sent and summed in bfloat16 or wider, within the bound.
A program may use at most 128 MiB of HBM per device.

v0:
```python
import jax
import jax.numpy as jnp
from jax import lax
from jax.sharding import PartitionSpec as P

eps = 1e-06
block_rows = 512


def key_block(carried, query_first, key_rows, value_rows, offset_rows):
    running_max, running_sum, weighted = carried
    key_first = jnp.transpose(key_rows, (1, 0, 2))
    value_first = jnp.transpose(value_rows, (1, 0, 2))
    scores = jnp.einsum("hqd,hkd->hqk", query_first, key_first, preferred_element_type=jnp.float32)
    scores = scores + jnp.transpose(offset_rows.astype(jnp.float32))[:, None, :]
    new_max = jnp.maximum(running_max, jnp.max(scores, axis=2))
    factor = jnp.exp(running_max - new_max)
    unscaled = jnp.exp(scores - new_max[:, :, None])
    running_sum = running_sum * factor + jnp.sum(unscaled, axis=2)
    weighted = weighted * factor[:, :, None] + jnp.einsum(
        "hqk,hkd->hqd",
        unscaled.astype(jnp.bfloat16),
        value_first,
        preferred_element_type=jnp.float32,
    )
    return (new_max, running_sum, weighted)


def layer_norm(mixed, shift_row, scale_row):
    center = jnp.mean(mixed, axis=-1, keepdims=True)
    deviation = mixed - center
    variance = jnp.mean(deviation * deviation, axis=-1, keepdims=True)
    return deviation * lax.rsqrt(variance + eps) * (1.0 + scale_row) + shift_row


def on_device(
    latents,
    queries,
    keys,
    values,
    inpaint_mask,
    key_bias,
    out_weight,
    modulation,
    branch_gates,
    expert_ids,
    gate_values,
    up_weight,
    down_weight,
):
    tok_rows = latents.shape[1]
    model_width = latents.shape[2]
    head_count = key_bias.shape[0]
    head_width = model_width // head_count
    score_scale = head_width ** (-0.5)
    scaled_queries = queries[0] * jnp.asarray(score_scale, jnp.bfloat16)
    query_heads = scaled_queries.reshape(tok_rows, head_count, head_width)
    key_heads = keys[0].reshape(tok_rows, head_count, head_width)
    value_heads = values[0].reshape(tok_rows, head_count, head_width)
    offsets = jnp.where(
        inpaint_mask[0][:, None] == 1, key_bias[None, :], jnp.zeros((), jnp.bfloat16)
    )
    full_up, full_down = (
        lax.all_gather(up_weight, "tm", axis=2, tiled=True),
        lax.all_gather(down_weight, "tm", axis=1, tiled=True),
    )
    query_first = jnp.transpose(query_heads, (1, 0, 2))
    initial = (
        jnp.full((head_count, tok_rows), -1e30, jnp.float32),
        jnp.zeros((head_count, tok_rows), jnp.float32),
        jnp.zeros((head_count, tok_rows, head_width), jnp.float32),
    )
    carried = initial
    key_part = lax.all_gather(key_heads, "tm", axis=0, tiled=True)
    value_part = lax.all_gather(value_heads, "tm", axis=0, tiled=True)
    offset_part = lax.all_gather(offsets, "tm", axis=0, tiled=True)
    row_count = key_part.shape[0]
    for first_row in range(0, row_count, block_rows):
        last_row = min(row_count, first_row + block_rows)
        carried = key_block(
            carried,
            query_first,
            key_part[first_row:last_row],
            value_part[first_row:last_row],
            offset_part[first_row:last_row],
        )
    running_max, running_sum, weighted = carried
    attended = jnp.transpose(weighted / running_sum[:, :, None], (1, 0, 2)).astype(jnp.bfloat16)
    projected = jnp.dot(
        attended.reshape(tok_rows, model_width), out_weight, preferred_element_type=jnp.float32
    )
    mixed = latents[0].astype(jnp.float32) + branch_gates[0, 0][None, :] * projected
    normed = layer_norm(mixed, modulation[0, 0][None, :], modulation[0, 1][None, :]).astype(
        jnp.bfloat16
    )
    local_experts = up_weight.shape[0]
    source_count = lax.axis_size("expert")
    expert_count = local_experts * source_count
    capacity = 4 * tok_rows // expert_count
    choice_list = expert_ids[0].reshape(2 * tok_rows)
    hits = (choice_list[:, None] == jnp.arange(expert_count, dtype=jnp.int32)[None, :]).astype(
        jnp.int32
    )
    ranks = jnp.sum((jnp.cumsum(hits, axis=0) - 1) * hits, axis=1)
    target = ranks * expert_count + choice_list
    placing = (
        jnp.arange(capacity * expert_count, dtype=jnp.int32)[:, None] == target[None, :]
    ).astype(jnp.bfloat16)
    doubled = jnp.repeat(normed, 2, axis=0)
    slots = jnp.dot(placing, doubled, preferred_element_type=jnp.float32).astype(jnp.bfloat16)
    slots = slots.reshape(capacity, expert_count, model_width)
    arrived = lax.all_to_all(slots, "expert", split_axis=1, concat_axis=1, tiled=True)
    slot_count = arrived.shape[0]
    grouped = arrived.reshape(slot_count, source_count, local_experts, model_width)
    hidden = jax.nn.gelu(
        jnp.einsum("csed,edf->csef", grouped, full_up, preferred_element_type=jnp.float32),
        approximate=True,
    ).astype(jnp.bfloat16)
    produced = jnp.einsum(
        "csef,efd->csed", hidden, full_down, preferred_element_type=jnp.float32
    ).astype(jnp.bfloat16)
    produced = produced.reshape(slot_count, source_count * local_experts, model_width)
    returned = lax.all_to_all(produced, "expert", split_axis=1, concat_axis=1, tiled=True)
    picked = jnp.einsum(
        "sa,sd->ad",
        placing,
        returned.reshape(capacity * expert_count, model_width),
        preferred_element_type=jnp.float32,
    )
    picked = picked.reshape(tok_rows, 2, model_width)
    combined = jnp.sum(gate_values[0][:, :, None] * picked, axis=1)
    layer_out = (mixed + branch_gates[0, 1][None, :] * combined).astype(jnp.bfloat16)
    return layer_out[None]


def solution(mesh):
    placed = (
        P("expert", "tm", None),
        P("expert", "tm", None),
        P("expert", "tm", None),
        P("expert", "tm", None),
        P("expert", "tm"),
        P(),
        P(),
        P("expert", None, None),
        P("expert", None, None),
        P("expert", "tm", None),
        P("expert", "tm", None),
        P("expert", None, "tm"),
        P("expert", "tm", None),
    )
    return jax.shard_map(
        on_device, mesh=mesh, in_specs=placed, out_specs=P("expert", "tm", None), check_vma=False
    )
```

profile of v0, /device:TPU:32, one launch (start us, length us, event | category | flops | bytes accessed | tf_op | source)
XLA Modules:
  0.0 301.7 jit_solution(3586965806504751508)
XLA Ops:
  6.5 1.9 copy.27
  8.6 1.8 copy.28
  11.1 0.8 copy.29
  12.8 0.7 broadcast_select_fusion
  13.6 20.1 %all_gather.16 = bf16[2048,16]{0,1:T(8,128)(2,1)S(1)} all-gather(bf16[128,16]{0,1:T(8,128)(2,1)S(1)} %broadcast_select_fusion), channel_id=1, replica_groups=mesh['tm'=16,'expert'=32] {'tm'}, dimensions={0}, use_global_device_ids=true | all-gather | bytes 69632 | tf_op jit(solution)/shard_map/all_gather | solution.py:76
  33.7 1.1 copy.26
  34.8 0.8 fusion.115
  35.6 0.8 slice_add_fusion
  37.4 29.1 %all-gather.5.cloned.1.call-done = bf16[2048,16,64]{0,2,1:T(8,128)(2,1)} async-done(((bf16[128,16,64]{0,2,1:T(8,128)(2,1)}), bf16[2048,16,64]{0,2,1:T(8,128)(2,1)}) %all-gather.5.cloned.1.call-update) | async-done | bytes 4194320 | tf_op jit(solution)/shard_map/all_gather | solution.py:74
  66.4 2.2 add_reduce_fusion
  68.9 0.8 add_reduce_fusion.1
  69.8 0.8 add_reduce_fusion.2
  70.6 0.8 add_reduce_fusion.3
  71.5 2.4 fusion
  74.4 2.4 fusion.4
  76.8 44.9 %all-gather.7.cloned.1.call-done = bf16[2048,16,64]{0,2,1:T(8,128)(2,1)} async-done(((bf16[128,16,64]{0,2,1:T(8,128)(2,1)}), bf16[2048,16,64]{0,2,1:T(8,128)(2,1)}) %all-gather.7.cloned.1.call-update) | async-done | bytes 4194320 | tf_op jit(solution)/shard_map/all_gather | solution.py:75
  121.7 3.6 %fusion.76 = f32[128,16,64]{0,2,1:T(8,128)S(1)} fusion(f32[16,128,512]{2,1,0:T(8,128)} %copy-done.5, f32[16,128]{1,0:T(8,128)S(1)} %get-tuple-element.21, f32[16,512]{1,0:T(8,128)S(1)} %get-tuple-element.14, bf16[2048,16,64]{0,2,1:T(8,128)(2,1)} %all-gather.7.cloned.1.call-done, f32[128,16]{0,1:T(8,128)S(1)} %get-tuple-element.15, ...), kind=kOutput, calls=%fused_computation.58 | convolution fusion | flops 137625600 | bytes 5824512 | tf_op jit(solution)/shard_map/hqk,hkd->hqd/dot_general | solution.py:20
  125.5 2.4 fusion.70
  127.9 2.4 fusion.64
  130.4 2.3 fusion.82
  133.9 1.0 reshape.204
  134.9 1.5 convolution_convert_fusion
  136.4 1.6 copy.32
  137.9 15.0 %all-to-all-start = ((bf16[16,32,1024]{2,0,1:T(8,128)(2,1)}), bf16[16,32,1024]{2,0,1:T(8,128)(2,1)}, u32[]{:S(2)}, u32[]{:S(2)}) async-start(bf16[16,32,1024]{2,0,1:T(8,128)(2,1)} %copy.32), calls=%async_computation | async-start | bytes 2097152 | tf_op jit(solution)/shard_map/all_to_all | solution.py:112
  153.5 12.9 %all-gather.11.cloned.1.call-done = bf16[1,1024,1024]{2,1,0:T(8,128)(2,1)} async-done(((bf16[1,64,1024]{2,1,0:T(8,128)(2,1)}), bf16[1,1024,1024]{2,1,0:T(8,128)(2,1)}) %all-gather.11.cloned.1.call-update) | async-done | bytes 2097168 | tf_op jit(solution)/shard_map/all_gather | solution.py:65
  166.4 44.3 %all-gather.9.cloned.1.call-done = bf16[1,1024,1024]{1,2,0:T(8,128)(2,1)} async-done(((bf16[1,1024,64]{1,2,0:T(8,128)(2,1)}), bf16[1,1024,1024]{1,2,0:T(8,128)(2,1)}) %all-gather.9.cloned.1.call-update) | async-done | bytes 2097168 | tf_op jit(solution)/shard_map/all_gather | solution.py:64
  210.8 6.2 %fusion.38 = bf16[16,32,1024]{2,1,0:T(8,128)(2,1)} fusion(bf16[1,1024,1024]{2,1,0:T(8,128)(2,1)} %all-gather.11.cloned.1.call-done, bf16[1,1024,1024]{1,2,0:T(8,128)(2,1)} %all-gather.9.cloned.1.call-done, bf16[16,32,1024]{2,0,1:T(8,128)(2,1)} %all-to-all-done), kind=kOutput, calls=%fused_computation.41 | convolution fusion | flops 2152726528 | bytes 6291456 | tf_op jit(solution)/shard_map/csef,efd->csed/dot_general | solution.py:119
  217.0 2.8 copy.35
  219.8 15.9 %all-to-all-start.1 = ((bf16[16,32,1024]{2,0,1:T(8,128)(2,1)}), bf16[16,32,1024]{2,0,1:T(8,128)(2,1)}, u32[]{:S(2)}, u32[]{:S(2)}) async-start(bf16[16,32,1024]{2,0,1:T(8,128)(2,1)} %copy.35), calls=%async_computation.1 | async-start | bytes 2097152 | tf_op jit(solution)/shard_map/all_to_all | solution.py:123
  236.0 56.1 %all-to-all-done.1 = bf16[16,32,1024]{2,0,1:T(8,128)(2,1)} async-done(((bf16[16,32,1024]{2,0,1:T(8,128)(2,1)}), bf16[16,32,1024]{2,0,1:T(8,128)(2,1)}, u32[]{:S(2)}, u32[]{:S(2)}) %all-to-all-start.1) | async-done | bytes 1048608 | tf_op jit(solution)/shard_map/all_to_all | solution.py:123
  292.1 1.8 copy.36
  294.4 0.8 fusion.95
  (54 shorter events, 6.3 us)
Async XLA Ops:
  6.5 126.1 %copy-start = (bf16[1024,1024]{1,0:T(8,128)(2,1)S(1)}, bf16[1024,1024]{1,0:T(8,128)(2,1)}, u32[]{:S(2)}) copy-start(bf16[1024,1024]{1,0:T(8,128)(2,1)} %param.19) | copy-start | bytes 6291460
  6.5 59.9 %all-gather.5.cloned.1.call-start = ((), (), s32[]{:S(2)}) async-start(), calls=%async_computation.2 | async-start | bytes 4456448 | tf_op jit(solution)/shard_map/all_gather | solution.py:74
  8.5 113.2 %all-gather.7.cloned.1.call-start = ((), (), s32[]{:S(2)}) async-start(), calls=%async_computation.3 | async-start | bytes 4456448 | tf_op jit(solution)/shard_map/all_gather | solution.py:75
  10.4 156.1 %all-gather.11.cloned.1.call-start = ((), (), s32[]{:S(2)}) async-start(), calls=%async_computation.5 | async-start | bytes 2228224 | tf_op jit(solution)/shard_map/all_gather | solution.py:65
  66.4 2.5 copy-start.8
  68.6 5.7 %copy-start.6 = (f32[16,128,512]{2,1,0:T(8,128)}, f32[16,128,512]{2,1,0:T(8,128)S(1)}, u32[]{:S(2)}) copy-start(f32[16,128,512]{2,1,0:T(8,128)S(1)} %get-tuple-element.23) | copy-start | bytes 12582916
  69.8 4.6 %copy-start.1 = (f32[16,128,512]{2,1,0:T(8,128)}, f32[16,128,512]{2,1,0:T(8,128)S(1)}, u32[]{:S(2)}) copy-start(f32[16,128,512]{2,1,0:T(8,128)S(1)} %get-tuple-element.25) | copy-start | bytes 12582916
  70.6 3.3 %copy-start.3 = (f32[16,128,512]{2,1,0:T(8,128)}, f32[16,128,512]{2,1,0:T(8,128)S(1)}, u32[]{:S(2)}) copy-start(f32[16,128,512]{2,1,0:T(8,128)S(1)} %get-tuple-element.27) | copy-start | bytes 12582916
  71.5 2.9 copy-start.5
  121.7 3.8 %copy-start.4 = (f32[16,128,512]{2,1,0:T(8,128)S(1)}, f32[16,128,512]{2,1,0:T(8,128)}, u32[]{:S(2)}) copy-start(f32[16,128,512]{2,1,0:T(8,128)} %copy-done.3) | copy-start | bytes 12582916
  125.3 2.5 copy-start.2
  127.8 2.5 copy-start.7
  130.3 2.4 copy-start.9
  137.9 72.8 %all-to-all-start = ((bf16[16,32,1024]{2,0,1:T(8,128)(2,1)}), bf16[16,32,1024]{2,0,1:T(8,128)(2,1)}, u32[]{:S(2)}, u32[]{:S(2)}) async-start(bf16[16,32,1024]{2,0,1:T(8,128)(2,1)} %copy.32), calls=%async_computation | async-start | bytes 2097152 | tf_op jit(solution)/shard_map/all_to_all | solution.py:112
  152.9 57.8 %all-gather.9.cloned.1.call-start = ((), (), s32[]{:S(2)}) async-start(), calls=%async_computation.4 | async-start | bytes 2228224 | tf_op jit(solution)/shard_map/all_gather | solution.py:64
  217.0 77.0 %copy-start.10 = (f32[1,128,2]{1,2,0:T(2,128)S(1)}, f32[1,128,2]{1,2,0:T(2,128)}, u32[]{:S(2)}) copy-start(f32[1,128,2]{1,2,0:T(2,128)} %param.23) | copy-start | bytes 3076
  219.8 72.4 %all-to-all-start.1 = ((bf16[16,32,1024]{2,0,1:T(8,128)(2,1)}), bf16[16,32,1024]{2,0,1:T(8,128)(2,1)}, u32[]{:S(2)}, u32[]{:S(2)}) async-start(bf16[16,32,1024]{2,0,1:T(8,128)(2,1)} %copy.35), calls=%async_computation.1 | async-start | bytes 2097152 | tf_op jit(solution)/shard_map/all_to_all | solution.py:123
Sparse Core Ops, SparseCore 0:
  9.4 56.9 all-gather.4
  68.5 53.1 all-gather.6
  123.9 42.5 all-gather.10
  168.4 42.2 all-gather.8
where the time goes:
time: 302 us
  waiting for transfers between devices  188 us (62%)
  starting transfers between devices  31.2 us (10%)
  matrix products  24.1 us (8%)
  blocking collectives  20.1 us (7%)
  local copies, waits for them, and re-layouts  15.5 us (5%)
  between operations  13.4 us (4%)
  other arithmetic  9.02 us (3%)
    all_to_all x1, waiting for transfers between devices, on_device(): lax.all_to_all(produced, 'expert', split_axis=1, concat_axis=1, tiled=True)  56.1 us
    all_gather x1, waiting for transfers between devices, on_device(): value_part = lax.all_gather(value_heads, 'tm', axis=0, tiled=True)  44.9 us
    all_gather x1, waiting for transfers between devices, on_device(): lax.all_gather(up_weight, 'tm', axis=2, tiled=True)  44.3 us
    all_gather x1, waiting for transfers between devices, on_device(): key_part = lax.all_gather(key_heads, 'tm', axis=0, tiled=True)  29.1 us
    all_gather x1, blocking collectives, on_device(): offset_part = lax.all_gather(offsets, 'tm', axis=0, tiled=True)  20.1 us
    all_to_all x1, starting transfers between devices, on_device(): lax.all_to_all(produced, 'expert', split_axis=1, concat_axis=1, tiled=True)  15.9 us
    all_to_all x1, starting transfers between devices, on_device(): lax.all_to_all(slots, 'expert', split_axis=1, concat_axis=1, tiled=True)  15 us
    all_gather x1, waiting for transfers between devices, on_device(): lax.all_gather(down_weight, 'tm', axis=1, tiled=True)  12.9 us
  transfers between devices with their start and end apart: 6, of which 5 were waited for; matrix products, arithmetic and copies ran while one was open for 11% of the time, Pallas kernels for 0%

commit v1 on v0

--- a/solution.py
+++ b/solution.py
@@ -4,26 +4,22 @@
 from jax.sharding import PartitionSpec as P
 
 eps = 1e-06
-block_rows = 512
+query_block = 512
 
 
-def key_block(carried, query_first, key_rows, value_rows, offset_rows):
-    running_max, running_sum, weighted = carried
-    key_first = jnp.transpose(key_rows, (1, 0, 2))
-    value_first = jnp.transpose(value_rows, (1, 0, 2))
-    scores = jnp.einsum("hqd,hkd->hqk", query_first, key_first, preferred_element_type=jnp.float32)
-    scores = scores + jnp.transpose(offset_rows.astype(jnp.float32))[:, None, :]
-    new_max = jnp.maximum(running_max, jnp.max(scores, axis=2))
-    factor = jnp.exp(running_max - new_max)
-    unscaled = jnp.exp(scores - new_max[:, :, None])
-    running_sum = running_sum * factor + jnp.sum(unscaled, axis=2)
-    weighted = weighted * factor[:, :, None] + jnp.einsum(
-        "hqk,hkd->hqd",
-        unscaled.astype(jnp.bfloat16),
-        value_first,
-        preferred_element_type=jnp.float32,
-    )
-    return (new_max, running_sum, weighted)
+def head_attention(query_rows, key_rows, value_rows, offset_row):
+    outputs = []
+    for first in range(0, query_rows.shape[0], query_block):
+        block = query_rows[first:first + query_block]
+        scores = jnp.dot(block, key_rows.T, preferred_element_type=jnp.float32) + offset_row[None, :]
+        highest = jnp.max(scores, axis=1, keepdims=True)
+        unscaled = jnp.exp(scores - highest)
+        total = jnp.sum(unscaled, axis=1, keepdims=True)
+        weighted = jnp.dot(
+            unscaled.astype(jnp.bfloat16), value_rows, preferred_element_type=jnp.float32
+        )
+        outputs.append((weighted / total).astype(jnp.bfloat16))
+    return jnp.concatenate(outputs, axis=0)
 
 
 def layer_norm(mixed, shift_row, scale_row):
@@ -53,41 +49,40 @@
     head_count = key_bias.shape[0]
     head_width = model_width // head_count
     score_scale = head_width ** (-0.5)
-    scaled_queries = queries[0] * jnp.asarray(score_scale, jnp.bfloat16)
-    query_heads = scaled_queries.reshape(tok_rows, head_count, head_width)
-    key_heads = keys[0].reshape(tok_rows, head_count, head_width)
-    value_heads = values[0].reshape(tok_rows, head_count, head_width)
-    offsets = jnp.where(
-        inpaint_mask[0][:, None] == 1, key_bias[None, :], jnp.zeros((), jnp.bfloat16)
-    )
     full_up, full_down = (
         lax.all_gather(up_weight, "tm", axis=2, tiled=True),
         lax.all_gather(down_weight, "tm", axis=1, tiled=True),
     )
-    query_first = jnp.transpose(query_heads, (1, 0, 2))
-    initial = (
-        jnp.full((head_count, tok_rows), -1e30, jnp.float32),
-        jnp.zeros((head_count, tok_rows), jnp.float32),
-        jnp.zeros((head_count, tok_rows, head_width), jnp.float32),
+    scaled_queries = queries[0] * jnp.asarray(score_scale, jnp.bfloat16)
+    offsets = jnp.where(
+        inpaint_mask[0][:, None] == 1, key_bias[None, :], jnp.zeros((), jnp.bfloat16)
     )
-    carried = initial
-    key_part = lax.all_gather(key_heads, "tm", axis=0, tiled=True)
-    value_part = lax.all_gather(value_heads, "tm", axis=0, tiled=True)
-    offset_part = lax.all_gather(offsets, "tm", axis=0, tiled=True)
-    row_count = key_part.shape[0]
-    for first_row in range(0, row_count, block_rows):
-        last_row = min(row_count, first_row + block_rows)
-        carried = key_block(
-            carried,
-            query_first,
-            key_part[first_row:last_row],
-            value_part[first_row:last_row],
-            offset_part[first_row:last_row],
-        )
-    running_max, running_sum, weighted = carried
-    attended = jnp.transpose(weighted / running_sum[:, :, None], (1, 0, 2)).astype(jnp.bfloat16)
-    projected = jnp.dot(
-        attended.reshape(tok_rows, model_width), out_weight, preferred_element_type=jnp.float32
+    offset_cols = jnp.zeros((tok_rows, head_count, head_width), jnp.bfloat16).at[:, :, 0].set(offsets)
+    packed = jnp.concatenate(
+        [
+            scaled_queries.reshape(tok_rows, head_count, head_width),
+            keys[0].reshape(tok_rows, head_count, head_width),
+            values[0].reshape(tok_rows, head_count, head_width),
+            offset_cols,
+        ],
+        axis=2,
+    )
+    packed = jnp.transpose(packed, (1, 0, 2))
+    gathered = lax.all_to_all(packed, "tm", split_axis=0, concat_axis=0, tiled=True)
+    clip_rows = gathered.reshape(-1, 4 * head_width)
+    head_out = head_attention(
+        clip_rows[:, :head_width],
+        clip_rows[:, head_width:2 * head_width],
+        clip_rows[:, 2 * head_width:3 * head_width],
+        clip_rows[:, 3 * head_width].astype(jnp.float32),
+    )
+    head_out = head_out.reshape(head_count, tok_rows, head_width)
+    attended_heads = lax.all_to_all(head_out, "tm", split_axis=0, concat_axis=0, tiled=True)
+    projected = jnp.einsum(
+        "hid,hdo->io",
+        attended_heads,
+        out_weight.reshape(head_count, head_width, model_width),
+        preferred_element_type=jnp.float32,
     )
     mixed = latents[0].astype(jnp.float32) + branch_gates[0, 0][None, :] * projected
     normed = layer_norm(mixed, modulation[0, 0][None, :], modulation[0, 1][None, :]).astype(

time: 302 us -> 220 us (0.73)
  waiting for transfers between devices: 188 us -> 136 us
  blocking collectives: 20.1 us -> 0 us
  matrix products: 24.1 us -> 17 us
    all_gather x2 -> x0, waiting for transfers between devices: 74 us -> none  [the longest x1 44.9 us: on_device(): value_part = lax.all_gather(value_heads, 'tm', axis=0, tiled=True)]
    all_gather x1, waiting for transfers between devices: 44.3 us -> 0.02 us  [on_device(): lax.all_gather(up_weight, 'tm', axis=2, tiled=True)]
    all_gather x1, waiting for transfers between devices: 12.9 us -> 43 us  [on_device(): lax.all_gather(down_weight, 'tm', axis=1, tiled=True)]
    all_to_all x0 -> x2, waiting for transfers between devices: none -> 23.6 us  [the longest x1 14.5 us: on_device(): lax.all_to_all(packed, 'tm', split_axis=0, concat_axis=0, tiled=True)]
    all_gather x1 -> x0, blocking collectives: 20.1 us -> none  [on_device(): offset_part = lax.all_gather(offsets, 'tm', axis=0, tiled=True)]
    all_to_all x1, waiting for transfers between devices: 0.01 us -> 12.3 us  [on_device(): lax.all_to_all(slots, 'expert', split_axis=1, concat_axis=1, tiled=True)]
    all_to_all x1, starting transfers between devices: 15.9 us -> 4.5 us  [on_device(): lax.all_to_all(produced, 'expert', split_axis=1, concat_axis=1, tiled=True)]
    all_to_all x0 -> x2, starting transfers between devices: none -> 9.27 us  [the longest x1 5.55 us: on_device(): lax.all_to_all(packed, 'tm', split_axis=0, concat_axis=0, tiled=True)]
  transfers between devices with their start and end apart: 6 -> 6, of which waited for: 5 -> 5; matrix products, arithmetic and copies ran while one was open for 11% -> 9% of each run, Pallas kernels for 0% -> 0%
where the time goes in v1:
time: 220 us
  waiting for transfers between devices  136 us (62%)
  starting transfers between devices  31.3 us (14%)
  matrix products  17 us (8%)
  between operations  13.7 us (6%)
  local copies, waits for them, and re-layouts  13.2 us (6%)
  other arithmetic  8.24 us (4%)
    all_to_all x1, waiting for transfers between devices, on_device(): lax.all_to_all(produced, 'expert', split_axis=1, concat_axis=1, tiled=True)  55.7 us
    all_gather x1, waiting for transfers between devices, on_device(): lax.all_gather(down_weight, 'tm', axis=1, tiled=True)  43 us
    all_to_all x1, starting transfers between devices, on_device(): lax.all_to_all(slots, 'expert', split_axis=1, concat_axis=1, tiled=True)  17.5 us
    all_to_all x1, waiting for transfers between devices, on_device(): lax.all_to_all(packed, 'tm', split_axis=0, concat_axis=0, tiled=True)  14.5 us
    all_to_all x1, waiting for transfers between devices, on_device(): lax.all_to_all(slots, 'expert', split_axis=1, concat_axis=1, tiled=True)  12.3 us
    all_to_all x1, waiting for transfers between devices, on_device(): lax.all_to_all(head_out, 'tm', split_axis=0, concat_axis=0, tiled=True)  9.1 us
    dot_general x1, matrix products, on_device(): jnp.einsum('csef,efd->csed', hidden, full_down, preferred_element_type=jn...  6.21 us
    all_to_all x1, starting transfers between devices, on_device(): lax.all_to_all(packed, 'tm', split_axis=0, concat_axis=0, tiled=True)  5.55 us
  transfers between devices with their start and end apart: 6, of which 5 were waited for; matrix products, arithmetic and copies ran while one was open for 9% of the time, Pallas kernels for 0%

profile of v1, /device:TPU:32, one launch (start us, length us, event | category | flops | bytes accessed | tf_op | source)
XLA Modules:
  0.0 219.5 jit_solution(16701565516031589247)
XLA Ops:
  6.5 1.3 copy.26
  7.8 1.1 copy.27
  9.0 1.1 copy.28
  10.8 0.7 broadcast_select_fusion
  11.5 1.1 fusion.65
  12.6 5.6 %all-to-all-start = ((bf16[16,128,256]{1,2,0:T(8,128)(2,1)}), bf16[16,128,256]{1,2,0:T(8,128)(2,1)}, u32[]{:S(2)}, u32[]{:S(2)}) async-start(bf16[16,128,256]{1,2,0:T(8,128)(2,1)} %fusion.65), calls=%async_computation | async-start | bytes 2097152 | tf_op jit(solution)/shard_map/all_to_all | solution.py:71
  20.3 14.5 %all-to-all-done = bf16[16,128,256]{1,2,0:T(8,128)(2,1)} async-done(((bf16[16,128,256]{1,2,0:T(8,128)(2,1)}), bf16[16,128,256]{1,2,0:T(8,128)(2,1)}, u32[]{:S(2)}, u32[]{:S(2)}) %all-to-all-start) | async-done | bytes 1048608 | tf_op jit(solution)/shard_map/all_to_all | solution.py:71
  34.8 1.5 copy.29
  36.7 0.8 fusion.76
  37.5 0.8 fusion.78
  38.3 0.9 add_reduce_fusion.3
  39.2 2.1 fusion
  41.3 1.0 fusion.43
  42.2 2.5 %fusion.2 = (f32[512]{0:T(512)S(1)}, f32[512]{0:T(512)S(1)}, f32[512]{0:T(512)S(1)}) fusion(f32[512,2048]{1,0:T(8,128)S(1)} %get-tuple-element.30, f32[512]{0:T(512)S(1)} %get-tuple-element.18, f32[2048]{0:T(1024)S(1)} %convert_reduce_fusion, f32[512]{0:T(512)S(1)} %get-tuple-element.19, f32[512,2048]{1,0:T(8,128)S(1)} %fusion.78, ...), kind=kLoop, calls=%fused_computation.10 | loop fusion | flops 9435648 | bytes 12603392 | tf_op jit(solution)/shard_map/reduce_sum | solution.py:17
  44.7 1.0 fusion.49
  45.7 1.0 fusion.55
  46.7 1.0 fusion.61
  47.6 0.8 copy_bitcast_fusion
  48.4 3.7 %all-to-all-start.1 = ((bf16[16,128,64]{1,2,0:T(8,128)(2,1)}), bf16[16,128,64]{1,2,0:T(8,128)(2,1)S(1)}, u32[]{:S(2)}, u32[]{:S(2)}) async-start(bf16[16,128,64]{1,2,0:T(8,128)(2,1)} %copy_bitcast_fusion), calls=%async_computation.1 | async-start | bytes 524288 | tf_op jit(solution)/shard_map/all_to_all | solution.py:80
  52.2 9.1 %all-to-all-done.1 = bf16[16,128,64]{1,2,0:T(8,128)(2,1)S(1)} async-done(((bf16[16,128,64]{1,2,0:T(8,128)(2,1)}), bf16[16,128,64]{1,2,0:T(8,128)(2,1)S(1)}, u32[]{:S(2)}, u32[]{:S(2)}) %all-to-all-start.1) | async-done | bytes 262176 | tf_op jit(solution)/shard_map/all_to_all | solution.py:80
  62.5 1.0 reshape.208
  63.5 1.5 convolution_convert_fusion
  65.0 1.6 copy.34
  66.6 17.5 %all-to-all-start.2 = ((bf16[16,32,1024]{2,0,1:T(8,128)(2,1)}), bf16[16,32,1024]{2,0,1:T(8,128)(2,1)}, u32[]{:S(2)}, u32[]{:S(2)}) async-start(bf16[16,32,1024]{2,0,1:T(8,128)(2,1)} %copy.34), calls=%async_computation.2 | async-start | bytes 2097152 | tf_op jit(solution)/shard_map/all_to_all | solution.py:107
  84.8 43.0 %all-gather.5.cloned.1.call-done = bf16[1,1024,1024]{2,1,0:T(8,128)(2,1)} async-done(((bf16[1,64,1024]{2,1,0:T(8,128)(2,1)}), bf16[1,1024,1024]{2,1,0:T(8,128)(2,1)}) %all-gather.5.cloned.1.call-update) | async-done | bytes 2097168 | tf_op jit(solution)/shard_map/all_gather | solution.py:54
  127.8 12.3 %all-to-all-done.2 = bf16[16,32,1024]{2,0,1:T(8,128)(2,1)} async-done(((bf16[16,32,1024]{2,0,1:T(8,128)(2,1)}), bf16[16,32,1024]{2,0,1:T(8,128)(2,1)}, u32[]{:S(2)}, u32[]{:S(2)}) %all-to-all-start.2) | async-done | bytes 1048608 | tf_op jit(solution)/shard_map/all_to_all | solution.py:107
  140.1 6.2 %fusion.31 = bf16[16,32,1024]{2,1,0:T(8,128)(2,1)} fusion(bf16[1,1024,1024]{2,1,0:T(8,128)(2,1)} %all-gather.5.cloned.1.call-done, bf16[1,1024,1024]{1,2,0:T(8,128)(2,1)} %all-gather.3.cloned.1.call-done, bf16[16,32,1024]{2,0,1:T(8,128)(2,1)} %all-to-all-done.2), kind=kOutput, calls=%fused_computation.35 | convolution fusion | flops 2152726528 | bytes 6291456 | tf_op jit(solution)/shard_map/csef,efd->csed/dot_general | solution.py:114
  146.3 2.8 %copy.37 = bf16[16,32,1024]{2,0,1:T(8,128)(2,1)} copy(bf16[16,32,1024]{2,1,0:T(8,128)(2,1)} %fusion.31) | data formatting | bytes 2097152 | tf_op jit(solution)/shard_map/convert_element_type | solution.py:116
  149.1 4.5 %all-to-all-start.3 = ((bf16[16,32,1024]{2,0,1:T(8,128)(2,1)}), bf16[16,32,1024]{2,0,1:T(8,128)(2,1)}, u32[]{:S(2)}, u32[]{:S(2)}) async-start(bf16[16,32,1024]{2,0,1:T(8,128)(2,1)} %copy.37), calls=%async_computation.3 | async-start | bytes 2097152 | tf_op jit(solution)/shard_map/all_to_all | solution.py:118
  154.0 55.7 %all-to-all-done.3 = bf16[16,32,1024]{2,0,1:T(8,128)(2,1)} async-done(((bf16[16,32,1024]{2,0,1:T(8,128)(2,1)}), bf16[16,32,1024]{2,0,1:T(8,128)(2,1)}, u32[]{:S(2)}, u32[]{:S(2)}) %all-to-all-start.3) | async-done | bytes 1048608 | tf_op jit(solution)/shard_map/all_to_all | solution.py:118
  209.7 1.8 copy.38
  211.9 0.8 fusion.84
  (41 shorter events, 5.9 us)
Async XLA Ops:
  6.5 54.7 %copy-start = (bf16[1024,1024]{1,0:T(8,128)(2,1)S(1)}, bf16[1024,1024]{1,0:T(8,128)(2,1)}, u32[]{:S(2)}) copy-start(bf16[1024,1024]{1,0:T(8,128)(2,1)} %param.21) | copy-start | bytes 6291460
  6.5 12.4 %copy-start.4 = (s32[1,128,2]{1,2,0:T(2,128)S(1)}, s32[1,128,2]{1,2,0:T(2,128)}, u32[]{:S(2)}) copy-start(s32[1,128,2]{1,2,0:T(2,128)} %param.24) | copy-start | bytes 3076
  6.5 13.7 %copy-start.2 = (f32[1,2,1024]{2,1,0:T(2,128)S(1)}, f32[1,2,1024]{2,1,0:T(2,128)}, u32[]{:S(2)}) copy-start(f32[1,2,1024]{2,1,0:T(2,128)} %param.23) | copy-start | bytes 24580
  12.6 22.2 %all-to-all-start = ((bf16[16,128,256]{1,2,0:T(8,128)(2,1)}), bf16[16,128,256]{1,2,0:T(8,128)(2,1)}, u32[]{:S(2)}, u32[]{:S(2)}) async-start(bf16[16,128,256]{1,2,0:T(8,128)(2,1)} %fusion.65), calls=%async_computation | async-start | bytes 2097152 | tf_op jit(solution)/shard_map/all_to_all | solution.py:71
  18.2 66.6 %all-gather.3.cloned.1.call-start = ((), (), s32[]{:S(2)}) async-start(), calls=%async_computation.4 | async-start | bytes 2228224 | tf_op jit(solution)/shard_map/all_gather | solution.py:53
  46.6 5.5 %copy-start.3 = (f32[1,2,1024]{2,1,0:T(2,128)S(1)}, f32[1,2,1024]{2,1,0:T(2,128)}, u32[]{:S(2)}) copy-start(f32[1,2,1024]{2,1,0:T(2,128)} %param.22) | copy-start | bytes 24580
  46.6 14.6 %copy-start.1 = (bf16[1,128,1024]{2,1,0:T(8,128)(2,1)S(1)}, bf16[1,128,1024]{2,1,0:T(8,128)(2,1)}, u32[]{:S(2)}) copy-start(bf16[1,128,1024]{2,1,0:T(8,128)(2,1)} %param.15) | copy-start | bytes 786436
  48.4 12.9 %all-to-all-start.1 = ((bf16[16,128,64]{1,2,0:T(8,128)(2,1)}), bf16[16,128,64]{1,2,0:T(8,128)(2,1)S(1)}, u32[]{:S(2)}, u32[]{:S(2)}) async-start(bf16[16,128,64]{1,2,0:T(8,128)(2,1)} %copy_bitcast_fusion), calls=%async_computation.1 | async-start | bytes 524288 | tf_op jit(solution)/shard_map/all_to_all | solution.py:80
  66.6 73.5 %all-to-all-start.2 = ((bf16[16,32,1024]{2,0,1:T(8,128)(2,1)}), bf16[16,32,1024]{2,0,1:T(8,128)(2,1)}, u32[]{:S(2)}, u32[]{:S(2)}) async-start(bf16[16,32,1024]{2,0,1:T(8,128)(2,1)} %copy.34), calls=%async_computation.2 | async-start | bytes 2097152 | tf_op jit(solution)/shard_map/all_to_all | solution.py:107
  84.0 43.8 %all-gather.5.cloned.1.call-start = ((), (), s32[]{:S(2)}) async-start(), calls=%async_computation.5 | async-start | bytes 2228224 | tf_op jit(solution)/shard_map/all_gather | solution.py:54
  146.3 65.1 %copy-start.5 = (f32[1,128,2]{1,2,0:T(2,128)S(1)}, f32[1,128,2]{1,2,0:T(2,128)}, u32[]{:S(2)}) copy-start(f32[1,128,2]{1,2,0:T(2,128)} %param.25) | copy-start | bytes 3076
  149.1 60.5 %all-to-all-start.3 = ((bf16[16,32,1024]{2,0,1:T(8,128)(2,1)}), bf16[16,32,1024]{2,0,1:T(8,128)(2,1)}, u32[]{:S(2)}, u32[]{:S(2)}) async-start(bf16[16,32,1024]{2,0,1:T(8,128)(2,1)} %copy.37), calls=%async_computation.3 | async-start | bytes 2097152 | tf_op jit(solution)/shard_map/all_to_all | solution.py:118
Sparse Core Ops, SparseCore 0:
  21.2 47.8 all-gather.2
  87.0 40.7 all-gather.4

commit v2 on v1

--- a/solution.py
+++ b/solution.py
@@ -1,6 +1,10 @@
+import functools
+
 import jax
 import jax.numpy as jnp
 from jax import lax
+from jax.experimental import pallas as pl
+from jax.experimental.pallas import tpu as pltpu
 from jax.sharding import PartitionSpec as P
 
 eps = 1e-06
@@ -20,6 +24,60 @@
         )
         outputs.append((weighted / total).astype(jnp.bfloat16))
     return jnp.concatenate(outputs, axis=0)
+
+
+def exchange_kernel(axis, n, x_ref, y_ref, send_sems, recv_sems, local_sem):
+    me = lax.axis_index(axis)
+    barrier = pltpu.get_barrier_semaphore()
+    for k in range(1, n):
+        pl.semaphore_signal(
+            barrier, inc=1, device_id={axis: lax.rem(me + k, n)}, device_id_type=pl.DeviceIdType.MESH
+        )
+    pl.semaphore_wait(barrier, n - 1)
+    local = pltpu.make_async_copy(x_ref.at[me], y_ref.at[me], local_sem)
+    local.start()
+    copies = []
+    for k in range(1, n):
+        peer = lax.rem(me + k, n)
+        copy = pltpu.make_async_remote_copy(
+            src_ref=x_ref.at[peer],
+            dst_ref=y_ref.at[me],
+            send_sem=send_sems.at[k],
+            recv_sem=recv_sems.at[k],
+            device_id={axis: peer},
+            device_id_type=pl.DeviceIdType.MESH,
+        )
+        copy.start()
+        copies.append(copy)
+    local.wait()
+    for copy in copies:
+        copy.wait_send()
+    for k in range(1, n):
+        source = lax.rem(me + n - k, n)
+        pltpu.make_async_remote_copy(
+            src_ref=x_ref.at[source],
+            dst_ref=y_ref.at[source],
+            send_sem=send_sems.at[k],
+            recv_sem=recv_sems.at[k],
+            device_id={axis: source},
+            device_id_type=pl.DeviceIdType.MESH,
+        ).wait_recv()
+
+
+def exchange(x, axis, collective_id):
+    n = x.shape[0]
+    return pl.pallas_call(
+        functools.partial(exchange_kernel, axis, n),
+        out_shape=jax.ShapeDtypeStruct(x.shape, x.dtype),
+        in_specs=[pl.BlockSpec(memory_space=pl.ANY)],
+        out_specs=pl.BlockSpec(memory_space=pl.ANY),
+        scratch_shapes=[
+            pltpu.SemaphoreType.DMA((n,)),
+            pltpu.SemaphoreType.DMA((n,)),
+            pltpu.SemaphoreType.DMA,
+        ],
+        compiler_params=pltpu.CompilerParams(collective_id=collective_id, has_side_effects=True),
+    )(x)
 
 
 def layer_norm(mixed, shift_row, scale_row):
@@ -68,7 +126,7 @@
         axis=2,
     )
     packed = jnp.transpose(packed, (1, 0, 2))
-    gathered = lax.all_to_all(packed, "tm", split_axis=0, concat_axis=0, tiled=True)
+    gathered = exchange(packed, "tm", 0)
     clip_rows = gathered.reshape(-1, 4 * head_width)
     head_out = head_attention(
         clip_rows[:, :head_width],
@@ -77,7 +135,7 @@
         clip_rows[:, 3 * head_width].astype(jnp.float32),
     )
     head_out = head_out.reshape(head_count, tok_rows, head_width)
-    attended_heads = lax.all_to_all(head_out, "tm", split_axis=0, concat_axis=0, tiled=True)
+    attended_heads = exchange(head_out, "tm", 1)
     projected = jnp.einsum(
         "hid,hdo->io",
         attended_heads,

time: 220 us -> 235 us (1.068)
  Pallas kernels: 0 us -> 31.7 us
  waiting for transfers between devices: 136 us -> 113 us
  starting transfers between devices: 31.3 us -> 23 us
  matrix products: 17 us -> 25 us
  local copies, waits for them, and re-layouts: 13.2 us -> 18.3 us
    pallas_call x0 -> x2, Pallas kernels: none -> 31.7 us  [exchange(): pl.pallas_call(functools.partial(exchange_kernel, axis, n), out_shape=jax...]
    all_to_all x2 -> x0, waiting for transfers between devices: 23.6 us -> none  [the longest x1 14.5 us: on_device(): lax.all_to_all(packed, 'tm', split_axis=0, concat_axis=0, tiled=True)]
    all_to_all x2 -> x0, starting transfers between devices: 9.27 us -> none  [the longest x1 5.55 us: on_device(): lax.all_to_all(packed, 'tm', split_axis=0, concat_axis=0, tiled=True)]
    dot_general x4, matrix products: 4.52 us -> 11.5 us  [head_attention(): jnp.dot(block, key_rows.T, preferred_element_type=jnp.float32)]
    unnamed x16 -> x27, local copies, waits for them, and re-layouts: 3.65 us -> 7.66 us
  transfers between devices with their start and end apart: 6 -> 4, of which waited for: 5 -> 3; matrix products, arithmetic and copies ran while one was open for 9% -> 16% of each run, Pallas kernels for 0% -> 14%
where the time goes in v2:
time: 235 us; the launch traced here: 234 us
  waiting for transfers between devices  113 us (48%)
  Pallas kernels  31.7 us (13%)
  matrix products  25 us (11%)
  starting transfers between devices  23 us (10%)
  local copies, waits for them, and re-layouts  18.3 us (8%)
  between operations  13.7 us (6%)
  other arithmetic  9.81 us (4%)
    all_to_all x1, waiting for transfers between devices, on_device(): lax.all_to_all(produced, 'expert', split_axis=1, concat_axis=1, tiled=True)  55.7 us
    all_gather x1, waiting for transfers between devices, on_device(): lax.all_gather(down_weight, 'tm', axis=1, tiled=True)  44.3 us
    pallas_call x2, Pallas kernels, exchange(): pl.pallas_call(functools.partial(exchange_kernel, axis, n), out_shape=jax...  31.7 us
    all_to_all x1, starting transfers between devices, on_device(): lax.all_to_all(slots, 'expert', split_axis=1, concat_axis=1, tiled=True)  18.3 us
    all_to_all x1, waiting for transfers between devices, on_device(): lax.all_to_all(slots, 'expert', split_axis=1, concat_axis=1, tiled=True)  11.6 us
    dot_general x4, matrix products, head_attention(): jnp.dot(block, key_rows.T, preferred_element_type=jnp.float32)  11.5 us
    unnamed x27, local copies, waits for them, and re-layouts  7.66 us
    dot_general x1, matrix products, on_device(): jnp.einsum('csef,efd->csed', hidden, full_down, preferred_element_type=jn...  6.19 us
  transfers between devices with their start and end apart: 4, of which 3 were waited for; matrix products, arithmetic and copies ran while one was open for 16% of the time, Pallas kernels for 14%

profile of v2, /device:TPU:32, one launch (start us, length us, event | category | flops | bytes accessed | tf_op | source)
XLA Modules:
  0.0 234.4 jit_solution(838785778843990915)
XLA Ops:
  7.3 1.1 copy.31
  8.7 1.1 copy.32
  10.1 1.1 copy.33
  11.3 1.0 copy.36
  12.4 2.8 %fusion.65.x_ref = bf16[16,128,256]{2,1,0:T(8,128)(2,1)} fusion(bf16[128,16,1]{2,0,1:T(8,128)(2,1)S(1)} %broadcast_select_fusion, bf16[128,16,64]{2,0,1:T(8,128)(2,1)} %copy.36, bf16[128,16,64]{2,0,1:T(8,128)(2,1)S(1)} %copy.35, bf16[128,16,64]{2,0,1:T(8,128)(2,1)S(1)} %copy.34), kind=kLoop, calls=%fused_computation.52 | loop fusion | flops 5242880 | bytes 1839104 | tf_op jit(solution)/shard_map/transpose | solution.py:128
  15.2 18.8 %shard_map.127 = bf16[16,128,256]{2,1,0:T(8,128)(2,1)} custom-call(bf16[16,128,256]{2,1,0:T(8,128)(2,1)} %fusion.65.x_ref), custom_call_target="tpu_custom_call" | custom-call | tf_op jit(solution)/shard_map/pallas_call | solution.py:69
  34.0 2.3 slice_convert_fusion
  36.4 3.8 %fusion.76 = f32[512,2048]{1,0:T(8,128)} fusion(bf16[2048,256]{1,0:T(8,128)(2,1)} %bitcast.83), kind=kOutput, calls=%fused_computation.66 | convolution fusion | flops 134217728 | bytes 4849664 | tf_op jit(solution)/shard_map/dot_general | solution.py:18
  40.2 2.8 %fusion.78 = f32[512,2048]{1,0:T(8,128)} fusion(bf16[2048,256]{1,0:T(8,128)(2,1)S(1)} %bitcast.84), kind=kOutput, calls=%fused_computation.68 | convolution fusion | flops 134217728 | bytes 4849664 | tf_op jit(solution)/shard_map/dot_general | solution.py:18
  43.4 1.6 copy.52
  45.8 1.3 copy-done.1
  47.2 4.0 %fusion = (f32[512]{0:T(512)S(1)}, f32[512]{0:T(512)S(1)}, f32[512]{0:T(512)S(1)}, f32[512]{0:T(512)S(1)}, f32[512,2048]{1,0:T(8,128)S(1)}) fusion(f32[512,2048]{1,0:T(8,128)S(1)} %get-tuple-element.29, f32[512]{0:T(512)S(1)} %get-tuple-element.28, f32[2048]{0:T(1024)S(1)} %bitcast.98, f32[512,2048]{1,0:T(8,128)} %fusion.78, f32[512,2048]{1,0:T(8,128)S(1)} %copy-done.1, ...), kind=kOutput, calls=%fused_computation.8 | convolution fusion | flops 143652864 | bytes 17451008 | tf_op jit(solution)/shard_map/dot_general | solution.py:18
  51.2 1.0 fusion.43
  52.1 1.3 copy-done.2
  53.4 2.5 %fusion.2 = (f32[512]{0:T(512)S(1)}, f32[512]{0:T(512)S(1)}, f32[512]{0:T(512)S(1)}) fusion(f32[512,2048]{1,0:T(8,128)S(1)} %get-tuple-element.30, f32[512]{0:T(512)S(1)} %get-tuple-element.18, f32[2048]{0:T(1024)S(1)} %bitcast.100, f32[512]{0:T(512)S(1)} %get-tuple-element.19, f32[512,2048]{1,0:T(8,128)S(1)} %copy-done.2, f32[512]{0:T(512)S(1)} %get-tuple-element.20, ...), kind=kLoop, calls=%fused_computation.10 | loop fusion | flops 9435648 | bytes 12603392 | tf_op jit(solution)/shard_map/reduce_sum | solution.py:21
  55.9 1.0 fusion.49
  56.8 1.0 fusion.55
  57.8 1.0 fusion.61
  58.8 1.0 copy.38
  59.8 12.9 %shard_map.128 = bf16[16,128,64]{2,1,0:T(8,128)(2,1)} custom-call(bf16[16,128,64]{2,1,0:T(8,128)(2,1)} %bitcast.92), custom_call_target="tpu_custom_call" | custom-call | tf_op jit(solution)/shard_map/pallas_call | solution.py:69
  72.8 1.6 fusion.98
  75.1 1.0 reshape.208
  77.0 1.5 convolution_convert_fusion
  78.5 1.6 copy.43
  80.1 18.3 %all-to-all-start = ((bf16[16,32,1024]{2,0,1:T(8,128)(2,1)}), bf16[16,32,1024]{2,0,1:T(8,128)(2,1)}, u32[]{:S(2)}, u32[]{:S(2)}) async-start(bf16[16,32,1024]{2,0,1:T(8,128)(2,1)} %copy.43), calls=%async_computation | async-start | bytes 2097152 | tf_op jit(solution)/shard_map/all_to_all | solution.py:165
  99.2 44.3 %all-gather.5.cloned.1.call-done = bf16[1,1024,1024]{2,1,0:T(8,128)(2,1)} async-done(((bf16[1,64,1024]{2,1,0:T(8,128)(2,1)}), bf16[1,1024,1024]{2,1,0:T(8,128)(2,1)}) %all-gather.5.cloned.1.call-update) | async-done | bytes 2097168 | tf_op jit(solution)/shard_map/all_gather | solution.py:112
  143.5 11.6 %all-to-all-done = bf16[16,32,1024]{2,0,1:T(8,128)(2,1)} async-done(((bf16[16,32,1024]{2,0,1:T(8,128)(2,1)}), bf16[16,32,1024]{2,0,1:T(8,128)(2,1)}, u32[]{:S(2)}, u32[]{:S(2)}) %all-to-all-start) | async-done | bytes 1048608 | tf_op jit(solution)/shard_map/all_to_all | solution.py:165
  155.1 6.2 %fusion.31 = bf16[16,32,1024]{2,1,0:T(8,128)(2,1)} fusion(bf16[1,1024,1024]{2,1,0:T(8,128)(2,1)} %all-gather.5.cloned.1.call-done, bf16[1,1024,1024]{1,2,0:T(8,128)(2,1)} %all-gather.3.cloned.1.call-done, bf16[16,32,1024]{2,0,1:T(8,128)(2,1)} %all-to-all-done), kind=kOutput, calls=%fused_computation.35 | convolution fusion | flops 2152726528 | bytes 6291456 | tf_op jit(solution)/shard_map/csef,efd->csed/dot_general | solution.py:172
  161.3 2.8 %copy.46 = bf16[16,32,1024]{2,0,1:T(8,128)(2,1)} copy(bf16[16,32,1024]{2,1,0:T(8,128)(2,1)} %fusion.31) | data formatting | bytes 2097152 | tf_op jit(solution)/shard_map/convert_element_type | solution.py:174
  164.1 4.5 %all-to-all-start.1 = ((bf16[16,32,1024]{2,0,1:T(8,128)(2,1)}), bf16[16,32,1024]{2,0,1:T(8,128)(2,1)}, u32[]{:S(2)}, u32[]{:S(2)}) async-start(bf16[16,32,1024]{2,0,1:T(8,128)(2,1)} %copy.46), calls=%async_computation.1 | async-start | bytes 2097152 | tf_op jit(solution)/shard_map/all_to_all | solution.py:176
  168.9 55.7 %all-to-all-done.1 = bf16[16,32,1024]{2,0,1:T(8,128)(2,1)} async-done(((bf16[16,32,1024]{2,0,1:T(8,128)(2,1)}), bf16[16,32,1024]{2,0,1:T(8,128)(2,1)}, u32[]{:S(2)}, u32[]{:S(2)}) %all-to-all-start.1) | async-done | bytes 1048608 | tf_op jit(solution)/shard_map/all_to_all | solution.py:176
  224.6 1.8 copy.47
  (53 shorter events, 6.6 us)
Async XLA Ops:
  6.5 66.2 %copy-start = (bf16[1024,1024]{1,0:T(8,128)(2,1)S(1)}, bf16[1024,1024]{1,0:T(8,128)(2,1)}, u32[]{:S(2)}) copy-start(bf16[1024,1024]{1,0:T(8,128)(2,1)} %param.21) | copy-start | bytes 6291460
  6.5 5.8 %copy-start.10 = (s32[1,128]{1,0:T(1,128)S(1)}, s32[1,128]{1,0:T(1,128)}, u32[]{:S(2)}) copy-start(s32[1,128]{1,0:T(1,128)} %param.19) | copy-start | bytes 1540
  6.5 5.8 %copy-start.7 = (bf16[16]{0:T(256)(128)(2,1)S(1)}, bf16[16]{0:T(256)(128)(2,1)}, u32[]{:S(2)}) copy-start(bf16[16]{0:T(256)(128)(2,1)} %param.20) | copy-start | bytes 100
  6.5 92.6 %all-gather.3.cloned.1.call-start = ((), (), s32[]{:S(2)}) async-start(), calls=%async_computation.2 | async-start | bytes 2228224 | tf_op jit(solution)/shard_map/all_gather | solution.py:111
  34.0 6.2 %copy-start.3 = (bf16[16,128,256]{2,1,0:T(8,128)(2,1)S(1)}, bf16[16,128,256]{2,1,0:T(8,128)(2,1)}, u32[]{:S(2)}) copy-start(bf16[16,128,256]{2,1,0:T(8,128)(2,1)} %shard_map.127) | copy-start | bytes 3145732
  36.4 6.6 %copy-start.6 = (s32[1,128,2]{1,2,0:T(2,128)S(1)}, s32[1,128,2]{1,2,0:T(2,128)}, u32[]{:S(2)}) copy-start(s32[1,128,2]{1,2,0:T(2,128)} %param.24) | copy-start | bytes 3076
  44.9 2.2 copy-start.1
  51.1 2.2 copy-start.2
  57.8 14.9 %copy-start.4 = (f32[1,2,1024]{2,1,0:T(2,128)S(1)}, f32[1,2,1024]{2,1,0:T(2,128)}, u32[]{:S(2)}) copy-start(f32[1,2,1024]{2,1,0:T(2,128)} %param.23) | copy-start | bytes 24580
  57.8 15.0 %copy-start.8 = (bf16[1,128,1024]{2,1,0:T(8,128)(2,1)S(1)}, bf16[1,128,1024]{2,1,0:T(8,128)(2,1)}, u32[]{:S(2)}) copy-start(bf16[1,128,1024]{2,1,0:T(8,128)(2,1)} %param.15) | copy-start | bytes 786436
  58.8 15.8 %copy-start.5 = (f32[1,2,1024]{2,1,0:T(2,128)S(1)}, f32[1,2,1024]{2,1,0:T(2,128)}, u32[]{:S(2)}) copy-start(f32[1,2,1024]{2,1,0:T(2,128)} %param.22) | copy-start | bytes 24580
  80.1 75.0 %all-to-all-start = ((bf16[16,32,1024]{2,0,1:T(8,128)(2,1)}), bf16[16,32,1024]{2,0,1:T(8,128)(2,1)}, u32[]{:S(2)}, u32[]{:S(2)}) async-start(bf16[16,32,1024]{2,0,1:T(8,128)(2,1)} %copy.43), calls=%async_computation | async-start | bytes 2097152 | tf_op jit(solution)/shard_map/all_to_all | solution.py:165
  98.4 45.1 %all-gather.5.cloned.1.call-start = ((), (), s32[]{:S(2)}) async-start(), calls=%async_computation.3 | async-start | bytes 2228224 | tf_op jit(solution)/shard_map/all_gather | solution.py:112
  161.3 65.1 %copy-start.9 = (f32[1,128,2]{1,2,0:T(2,128)S(1)}, f32[1,128,2]{1,2,0:T(2,128)}, u32[]{:S(2)}) copy-start(f32[1,128,2]{1,2,0:T(2,128)} %param.25) | copy-start | bytes 3076
  164.1 60.5 %all-to-all-start.1 = ((bf16[16,32,1024]{2,0,1:T(8,128)(2,1)}), bf16[16,32,1024]{2,0,1:T(8,128)(2,1)}, u32[]{:S(2)}, u32[]{:S(2)}) async-start(bf16[16,32,1024]{2,0,1:T(8,128)(2,1)} %copy.46), calls=%async_computation.1 | async-start | bytes 2097152 | tf_op jit(solution)/shard_map/all_to_all | solution.py:176
Sparse Core Ops, SparseCore 0:
  9.5 46.1 all-gather.2
  101.4 42.0 all-gather.4

commit v3 on v1

--- a/solution.py
+++ b/solution.py
@@ -49,10 +49,18 @@
     head_count = key_bias.shape[0]
     head_width = model_width // head_count
     score_scale = head_width ** (-0.5)
-    full_up, full_down = (
-        lax.all_gather(up_weight, "tm", axis=2, tiled=True),
-        lax.all_gather(down_weight, "tm", axis=1, tiled=True),
+    tm_count = lax.axis_size("tm")
+    parity_groups = [list(range(p, tm_count, 2)) for p in range(2)]
+    own_slices = jnp.stack([jnp.transpose(up_weight[0]), down_weight[0]])
+    parity_slices = lax.all_gather(
+        own_slices, "tm", axis=1, tiled=True, axis_index_groups=parity_groups
     )
+    sibling_slices = lax.ppermute(
+        parity_slices, "tm", [(t, t ^ 1) for t in range(tm_count)]
+    )
+    both = jnp.concatenate([parity_slices, sibling_slices], axis=1)
+    full_up = jnp.transpose(both[0])[None]
+    full_down = both[1][None]
     scaled_queries = queries[0] * jnp.asarray(score_scale, jnp.bfloat16)
     offsets = jnp.where(
         inpaint_mask[0][:, None] == 1, key_bias[None, :], jnp.zeros((), jnp.bfloat16)

time: 220 us -> 222 us (level)
  waiting for transfers between devices: 136 us -> 130 us
  local copies, waits for them, and re-layouts: 13.2 us -> 17.7 us
    all_gather x2 -> x1, waiting for transfers between devices: 43 us -> 2.16 us  [on_device(): lax.all_gather(own_slices, 'tm', axis=1, tiled=True, axis_index_groups=pa...]
    all_to_all x1, waiting for transfers between devices: 12.3 us -> 45.5 us  [on_device(): lax.all_to_all(slots, 'expert', split_axis=1, concat_axis=1, tiled=True)]
    unnamed x16 -> x21, local copies, waits for them, and re-layouts: 3.65 us -> 6.73 us
    convert_element_type x1 -> x0, local copies, waits for them, and re-layouts: 2.81 us -> none  [on_device(): produced = jnp.einsum('csef,efd->csed', hidden, full_down, preferred_elem...]
    reshape x0 -> x1, local copies, waits for them, and re-layouts: none -> 2.81 us  [on_device(): produced.reshape(slot_count, source_count * local_experts, model_width)]
  transfers between devices with their start and end apart: 6 -> 6, of which waited for: 5 -> 6; matrix products, arithmetic and copies ran while one was open for 9% -> 12% of each run, Pallas kernels for 0% -> 0%
where the time goes in v3:
time: 222 us; the launch traced here: 221 us
  waiting for transfers between devices  130 us (59%)
  starting transfers between devices  33.3 us (15%)
  local copies, waits for them, and re-layouts  17.7 us (8%)
  matrix products  16.9 us (8%)
  between operations  13.7 us (6%)
  other arithmetic  9.05 us (4%)
    all_to_all x1, waiting for transfers between devices, on_device(): lax.all_to_all(produced, 'expert', split_axis=1, concat_axis=1, tiled=True)  55.7 us
    all_to_all x1, waiting for transfers between devices, on_device(): lax.all_to_all(slots, 'expert', split_axis=1, concat_axis=1, tiled=True)  45.5 us
    all_to_all x1, starting transfers between devices, on_device(): lax.all_to_all(slots, 'expert', split_axis=1, concat_axis=1, tiled=True)  17.6 us
    all_to_all x1, waiting for transfers between devices, on_device(): lax.all_to_all(packed, 'tm', split_axis=0, concat_axis=0, tiled=True)  14.4 us
    all_to_all x1, waiting for transfers between devices, on_device(): lax.all_to_all(head_out, 'tm', split_axis=0, concat_axis=0, tiled=True)  10.9 us
    unnamed x21, local copies, waits for them, and re-layouts  6.73 us
    dot_general x1, matrix products, on_device(): jnp.einsum('csef,efd->csed', hidden, full_down, preferred_element_type=jn...  6.1 us
    all_to_all x1, starting transfers between devices, on_device(): lax.all_to_all(packed, 'tm', split_axis=0, concat_axis=0, tiled=True)  5.55 us
  transfers between devices with their start and end apart: 6, of which 6 were waited for; matrix products, arithmetic and copies ran while one was open for 12% of the time, Pallas kernels for 0%

profile of v3, /device:TPU:32, one launch (start us, length us, event | category | flops | bytes accessed | tf_op | source)
XLA Modules:
  0.0 220.8 jit_solution(12134565212137798740)
XLA Ops:
  6.5 1.3 copy.24
  7.9 1.1 copy.25
  9.0 1.1 copy.26
  11.5 1.2 fusion.58
  12.7 5.6 %all-to-all-start = ((bf16[16,128,256]{1,2,0:T(8,128)(2,1)}), bf16[16,128,256]{1,2,0:T(8,128)(2,1)}, u32[]{:S(2)}, u32[]{:S(2)}) async-start(bf16[16,128,256]{1,2,0:T(8,128)(2,1)} %fusion.58), calls=%async_computation | async-start | bytes 2097152 | tf_op jit(solution)/shard_map/all_to_all | solution.py:79
  20.5 14.4 %all-to-all-done = bf16[16,128,256]{1,2,0:T(8,128)(2,1)} async-done(((bf16[16,128,256]{1,2,0:T(8,128)(2,1)}), bf16[16,128,256]{1,2,0:T(8,128)(2,1)}, u32[]{:S(2)}, u32[]{:S(2)}) %all-to-all-start) | async-done | bytes 1048608 | tf_op jit(solution)/shard_map/all_to_all | solution.py:79
  34.9 1.5 copy.27
  36.8 0.8 fusion.70
  38.4 0.9 add_reduce_fusion.3
  39.2 2.1 fusion
  41.3 1.0 fusion.36
  42.3 2.5 %fusion.2 = (f32[512]{0:T(512)S(1)}, f32[512]{0:T(512)S(1)}, f32[512]{0:T(512)S(1)}) fusion(f32[512,2048]{1,0:T(8,128)S(1)} %get-tuple-element.30, f32[512]{0:T(512)S(1)} %get-tuple-element.18, f32[2048]{0:T(1024)S(1)} %convert_reduce_fusion, f32[512]{0:T(512)S(1)} %get-tuple-element.19, f32[512,2048]{1,0:T(8,128)S(1)} %fusion.72, ...), kind=kLoop, calls=%fused_computation.10 | loop fusion | flops 9435648 | bytes 12603392 | tf_op jit(solution)/shard_map/reduce_sum | solution.py:17
  44.8 1.0 fusion.42
  45.7 1.0 fusion.48
  46.7 1.0 fusion.54
  48.4 3.7 %all-to-all-start.1 = ((bf16[16,128,64]{1,2,0:T(8,128)(2,1)}), bf16[16,128,64]{1,2,0:T(8,128)(2,1)S(1)}, u32[]{:S(2)}, u32[]{:S(2)}) async-start(bf16[16,128,64]{1,2,0:T(8,128)(2,1)} %copy_bitcast_fusion), calls=%async_computation.1 | async-start | bytes 524288 | tf_op jit(solution)/shard_map/all_to_all | solution.py:88
  52.2 10.9 %all-to-all-done.1 = bf16[16,128,64]{1,2,0:T(8,128)(2,1)S(1)} async-done(((bf16[16,128,64]{1,2,0:T(8,128)(2,1)}), bf16[16,128,64]{1,2,0:T(8,128)(2,1)S(1)}, u32[]{:S(2)}, u32[]{:S(2)}) %all-to-all-start.1) | async-done | bytes 262176 | tf_op jit(solution)/shard_map/all_to_all | solution.py:88
  64.4 1.0 reshape.210
  65.4 1.5 convolution_convert_fusion
  66.9 1.6 copy.32
  68.4 17.6 %all-to-all-start.2 = ((bf16[16,32,1024]{2,0,1:T(8,128)(2,1)}), bf16[16,32,1024]{2,0,1:T(8,128)(2,1)}, u32[]{:S(2)}, u32[]{:S(2)}) async-start(bf16[16,32,1024]{2,0,1:T(8,128)(2,1)} %copy.32), calls=%async_computation.2 | async-start | bytes 2097152 | tf_op jit(solution)/shard_map/all_to_all | solution.py:115
  86.0 2.2 all-gather.2.cloned.1.call-done
  88.2 1.9 collective-permute-start
  90.1 3.1 %constant_dynamic-update-slice_fusion.1 = bf16[2,1024,1024]{2,1,0:T(8,128)(2,1)} fusion(bf16[2,512,1024]{2,1,0:T(8,128)(2,1)} %all-gather.2.cloned.1.call-done), kind=kLoop, calls=%fused_computation.98 | loop fusion | bytes 4194304
  93.2 1.3 collective-permute-done
  94.4 1.5 constant_dynamic-update-slice_fusion
  95.9 45.5 %all-to-all-done.2 = bf16[16,32,1024]{2,0,1:T(8,128)(2,1)} async-done(((bf16[16,32,1024]{2,0,1:T(8,128)(2,1)}), bf16[16,32,1024]{2,0,1:T(8,128)(2,1)}, u32[]{:S(2)}, u32[]{:S(2)}) %all-to-all-start.2) | async-done | bytes 1048608 | tf_op jit(solution)/shard_map/all_to_all | solution.py:115
  141.4 6.1 %fusion.28 = bf16[16,32,1024]{2,1,0:T(8,128)(2,1)} fusion(bf16[2,1024,1024]{2,1,0:T(8,128)(2,1)} %constant_dynamic-update-slice_fusion, bf16[16,32,1024]{2,0,1:T(8,128)(2,1)} %all-to-all-done.2), kind=kOutput, calls=%fused_computation.37 | convolution fusion | flops 2152726528 | bytes 6291456 | tf_op jit(solution)/shard_map/csef,efd->csed/dot_general | solution.py:122
  147.5 2.8 %copy.34 = bf16[16,32,1024]{2,0,1:T(8,128)(2,1)} copy(bf16[16,32,1024]{2,1,0:T(8,128)(2,1)} %fusion.28) | data formatting | bytes 2097152 | tf_op jit(solution)/shard_map/reshape | solution.py:125
  150.3 4.5 %all-to-all-start.3 = ((bf16[16,32,1024]{2,0,1:T(8,128)(2,1)}), bf16[16,32,1024]{2,0,1:T(8,128)(2,1)}, u32[]{:S(2)}, u32[]{:S(2)}) async-start(bf16[16,32,1024]{2,0,1:T(8,128)(2,1)} %copy.34), calls=%async_computation.3 | async-start | bytes 2097152 | tf_op jit(solution)/shard_map/all_to_all | solution.py:126
  155.1 55.7 %all-to-all-done.3 = bf16[16,32,1024]{2,0,1:T(8,128)(2,1)} async-done(((bf16[16,32,1024]{2,0,1:T(8,128)(2,1)}), bf16[16,32,1024]{2,0,1:T(8,128)(2,1)}, u32[]{:S(2)}, u32[]{:S(2)}) %all-to-all-start.3) | async-done | bytes 1048608 | tf_op jit(solution)/shard_map/all_to_all | solution.py:126
  210.9 1.8 copy.35
  (47 shorter events, 8.3 us)
Async XLA Ops:
  6.5 56.6 %copy-start = (bf16[1024,1024]{1,0:T(8,128)(2,1)S(1)}, bf16[1024,1024]{1,0:T(8,128)(2,1)}, u32[]{:S(2)}) copy-start(bf16[1024,1024]{1,0:T(8,128)(2,1)} %param.21) | copy-start | bytes 6291460
  6.5 11.8 %copy-start.3 = (bf16[1,1024,64]{1,2,0:T(8,128)(2,1)S(1)}, bf16[1,1024,64]{1,2,0:T(8,128)(2,1)}, u32[]{:S(2)}) copy-start(bf16[1,1024,64]{1,2,0:T(8,128)(2,1)} %param.26) | copy-start | bytes 393220
  6.5 11.8 %copy-start.2 = (bf16[1,64,1024]{2,1,0:T(8,128)(2,1)S(1)}, bf16[1,64,1024]{2,1,0:T(8,128)(2,1)}, u32[]{:S(2)}) copy-start(bf16[1,64,1024]{2,1,0:T(8,128)(2,1)} %param.27) | copy-start | bytes 393220
  6.5 12.6 %copy-start.6 = (s32[1,128,2]{1,2,0:T(2,128)S(1)}, s32[1,128,2]{1,2,0:T(2,128)}, u32[]{:S(2)}) copy-start(s32[1,128,2]{1,2,0:T(2,128)} %param.24) | copy-start | bytes 3076
  6.5 13.9 %copy-start.4 = (f32[1,2,1024]{2,1,0:T(2,128)S(1)}, f32[1,2,1024]{2,1,0:T(2,128)}, u32[]{:S(2)}) copy-start(f32[1,2,1024]{2,1,0:T(2,128)} %param.23) | copy-start | bytes 24580
  12.7 22.2 %all-to-all-start = ((bf16[16,128,256]{1,2,0:T(8,128)(2,1)}), bf16[16,128,256]{1,2,0:T(8,128)(2,1)}, u32[]{:S(2)}, u32[]{:S(2)}) async-start(bf16[16,128,256]{1,2,0:T(8,128)(2,1)} %fusion.58), calls=%async_computation | async-start | bytes 2097152 | tf_op jit(solution)/shard_map/all_to_all | solution.py:79
  18.2 69.9 %all-gather.2.cloned.1.call-start = ((), (), s32[]{:S(2)}) async-start(), calls=%async_computation.4 | async-start | bytes 2359296 | tf_op jit(solution)/shard_map/all_gather | solution.py:55
  46.7 5.5 %copy-start.5 = (f32[1,2,1024]{2,1,0:T(2,128)S(1)}, f32[1,2,1024]{2,1,0:T(2,128)}, u32[]{:S(2)}) copy-start(f32[1,2,1024]{2,1,0:T(2,128)} %param.22) | copy-start | bytes 24580
  46.7 16.4 %copy-start.1 = (bf16[1,128,1024]{2,1,0:T(8,128)(2,1)S(1)}, bf16[1,128,1024]{2,1,0:T(8,128)(2,1)}, u32[]{:S(2)}) copy-start(bf16[1,128,1024]{2,1,0:T(8,128)(2,1)} %param.15) | copy-start | bytes 786436
  48.4 14.7 %all-to-all-start.1 = ((bf16[16,128,64]{1,2,0:T(8,128)(2,1)}), bf16[16,128,64]{1,2,0:T(8,128)(2,1)S(1)}, u32[]{:S(2)}, u32[]{:S(2)}) async-start(bf16[16,128,64]{1,2,0:T(8,128)(2,1)} %copy_bitcast_fusion), calls=%async_computation.1 | async-start | bytes 524288 | tf_op jit(solution)/shard_map/all_to_all | solution.py:88
  68.4 72.9 %all-to-all-start.2 = ((bf16[16,32,1024]{2,0,1:T(8,128)(2,1)}), bf16[16,32,1024]{2,0,1:T(8,128)(2,1)}, u32[]{:S(2)}, u32[]{:S(2)}) async-start(bf16[16,32,1024]{2,0,1:T(8,128)(2,1)} %copy.32), calls=%async_computation.2 | async-start | bytes 2097152 | tf_op jit(solution)/shard_map/all_to_all | solution.py:115
  88.2 6.3 %collective-permute-start = (bf16[2,512,1024]{2,1,0:T(8,128)(2,1)}, bf16[2,512,1024]{2,1,0:T(8,128)(2,1)S(1)}, u32[]{:S(2)}, u32[]{:S(2)}) collective-permute-start(bf16[2,512,1024]{2,1,0:T(8,128)(2,1)} %all-gather.2.cloned.1.call-done), channel_id=1, source_target_pairs={{0,32},{32,0},{64,96},{96,64},{128,160},{160,128},{192,224},{224,1... | collective-permute-start | bytes 6291464 | tf_op jit(solution)/shard_map/ppermute | solution.py:58
  147.5 65.2 %copy-start.7 = (f32[1,128,2]{1,2,0:T(2,128)S(1)}, f32[1,128,2]{1,2,0:T(2,128)}, u32[]{:S(2)}) copy-start(f32[1,128,2]{1,2,0:T(2,128)} %param.25) | copy-start | bytes 3076
  150.3 60.6 %all-to-all-start.3 = ((bf16[16,32,1024]{2,0,1:T(8,128)(2,1)}), bf16[16,32,1024]{2,0,1:T(8,128)(2,1)}, u32[]{:S(2)}, u32[]{:S(2)}) async-start(bf16[16,32,1024]{2,0,1:T(8,128)(2,1)} %copy.34), calls=%async_computation.3 | async-start | bytes 2097152 | tf_op jit(solution)/shard_map/all_to_all | solution.py:126
Sparse Core Ops, SparseCore 0:
  21.2 66.9 all-gather.1

commit v4 on v2

--- a/solution.py
+++ b/solution.py
@@ -107,10 +107,18 @@
     head_count = key_bias.shape[0]
     head_width = model_width // head_count
     score_scale = head_width ** (-0.5)
-    full_up, full_down = (
-        lax.all_gather(up_weight, "tm", axis=2, tiled=True),
-        lax.all_gather(down_weight, "tm", axis=1, tiled=True),
-    )
+    tm_count = lax.axis_size("tm")
+    parity_groups = [list(range(p, tm_count, 2)) for p in range(2)]
+    own_slices = jnp.stack([jnp.transpose(up_weight[0]), down_weight[0]])
+    parity_slices = lax.all_gather(
+        own_slices, "tm", axis=1, tiled=True, axis_index_groups=parity_groups
+    )
+    sibling_slices = lax.ppermute(
+        parity_slices, "tm", [(t, t ^ 1) for t in range(tm_count)]
+    )
+    both = jnp.concatenate([parity_slices, sibling_slices], axis=1)
+    full_up = jnp.transpose(both[0])[None]
+    full_down = both[1][None]
     scaled_queries = queries[0] * jnp.asarray(score_scale, jnp.bfloat16)
     offsets = jnp.where(
         inpaint_mask[0][:, None] == 1, key_bias[None, :], jnp.zeros((), jnp.bfloat16)
@@ -126,7 +134,7 @@
         axis=2,
     )
     packed = jnp.transpose(packed, (1, 0, 2))
-    gathered = exchange(packed, "tm", 0)
+    gathered = lax.all_to_all(packed, "tm", split_axis=0, concat_axis=0, tiled=True)
     clip_rows = gathered.reshape(-1, 4 * head_width)
     head_out = head_attention(
         clip_rows[:, :head_width],
@@ -135,7 +143,7 @@
         clip_rows[:, 3 * head_width].astype(jnp.float32),
     )
     head_out = head_out.reshape(head_count, tok_rows, head_width)
-    attended_heads = exchange(head_out, "tm", 1)
+    attended_heads = lax.all_to_all(head_out, "tm", split_axis=0, concat_axis=0, tiled=True)
     projected = jnp.einsum(
         "hid,hdo->io",
         attended_heads,
@@ -155,29 +163,28 @@
         jnp.int32
     )
     ranks = jnp.sum((jnp.cumsum(hits, axis=0) - 1) * hits, axis=1)
-    target = ranks * expert_count + choice_list
+    target = choice_list * capacity + ranks
     placing = (
         jnp.arange(capacity * expert_count, dtype=jnp.int32)[:, None] == target[None, :]
     ).astype(jnp.bfloat16)
     doubled = jnp.repeat(normed, 2, axis=0)
     slots = jnp.dot(placing, doubled, preferred_element_type=jnp.float32).astype(jnp.bfloat16)
-    slots = slots.reshape(capacity, expert_count, model_width)
-    arrived = lax.all_to_all(slots, "expert", split_axis=1, concat_axis=1, tiled=True)
-    slot_count = arrived.shape[0]
-    grouped = arrived.reshape(slot_count, source_count, local_experts, model_width)
+    slots = slots.reshape(expert_count, capacity, model_width)
+    arrived = exchange(slots, "expert", 2)
+    grouped = arrived.reshape(source_count, local_experts, capacity, model_width)
     hidden = jax.nn.gelu(
-        jnp.einsum("csed,edf->csef", grouped, full_up, preferred_element_type=jnp.float32),
+        jnp.einsum("secd,edf->secf", grouped, full_up, preferred_element_type=jnp.float32),
         approximate=True,
     ).astype(jnp.bfloat16)
     produced = jnp.einsum(
-        "csef,efd->csed", hidden, full_down, preferred_element_type=jnp.float32
+        "secf,efd->secd", hidden, full_down, preferred_element_type=jnp.float32
     ).astype(jnp.bfloat16)
-    produced = produced.reshape(slot_count, source_count * local_experts, model_width)
-    returned = lax.all_to_all(produced, "expert", split_axis=1, concat_axis=1, tiled=True)
+    produced = produced.reshape(source_count * local_experts, capacity, model_width)
+    returned = exchange(produced, "expert", 3)
     picked = jnp.einsum(
         "sa,sd->ad",
         placing,
-        returned.reshape(capacity * expert_count, model_width),
+        returned.reshape(expert_count * capacity, model_width),
         preferred_element_type=jnp.float32,
     )
     picked = picked.reshape(tok_rows, 2, model_width)

time: 235 us -> 240 us (1.021)
  the two profiles are of different devices: /device:TPU:32 before, /device:TPU:8 now
where the time goes in v4:
time: 240 us; the launch traced here: 239 us
  Pallas kernels  118 us (49%)
  waiting for transfers between devices  50.4 us (21%)
  matrix products  19 us (8%)
  starting transfers between devices  17.5 us (7%)
  between operations  13.7 us (6%)
  local copies, waits for them, and re-layouts  10.6 us (4%)
  other arithmetic  9.86 us (4%)
    pallas_call x2, Pallas kernels, exchange(): pl.pallas_call(functools.partial(exchange_kernel, axis, n), out_shape=jax...  118 us
    all_gather x1, waiting for transfers between devices, on_device(): lax.all_gather(own_slices, 'tm', axis=1, tiled=True, axis_index_groups=pa...  33.4 us
    all_to_all x1, waiting for transfers between devices, on_device(): lax.all_to_all(packed, 'tm', split_axis=0, concat_axis=0, tiled=True)  11.7 us
    all_to_all x1, starting transfers between devices, on_device(): lax.all_to_all(packed, 'tm', split_axis=0, concat_axis=0, tiled=True)  9.91 us
    all_to_all x1, starting transfers between devices, on_device(): lax.all_to_all(head_out, 'tm', split_axis=0, concat_axis=0, tiled=True)  5.62 us
    unnamed x21, local copies, waits for them, and re-layouts  5.51 us
    all_to_all x1, waiting for transfers between devices, on_device(): lax.all_to_all(head_out, 'tm', split_axis=0, concat_axis=0, tiled=True)  5.31 us
  transfers between devices with their start and end apart: 4, of which 3 were waited for; matrix products, arithmetic and copies ran while one was open for 10% of the time, Pallas kernels for 26%

profile of v4, /device:TPU:8, one launch (start us, length us, event | category | flops | bytes accessed | tf_op | source)
XLA Modules:
  0.0 239.4 jit_solution(704016720919162729)
XLA Ops:
  6.5 1.3 copy.17
  7.8 1.1 copy.18
  9.0 1.1 copy.19
  11.5 1.1 fusion.58
  12.6 9.9 %all-to-all-start = ((bf16[16,128,256]{1,2,0:T(8,128)(2,1)}), bf16[16,128,256]{1,2,0:T(8,128)(2,1)}, u32[]{:S(2)}, u32[]{:S(2)}) async-start(bf16[16,128,256]{1,2,0:T(8,128)(2,1)} %fusion.58), calls=%async_computation | async-start | bytes 2097152 | tf_op jit(solution)/shard_map/all_to_all | solution.py:137
  24.9 11.7 %all-to-all-done = bf16[16,128,256]{1,2,0:T(8,128)(2,1)} async-done(((bf16[16,128,256]{1,2,0:T(8,128)(2,1)}), bf16[16,128,256]{1,2,0:T(8,128)(2,1)}, u32[]{:S(2)}, u32[]{:S(2)}) %all-to-all-start) | async-done | bytes 1048608 | tf_op jit(solution)/shard_map/all_to_all | solution.py:137
  36.6 1.5 copy.20
  38.1 0.8 fusion.66
  39.2 0.8 fusion.68
  40.0 0.9 add_reduce_fusion.3
  40.9 2.1 fusion
  43.0 1.0 fusion.36
  44.0 2.5 %fusion.2 = (f32[512]{0:T(512)S(1)}, f32[512]{0:T(512)S(1)}, f32[512]{0:T(512)S(1)}) fusion(f32[512,2048]{1,0:T(8,128)S(1)} %get-tuple-element.30, f32[512]{0:T(512)S(1)} %get-tuple-element.18, f32[2048]{0:T(1024)S(1)} %convert_reduce_fusion, f32[512]{0:T(512)S(1)} %get-tuple-element.19, f32[512,2048]{1,0:T(8,128)S(1)} %fusion.68, ...), kind=kLoop, calls=%fused_computation.10 | loop fusion | flops 9435648 | bytes 12603392 | tf_op jit(solution)/shard_map/reduce_sum | solution.py:21
  46.5 1.0 fusion.42
  47.5 1.0 fusion.48
  48.5 1.6 fusion.54
  50.1 33.4 %all-gather.2.cloned.1.call-done = bf16[2,512,1024]{2,1,0:T(8,128)(2,1)} async-done(((bf16[2,64,1024]{2,1,0:T(8,128)(2,1)}), bf16[2,512,1024]{2,1,0:T(8,128)(2,1)}) %all-gather.2.cloned.1.call-update) | async-done | bytes 2097168 | tf_op jit(solution)/shard_map/all_gather | solution.py:113
  83.5 1.9 collective-permute-start
  85.4 1.6 copy_bitcast_fusion
  87.0 5.6 %all-to-all-start.1 = ((bf16[16,128,64]{1,2,0:T(8,128)(2,1)}), bf16[16,128,64]{1,2,0:T(8,128)(2,1)S(1)}, u32[]{:S(2)}, u32[]{:S(2)}) async-start(bf16[16,128,64]{1,2,0:T(8,128)(2,1)} %copy_bitcast_fusion), calls=%async_computation.1 | async-start | bytes 524288 | tf_op jit(solution)/shard_map/all_to_all | solution.py:146
  92.8 5.3 %all-to-all-done.1 = bf16[16,128,64]{1,2,0:T(8,128)(2,1)S(1)} async-done(((bf16[16,128,64]{1,2,0:T(8,128)(2,1)}), bf16[16,128,64]{1,2,0:T(8,128)(2,1)S(1)}, u32[]{:S(2)}, u32[]{:S(2)}) %all-to-all-start.1) | async-done | bytes 262176 | tf_op jit(solution)/shard_map/all_to_all | solution.py:146
  98.2 1.5 fusion.84
  100.3 1.0 reshape.210
  101.3 2.5 %convolution_convert_fusion = bf16[512,1024]{1,0:T(8,128)(2,1)} fusion(bf16[256,1024]{1,0:T(8,128)(2,1)} %reshape.210, s32[256]{0:T(256)S(1)} %multiply_add_fusion), kind=kOutput, calls=%fused_computation.35 | convolution fusion | flops 269090816 | bytes 1573888 | tf_op jit(solution)/shard_map/dot_general | solution.py:171
  103.8 61.9 %shard_map.127 = bf16[32,16,1024]{2,1,0:T(8,128)(2,1)} custom-call(bf16[32,16,1024]{2,1,0:T(8,128)(2,1)} %bitcast.98), custom_call_target="tpu_custom_call" | custom-call | tf_op jit(solution)/shard_map/pallas_call | solution.py:69
  165.7 1.9 constant_dynamic-update-slice_fusion.1
  167.6 1.8 constant_dynamic-update-slice_fusion
  169.4 1.9 fusion.29
  171.3 2.4 fusion.28.x_ref
  173.6 56.4 %shard_map.128 = bf16[32,16,1024]{2,1,0:T(8,128)(2,1)} custom-call(bf16[32,16,1024]{2,1,0:T(8,128)(2,1)} %fusion.28.x_ref), custom_call_target="tpu_custom_call" | custom-call | tf_op jit(solution)/shard_map/pallas_call | solution.py:69
  230.1 1.7 fusion.30
  231.8 0.8 fusion.74
  (43 shorter events, 4.9 us)
Async XLA Ops:
  6.5 91.6 %copy-start = (bf16[1024,1024]{1,0:T(8,128)(2,1)S(1)}, bf16[1024,1024]{1,0:T(8,128)(2,1)}, u32[]{:S(2)}) copy-start(bf16[1024,1024]{1,0:T(8,128)(2,1)} %param.21) | copy-start | bytes 6291460
  6.5 16.0 %copy-start.3 = (bf16[1,1024,64]{1,2,0:T(8,128)(2,1)S(1)}, bf16[1,1024,64]{1,2,0:T(8,128)(2,1)}, u32[]{:S(2)}) copy-start(bf16[1,1024,64]{1,2,0:T(8,128)(2,1)} %param.26) | copy-start | bytes 393220
  6.5 16.1 %copy-start.2 = (bf16[1,64,1024]{2,1,0:T(8,128)(2,1)S(1)}, bf16[1,64,1024]{2,1,0:T(8,128)(2,1)}, u32[]{:S(2)}) copy-start(bf16[1,64,1024]{2,1,0:T(8,128)(2,1)} %param.27) | copy-start | bytes 393220
  6.5 16.8 %copy-start.6 = (s32[1,128,2]{1,2,0:T(2,128)S(1)}, s32[1,128,2]{1,2,0:T(2,128)}, u32[]{:S(2)}) copy-start(s32[1,128,2]{1,2,0:T(2,128)} %param.24) | copy-start | bytes 3076
  12.6 23.9 %all-to-all-start = ((bf16[16,128,256]{1,2,0:T(8,128)(2,1)}), bf16[16,128,256]{1,2,0:T(8,128)(2,1)}, u32[]{:S(2)}, u32[]{:S(2)}) async-start(bf16[16,128,256]{1,2,0:T(8,128)(2,1)} %fusion.58), calls=%async_computation | async-start | bytes 2097152 | tf_op jit(solution)/shard_map/all_to_all | solution.py:137
  22.5 60.9 %all-gather.2.cloned.1.call-start = ((), (), s32[]{:S(2)}) async-start(), calls=%async_computation.2 | async-start | bytes 2359296 | tf_op jit(solution)/shard_map/all_gather | solution.py:113
  48.5 44.2 %copy-start.4 = (f32[1,2,1024]{2,1,0:T(2,128)S(1)}, f32[1,2,1024]{2,1,0:T(2,128)}, u32[]{:S(2)}) copy-start(f32[1,2,1024]{2,1,0:T(2,128)} %param.23) | copy-start | bytes 24580
  48.5 44.3 %copy-start.5 = (f32[1,2,1024]{2,1,0:T(2,128)S(1)}, f32[1,2,1024]{2,1,0:T(2,128)}, u32[]{:S(2)}) copy-start(f32[1,2,1024]{2,1,0:T(2,128)} %param.22) | copy-start | bytes 24580
  83.5 84.1 %collective-permute-start = (bf16[2,512,1024]{2,1,0:T(8,128)(2,1)}, bf16[2,512,1024]{2,1,0:T(8,128)(2,1)}, u32[]{:S(2)}, u32[]{:S(2)}) collective-permute-start(bf16[2,512,1024]{2,1,0:T(8,128)(2,1)} %all-gather.2.cloned.1.call-done), channel_id=1, source_target_pairs={{0,32},{32,0},{64,96},{96,64},{128,160},{160,128},{192,224},{224,1... | collective-permute-start | bytes 6291464 | tf_op jit(solution)/shard_map/ppermute | solution.py:116
  87.0 11.1 %all-to-all-start.1 = ((bf16[16,128,64]{1,2,0:T(8,128)(2,1)}), bf16[16,128,64]{1,2,0:T(8,128)(2,1)S(1)}, u32[]{:S(2)}, u32[]{:S(2)}) async-start(bf16[16,128,64]{1,2,0:T(8,128)(2,1)} %copy_bitcast_fusion), calls=%async_computation.1 | async-start | bytes 524288 | tf_op jit(solution)/shard_map/all_to_all | solution.py:146
  165.7 3.6 %copy-start.1 = (bf16[32,16,1024]{2,1,0:T(8,128)(2,1)S(1)}, bf16[32,16,1024]{2,1,0:T(8,128)(2,1)}, u32[]{:S(2)}) copy-start(bf16[32,16,1024]{2,1,0:T(8,128)(2,1)} %shard_map.127) | copy-start | bytes 3145732
  171.3 58.8 %copy-start.7 = (f32[1,128,2]{1,2,0:T(2,128)S(1)}, f32[1,128,2]{1,2,0:T(2,128)}, u32[]{:S(2)}) copy-start(f32[1,128,2]{1,2,0:T(2,128)} %param.25) | copy-start | bytes 3076
Sparse Core Ops, SparseCore 0:
  25.5 57.9 all-gather.1

commit v5 on v4

--- a/solution.py
+++ b/solution.py
@@ -80,6 +80,96 @@
     )(x)
 
 
+def dispatch_kernel(
+    expert_n, tm_n, slots_ref, own_ref, arrived_ref, gathered_ref,
+    send_sems, recv_sems, weight_send_sems, weight_recv_sems, local_sems,
+):
+    mesh_ids = pl.DeviceIdType.MESH
+    me_e = lax.axis_index("expert")
+    me_t = lax.axis_index("tm")
+    barrier = pltpu.get_barrier_semaphore()
+    for k in range(1, expert_n):
+        pl.semaphore_signal(barrier, inc=1, device_id={"expert": lax.rem(me_e + k, expert_n)}, device_id_type=mesh_ids)
+    for k in range(1, tm_n):
+        pl.semaphore_signal(barrier, inc=1, device_id={"tm": lax.rem(me_t + k, tm_n)}, device_id_type=mesh_ids)
+    pl.semaphore_wait(barrier, expert_n - 1 + tm_n - 1)
+    local_slots = pltpu.make_async_copy(slots_ref.at[me_e], arrived_ref.at[me_e], local_sems.at[0])
+    local_weights = pltpu.make_async_copy(own_ref, gathered_ref.at[me_t], local_sems.at[1])
+    local_slots.start()
+    local_weights.start()
+    copies = []
+    for k in range(1, max(expert_n, tm_n)):
+        if k < tm_n:
+            peer = lax.rem(me_t + k, tm_n)
+            copy = pltpu.make_async_remote_copy(
+                src_ref=own_ref,
+                dst_ref=gathered_ref.at[me_t],
+                send_sem=weight_send_sems.at[k],
+                recv_sem=weight_recv_sems.at[k],
+                device_id={"tm": peer},
+                device_id_type=mesh_ids,
+            )
+            copy.start()
+            copies.append(copy)
+        if k < expert_n:
+            peer = lax.rem(me_e + k, expert_n)
+            copy = pltpu.make_async_remote_copy(
+                src_ref=slots_ref.at[peer],
+                dst_ref=arrived_ref.at[me_e],
+                send_sem=send_sems.at[k],
+                recv_sem=recv_sems.at[k],
+                device_id={"expert": peer},
+                device_id_type=mesh_ids,
+            )
+            copy.start()
+            copies.append(copy)
+    local_slots.wait()
+    local_weights.wait()
+    for copy in copies:
+        copy.wait_send()
+    for k in range(1, expert_n):
+        source = lax.rem(me_e + expert_n - k, expert_n)
+        pltpu.make_async_remote_copy(
+            src_ref=slots_ref.at[source],
+            dst_ref=arrived_ref.at[source],
+            send_sem=send_sems.at[k],
+            recv_sem=recv_sems.at[k],
+            device_id={"expert": source},
+            device_id_type=mesh_ids,
+        ).wait_recv()
+    for k in range(1, tm_n):
+        source = lax.rem(me_t + tm_n - k, tm_n)
+        pltpu.make_async_remote_copy(
+            src_ref=own_ref,
+            dst_ref=gathered_ref.at[source],
+            send_sem=weight_send_sems.at[k],
+            recv_sem=weight_recv_sems.at[k],
+            device_id={"tm": source},
+            device_id_type=mesh_ids,
+        ).wait_recv()
+
+
+def dispatch(slots, own_slices, tm_n, collective_id):
+    expert_n = slots.shape[0]
+    return pl.pallas_call(
+        functools.partial(dispatch_kernel, expert_n, tm_n),
+        out_shape=(
+            jax.ShapeDtypeStruct(slots.shape, slots.dtype),
+            jax.ShapeDtypeStruct((tm_n,) + own_slices.shape, own_slices.dtype),
+        ),
+        in_specs=[pl.BlockSpec(memory_space=pl.ANY)] * 2,
+        out_specs=(pl.BlockSpec(memory_space=pl.ANY), pl.BlockSpec(memory_space=pl.ANY)),
+        scratch_shapes=[
+            pltpu.SemaphoreType.DMA((expert_n,)),
+            pltpu.SemaphoreType.DMA((expert_n,)),
+            pltpu.SemaphoreType.DMA((tm_n,)),
+            pltpu.SemaphoreType.DMA((tm_n,)),
+            pltpu.SemaphoreType.DMA((2,)),
+        ],
+        compiler_params=pltpu.CompilerParams(collective_id=collective_id, has_side_effects=True),
+    )(slots, own_slices)
+
+
 def layer_norm(mixed, shift_row, scale_row):
     center = jnp.mean(mixed, axis=-1, keepdims=True)
     deviation = mixed - center
@@ -107,18 +197,6 @@
     head_count = key_bias.shape[0]
     head_width = model_width // head_count
     score_scale = head_width ** (-0.5)
-    tm_count = lax.axis_size("tm")
-    parity_groups = [list(range(p, tm_count, 2)) for p in range(2)]
-    own_slices = jnp.stack([jnp.transpose(up_weight[0]), down_weight[0]])
-    parity_slices = lax.all_gather(
-        own_slices, "tm", axis=1, tiled=True, axis_index_groups=parity_groups
-    )
-    sibling_slices = lax.ppermute(
-        parity_slices, "tm", [(t, t ^ 1) for t in range(tm_count)]
-    )
-    both = jnp.concatenate([parity_slices, sibling_slices], axis=1)
-    full_up = jnp.transpose(both[0])[None]
-    full_down = both[1][None]
     scaled_queries = queries[0] * jnp.asarray(score_scale, jnp.bfloat16)
     offsets = jnp.where(
         inpaint_mask[0][:, None] == 1, key_bias[None, :], jnp.zeros((), jnp.bfloat16)
@@ -170,15 +248,16 @@
     doubled = jnp.repeat(normed, 2, axis=0)
     slots = jnp.dot(placing, doubled, preferred_element_type=jnp.float32).astype(jnp.bfloat16)
     slots = slots.reshape(expert_count, capacity, model_width)
-    arrived = exchange(slots, "expert", 2)
-    grouped = arrived.reshape(source_count, local_experts, capacity, model_width)
+    own_slices = jnp.stack([jnp.transpose(up_weight[0]), down_weight[0]])
+    arrived, gathered_slices = dispatch(slots, own_slices, lax.axis_size("tm"), 2)
+    up_rows = gathered_slices[:, 0].reshape(-1, model_width)
+    down_rows = gathered_slices[:, 1].reshape(-1, model_width)
+    grouped = arrived.reshape(source_count * local_experts * capacity, model_width)
     hidden = jax.nn.gelu(
-        jnp.einsum("secd,edf->secf", grouped, full_up, preferred_element_type=jnp.float32),
+        jnp.einsum("rd,fd->rf", grouped, up_rows, preferred_element_type=jnp.float32),
         approximate=True,
     ).astype(jnp.bfloat16)
-    produced = jnp.einsum(
-        "secf,efd->secd", hidden, full_down, preferred_element_type=jnp.float32
-    ).astype(jnp.bfloat16)
+    produced = jnp.dot(hidden, down_rows, preferred_element_type=jnp.float32).astype(jnp.bfloat16)
     produced = produced.reshape(source_count * local_experts, capacity, model_width)
     returned = exchange(produced, "expert", 3)
     picked = jnp.einsum(

time: 240 us -> 208 us (0.87)
  waiting for transfers between devices: 50.4 us -> 16.3 us
  Pallas kernels: 118 us -> 133 us
  between operations: 13.7 us -> 0.25 us
    pallas_call x0 -> x1, Pallas kernels: none -> 73.6 us  [dispatch(): pl.pallas_call(functools.partial(dispatch_kernel, expert_n, tm_n), out_sh...]
    pallas_call x2 -> x1, Pallas kernels: 118 us -> 59.9 us  [exchange(): pl.pallas_call(functools.partial(exchange_kernel, axis, n), out_shape=jax...]
    all_gather x1 -> x0, waiting for transfers between devices: 33.4 us -> none  [on_device(): lax.all_gather(own_slices, 'tm', axis=1, tiled=True, axis_index_groups=pa...]
    slice x0 -> x1, local copies, waits for them, and re-layouts: none -> 4.92 us  [on_device(): up_rows = gathered_slices[:, 0].reshape(-1, model_width)]
    unnamed x21 -> x16, local copies, waits for them, and re-layouts: 5.51 us -> 3.65 us
    dot_general x2 -> x1, matrix products: 4.23 us -> 6.02 us  [on_device(): jnp.dot(hidden, down_rows, preferred_element_type=jnp.float32)]
  transfers between devices with their start and end apart: 4 -> 2, of which waited for: 3 -> 2; matrix products, arithmetic and copies ran while one was open for 10% -> 2% of each run, Pallas kernels for 26% -> 0%
where the time goes in v5:
time: 208 us
  Pallas kernels  133 us (64%)
  matrix products  20 us (10%)
  waiting for transfers between devices  16.3 us (8%)
  starting transfers between devices  16.1 us (8%)
  local copies, waits for them, and re-layouts  11.9 us (6%)
  other arithmetic  9.81 us (5%)
    pallas_call x1, Pallas kernels, dispatch(): pl.pallas_call(functools.partial(dispatch_kernel, expert_n, tm_n), out_sh...  73.6 us
    pallas_call x1, Pallas kernels, exchange(): pl.pallas_call(functools.partial(exchange_kernel, axis, n), out_shape=jax...  59.9 us
    all_to_all x1, waiting for transfers between devices, on_device(): lax.all_to_all(packed, 'tm', split_axis=0, concat_axis=0, tiled=True)  12.5 us
    all_to_all x1, starting transfers between devices, on_device(): lax.all_to_all(packed, 'tm', split_axis=0, concat_axis=0, tiled=True)  9.9 us
    all_to_all x1, starting transfers between devices, on_device(): lax.all_to_all(head_out, 'tm', split_axis=0, concat_axis=0, tiled=True)  6.17 us
    dot_general x1, matrix products, on_device(): jnp.dot(hidden, down_rows, preferred_element_type=jnp.float32)  6.02 us
    slice x1, local copies, waits for them, and re-layouts, on_device(): up_rows = gathered_slices[:, 0].reshape(-1, model_width)  4.92 us
    dot_general x4, matrix products, head_attention(): jnp.dot(block, key_rows.T, preferred_element_type=jnp.float32)  4.52 us
  transfers between devices with their start and end apart: 2, of which 2 were waited for; matrix products, arithmetic and copies ran while one was open for 2% of the time, Pallas kernels for 0%

profile of v5, /device:TPU:8, one launch (start us, length us, event | category | flops | bytes accessed | tf_op | source)
XLA Modules:
  0.0 207.9 jit_solution(17278124498544787790)
XLA Ops:
  0.0 1.3 copy.15
  1.3 1.1 copy.16
  2.4 1.1 copy.17
  3.6 0.7 compare_bitcast_fusion
  4.2 0.7 broadcast_select_fusion
  5.0 1.2 fusion.53
  6.1 9.9 %all-to-all-start = ((bf16[16,128,256]{1,2,0:T(8,128)(2,1)}), bf16[16,128,256]{1,2,0:T(8,128)(2,1)}, u32[]{:S(2)}, u32[]{:S(2)}) async-start(bf16[16,128,256]{1,2,0:T(8,128)(2,1)} %fusion.53), calls=%async_computation | async-start | bytes 2097152 | tf_op jit(solution)/shard_map/all_to_all | solution.py:215
  17.6 12.5 %all-to-all-done = bf16[16,128,256]{1,2,0:T(8,128)(2,1)} async-done(((bf16[16,128,256]{1,2,0:T(8,128)(2,1)}), bf16[16,128,256]{1,2,0:T(8,128)(2,1)}, u32[]{:S(2)}, u32[]{:S(2)}) %all-to-all-start) | async-done | bytes 1048608 | tf_op jit(solution)/shard_map/all_to_all | solution.py:215
  30.1 1.5 copy.18
  32.0 0.8 fusion.64
  32.8 0.8 fusion.66
  33.6 0.9 add_reduce_fusion.3
  34.4 2.1 fusion
  36.5 1.0 fusion.31
  37.5 2.5 %fusion.2 = (f32[512]{0:T(512)S(1)}, f32[512]{0:T(512)S(1)}, f32[512]{0:T(512)S(1)}) fusion(f32[512,2048]{1,0:T(8,128)S(1)} %get-tuple-element.36, f32[512]{0:T(512)S(1)} %get-tuple-element.22, f32[2048]{0:T(1024)S(1)} %convert_reduce_fusion, f32[512]{0:T(512)S(1)} %get-tuple-element.23, f32[512,2048]{1,0:T(8,128)S(1)} %fusion.66, ...), kind=kLoop, calls=%fused_computation.10 | loop fusion | flops 9435648 | bytes 12603392 | tf_op jit(solution)/shard_map/reduce_sum | solution.py:21
  40.0 1.0 fusion.37
  40.9 1.0 fusion.43
  41.9 1.0 fusion.49
  42.9 0.8 copy_bitcast_fusion
  43.6 6.2 %all-to-all-start.1 = ((bf16[16,128,64]{1,2,0:T(8,128)(2,1)}), bf16[16,128,64]{1,2,0:T(8,128)(2,1)S(1)}, u32[]{:S(2)}, u32[]{:S(2)}) async-start(bf16[16,128,64]{1,2,0:T(8,128)(2,1)} %copy_bitcast_fusion), calls=%async_computation.1 | async-start | bytes 524288 | tf_op jit(solution)/shard_map/all_to_all | solution.py:224
  49.8 0.7 pad_maximum_fusion.own_ref
  50.7 0.8 slice_add_fusion
  51.5 3.8 %all-to-all-done.1 = bf16[16,128,64]{1,2,0:T(8,128)(2,1)S(1)} async-done(((bf16[16,128,64]{1,2,0:T(8,128)(2,1)}), bf16[16,128,64]{1,2,0:T(8,128)(2,1)S(1)}, u32[]{:S(2)}, u32[]{:S(2)}) %all-to-all-start.1) | async-done | bytes 262176 | tf_op jit(solution)/shard_map/all_to_all | solution.py:224
  55.3 1.5 fusion.87
  57.5 1.0 reshape.198
  58.5 2.5 %convolution_convert_fusion.1 = bf16[512,1024]{1,0:T(8,128)(2,1)} fusion(bf16[256,1024]{1,0:T(8,128)(2,1)} %reshape.198, s32[256]{0:T(256)S(1)} %multiply_add_fusion), kind=kOutput, calls=%fused_computation.32 | convolution fusion | flops 269090816 | bytes 1573888 | tf_op jit(solution)/shard_map/dot_general | solution.py:249
  61.0 73.6 %shard_map.127 = (bf16[32,16,1024]{2,1,0:T(8,128)(2,1)}, bf16[16,2,64,1024]{3,2,1,0:T(8,128)(2,1)}) custom-call(bf16[32,16,1024]{2,1,0:T(8,128)(2,1)} %bitcast.75, bf16[2,64,1024]{2,1,0:T(8,128)(2,1)} %pad_maximum_fusion.own_ref), custom_call_target="tpu_custom_call" | custom-call | tf_op jit(solution)/shard_map/pallas_call | solution.py:154
  134.5 4.9 %fusion.85 = (bf16[16,1,64,1024]{3,2,1,0:T(8,128)(2,1)}, bf16[16,1,64,1024]{3,2,1,0:T(8,128)(2,1)}) fusion(bf16[16,2,64,1024]{3,2,1,0:T(8,128)(2,1)} %get-tuple-element.20), kind=kLoop, calls=%fused_computation.99 | loop fusion | bytes 8388608 | tf_op jit(solution)/shard_map/slice | solution.py:253
  139.5 6.0 %convolution_convert_fusion = bf16[512,1024]{1,0:T(8,128)(2,1)} fusion(bf16[1024,1024]{1,0:T(8,128)(2,1)} %bitcast.77, bf16[512,1024]{1,0:T(8,128)(2,1)} %bitcast.88, bf16[1024,1024]{1,0:T(8,128)(2,1)} %bitcast.76), kind=kOutput, calls=%fused_computation.31 | convolution fusion | flops 2152726528 | bytes 6291456 | tf_op jit(solution)/shard_map/dot_general | solution.py:260
  145.5 59.9 %shard_map.128 = bf16[32,16,1024]{2,1,0:T(8,128)(2,1)} custom-call(bf16[32,16,1024]{2,1,0:T(8,128)(2,1)} %bitcast.81), custom_call_target="tpu_custom_call" | custom-call | tf_op jit(solution)/shard_map/pallas_call | solution.py:69
  205.4 1.7 fusion.25
  207.1 0.8 fusion.72
  (32 shorter events, 2.7 us)
Async XLA Ops:
  0.0 55.3 %copy-start = (bf16[1024,1024]{1,0:T(8,128)(2,1)S(1)}, bf16[1024,1024]{1,0:T(8,128)(2,1)}, u32[]{:S(2)}) copy-start(bf16[1024,1024]{1,0:T(8,128)(2,1)} %param.21) | copy-start | bytes 6291460
  0.0 16.0 %copy-start.4 = (s32[1,128,2]{1,2,0:T(2,128)S(1)}, s32[1,128,2]{1,2,0:T(2,128)}, u32[]{:S(2)}) copy-start(s32[1,128,2]{1,2,0:T(2,128)} %param.24) | copy-start | bytes 3076
  0.0 17.4 %copy-start.3 = (f32[1,2,1024]{2,1,0:T(2,128)S(1)}, f32[1,2,1024]{2,1,0:T(2,128)}, u32[]{:S(2)}) copy-start(f32[1,2,1024]{2,1,0:T(2,128)} %param.23) | copy-start | bytes 24580
  6.1 23.9 %all-to-all-start = ((bf16[16,128,256]{1,2,0:T(8,128)(2,1)}), bf16[16,128,256]{1,2,0:T(8,128)(2,1)}, u32[]{:S(2)}, u32[]{:S(2)}) async-start(bf16[16,128,256]{1,2,0:T(8,128)(2,1)} %fusion.53), calls=%async_computation | async-start | bytes 2097152 | tf_op jit(solution)/shard_map/all_to_all | solution.py:215
  41.9 7.9 %copy-start.1 = (bf16[1,64,1024]{2,1,0:T(8,128)(2,1)S(1)}, bf16[1,64,1024]{2,1,0:T(8,128)(2,1)}, u32[]{:S(2)}) copy-start(bf16[1,64,1024]{2,1,0:T(8,128)(2,1)} %param.27) | copy-start | bytes 393220
  41.9 7.9 %copy-start.2 = (bf16[1,1024,64]{1,2,0:T(8,128)(2,1)S(1)}, bf16[1,1024,64]{1,2,0:T(8,128)(2,1)}, u32[]{:S(2)}) copy-start(bf16[1,1024,64]{1,2,0:T(8,128)(2,1)} %param.26) | copy-start | bytes 393220
  43.6 11.7 %all-to-all-start.1 = ((bf16[16,128,64]{1,2,0:T(8,128)(2,1)}), bf16[16,128,64]{1,2,0:T(8,128)(2,1)S(1)}, u32[]{:S(2)}, u32[]{:S(2)}) async-start(bf16[16,128,64]{1,2,0:T(8,128)(2,1)} %copy_bitcast_fusion), calls=%async_computation.1 | async-start | bytes 524288 | tf_op jit(solution)/shard_map/all_to_all | solution.py:224
  139.5 65.9 %copy-start.5 = (f32[1,128,2]{1,2,0:T(2,128)S(1)}, f32[1,128,2]{1,2,0:T(2,128)}, u32[]{:S(2)}) copy-start(f32[1,128,2]{1,2,0:T(2,128)} %param.25) | copy-start | bytes 3076

commit v6 on v5

--- a/solution.py
+++ b/solution.py
@@ -212,7 +212,7 @@
         axis=2,
     )
     packed = jnp.transpose(packed, (1, 0, 2))
-    gathered = lax.all_to_all(packed, "tm", split_axis=0, concat_axis=0, tiled=True)
+    gathered = exchange(packed, "tm", 0)
     clip_rows = gathered.reshape(-1, 4 * head_width)
     head_out = head_attention(
         clip_rows[:, :head_width],
@@ -221,7 +221,7 @@
         clip_rows[:, 3 * head_width].astype(jnp.float32),
     )
     head_out = head_out.reshape(head_count, tok_rows, head_width)
-    attended_heads = lax.all_to_all(head_out, "tm", split_axis=0, concat_axis=0, tiled=True)
+    attended_heads = exchange(head_out, "tm", 1)
     projected = jnp.einsum(
         "hid,hdo->io",
         attended_heads,

time: 208 us -> 214 us (1.029)
  Pallas kernels: 133 us -> 166 us
  waiting for transfers between devices: 16.3 us -> 0 us
  starting transfers between devices: 16.1 us -> 0 us
  local copies, waits for them, and re-layouts: 11.9 us -> 14.6 us
    pallas_call x1 -> x3, Pallas kernels: 59.9 us -> 92.3 us  [exchange(): pl.pallas_call(functools.partial(exchange_kernel, axis, n), out_shape=jax...]
    all_to_all x2 -> x0, waiting for transfers between devices: 16.3 us -> none  [the longest x1 12.5 us: on_device(): lax.all_to_all(packed, 'tm', split_axis=0, concat_axis=0, tiled=True)]
    all_to_all x2 -> x0, starting transfers between devices: 16.1 us -> none  [the longest x1 9.9 us: on_device(): lax.all_to_all(packed, 'tm', split_axis=0, concat_axis=0, tiled=True)]
    unnamed x16 -> x25, local copies, waits for them, and re-layouts: 3.65 us -> 5.22 us
  transfers between devices with their start and end apart: 2 -> 0, of which waited for: 2 -> 0; matrix products, arithmetic and copies ran while one was open for 2% -> 0% of each run, Pallas kernels for 0% -> 0%
where the time goes in v6:
time: 214 us; the launch traced here: 213 us
  Pallas kernels  166 us (78%)
  matrix products  21.4 us (10%)
  local copies, waits for them, and re-layouts  14.6 us (7%)
  other arithmetic  10.8 us (5%)
    pallas_call x3, Pallas kernels, exchange(): pl.pallas_call(functools.partial(exchange_kernel, axis, n), out_shape=jax...  92.3 us
    pallas_call x1, Pallas kernels, dispatch(): pl.pallas_call(functools.partial(dispatch_kernel, expert_n, tm_n), out_sh...  73.8 us
    dot_general x1, matrix products, on_device(): jnp.dot(hidden, down_rows, preferred_element_type=jnp.float32)  6.01 us
    dot_general x4, matrix products, head_attention(): jnp.dot(block, key_rows.T, preferred_element_type=jnp.float32)  5.7 us
    unnamed x25, local copies, waits for them, and re-layouts  5.22 us
    slice x1, local copies, waits for them, and re-layouts, on_device(): up_rows = gathered_slices[:, 0].reshape(-1, model_width)  4.92 us

profile of v6, /device:TPU:8, one launch (start us, length us, event | category | flops | bytes accessed | tf_op | source)
XLA Modules:
  0.0 213.3 jit_solution(14115602988812505005)
XLA Ops:
  0.0 1.3 copy.16
  1.3 0.3 copy.19
  1.6 1.1 copy.17
  2.7 0.3 copy.20
  3.0 1.1 copy.18
  4.2 1.0 copy.21
  5.3 2.8 %fusion.53.x_ref = bf16[16,128,256]{2,1,0:T(8,128)(2,1)} fusion(bf16[128,16,1]{2,0,1:T(8,128)(2,1)S(1)} %broadcast_select_fusion, bf16[128,16,64]{2,0,1:T(8,128)(2,1)} %copy.21, bf16[128,16,64]{2,0,1:T(8,128)(2,1)S(1)} %copy.20, bf16[128,16,64]{2,0,1:T(8,128)(2,1)S(1)} %copy.19), kind=kLoop, calls=%fused_computation.47 | loop fusion | flops 5242880 | bytes 1839104 | tf_op jit(solution)/shard_map/transpose | solution.py:214
  8.1 20.1 %shard_map.127 = bf16[16,128,256]{2,1,0:T(8,128)(2,1)} custom-call(bf16[16,128,256]{2,1,0:T(8,128)(2,1)} %fusion.53.x_ref), custom_call_target="tpu_custom_call" | custom-call | tf_op jit(solution)/shard_map/pallas_call | solution.py:69
  28.2 2.4 %slice_convert_fusion = f32[2048,1]{1,0:T(8,128)} fusion(bf16[2048,256]{1,0:T(8,128)(2,1)} %bitcast.63), kind=kLoop, calls=%fused_computation.52 | loop fusion | flops 2048 | bytes 12288 | tf_op jit(solution)/shard_map/convert_element_type | solution.py:221
  30.5 1.6 copy.32
  32.1 2.0 add_reduce_fusion.3
  34.1 0.8 fusion.64
  34.9 0.8 fusion.66
  35.7 2.1 fusion
  37.8 1.0 fusion.31
  38.8 2.7 %fusion.2 = (f32[512]{0:T(512)S(1)}, f32[512]{0:T(512)S(1)}, f32[512]{0:T(512)S(1)}) fusion(f32[512,2048]{1,0:T(8,128)S(1)} %get-tuple-element.36, f32[512]{0:T(512)S(1)} %get-tuple-element.22, f32[2048]{0:T(1024)S(1)} %bitcast.85, f32[512]{0:T(512)S(1)} %get-tuple-element.23, f32[512,2048]{1,0:T(8,128)S(1)} %fusion.66, f32[512]{0:T(512)S(1)} %get-tuple-element.24, ...), kind=kLoop, calls=%fused_computation.10 | loop fusion | flops 9435648 | bytes 12603392 | tf_op jit(solution)/shard_map/reduce_sum | solution.py:21
  41.5 1.0 fusion.37
  42.4 1.0 fusion.43
  43.4 1.0 fusion.49
  44.4 1.0 copy.23
  45.4 12.5 %shard_map.128 = bf16[16,128,64]{2,1,0:T(8,128)(2,1)} custom-call(bf16[16,128,64]{2,1,0:T(8,128)(2,1)} %bitcast.73), custom_call_target="tpu_custom_call" | custom-call | tf_op jit(solution)/shard_map/pallas_call | solution.py:69
  57.9 1.7 fusion.87
  60.4 1.0 reshape.198
  61.6 0.6 reduce-window.6
  62.7 2.5 %convolution_convert_fusion.1 = bf16[512,1024]{1,0:T(8,128)(2,1)} fusion(bf16[256,1024]{1,0:T(8,128)(2,1)} %reshape.198, s32[256]{0:T(256)S(1)} %multiply_add_fusion), kind=kOutput, calls=%fused_computation.32 | convolution fusion | flops 269090816 | bytes 1573888 | tf_op jit(solution)/shard_map/dot_general | solution.py:249
  65.2 0.7 pad_maximum_fusion.1.own_ref
  65.9 73.8 %shard_map.129 = (bf16[32,16,1024]{2,1,0:T(8,128)(2,1)}, bf16[16,2,64,1024]{3,2,1,0:T(8,128)(2,1)}) custom-call(bf16[32,16,1024]{2,1,0:T(8,128)(2,1)} %bitcast.72, bf16[2,64,1024]{2,1,0:T(8,128)(2,1)} %pad_maximum_fusion.1.own_ref), custom_call_target="tpu_custom_call" | custom-call | tf_op jit(solution)/shard_map/pallas_call | solution.py:154
  139.8 4.9 %fusion.85 = (bf16[16,1,64,1024]{3,2,1,0:T(8,128)(2,1)}, bf16[16,1,64,1024]{3,2,1,0:T(8,128)(2,1)}) fusion(bf16[16,2,64,1024]{3,2,1,0:T(8,128)(2,1)} %get-tuple-element.20), kind=kLoop, calls=%fused_computation.98 | loop fusion | bytes 8388608 | tf_op jit(solution)/shard_map/slice | solution.py:253
  144.7 6.0 %convolution_convert_fusion = bf16[512,1024]{1,0:T(8,128)(2,1)} fusion(bf16[1024,1024]{1,0:T(8,128)(2,1)} %bitcast.75, bf16[512,1024]{1,0:T(8,128)(2,1)} %bitcast.93, bf16[1024,1024]{1,0:T(8,128)(2,1)} %bitcast.74), kind=kOutput, calls=%fused_computation.31 | convolution fusion | flops 2152726528 | bytes 6291456 | tf_op jit(solution)/shard_map/dot_general | solution.py:260
  150.7 59.8 %shard_map.130 = bf16[32,16,1024]{2,1,0:T(8,128)(2,1)} custom-call(bf16[32,16,1024]{2,1,0:T(8,128)(2,1)} %bitcast.80), custom_call_target="tpu_custom_call" | custom-call | tf_op jit(solution)/shard_map/pallas_call | solution.py:69
  210.8 1.7 fusion.25
  212.5 0.8 fusion.72
  (42 shorter events, 1.9 us)
Async XLA Ops:
  0.0 57.9 %copy-start = (bf16[1024,1024]{1,0:T(8,128)(2,1)S(1)}, bf16[1024,1024]{1,0:T(8,128)(2,1)}, u32[]{:S(2)}) copy-start(bf16[1024,1024]{1,0:T(8,128)(2,1)} %param.21) | copy-start | bytes 6291460
  0.0 5.2 %copy-start.9 = (s32[1,128]{1,0:T(1,128)S(1)}, s32[1,128]{1,0:T(1,128)}, u32[]{:S(2)}) copy-start(s32[1,128]{1,0:T(1,128)} %param.19) | copy-start | bytes 1540
  0.0 5.2 %copy-start.7 = (bf16[16]{0:T(256)(128)(2,1)S(1)}, bf16[16]{0:T(256)(128)(2,1)}, u32[]{:S(2)}) copy-start(bf16[16]{0:T(256)(128)(2,1)} %param.20) | copy-start | bytes 100
  28.1 5.9 %copy-start.1 = (bf16[16,128,256]{2,1,0:T(8,128)(2,1)S(1)}, bf16[16,128,256]{2,1,0:T(8,128)(2,1)}, u32[]{:S(2)}) copy-start(bf16[16,128,256]{2,1,0:T(8,128)(2,1)} %shard_map.127) | copy-start | bytes 3145732
  43.4 14.5 %copy-start.4 = (f32[1,2,1024]{2,1,0:T(2,128)S(1)}, f32[1,2,1024]{2,1,0:T(2,128)}, u32[]{:S(2)}) copy-start(f32[1,2,1024]{2,1,0:T(2,128)} %param.23) | copy-start | bytes 24580
  44.4 15.5 %copy-start.5 = (f32[1,2,1024]{2,1,0:T(2,128)S(1)}, f32[1,2,1024]{2,1,0:T(2,128)}, u32[]{:S(2)}) copy-start(f32[1,2,1024]{2,1,0:T(2,128)} %param.22) | copy-start | bytes 24580
  45.4 16.0 %copy-start.6 = (s32[1,128,2]{1,2,0:T(2,128)S(1)}, s32[1,128,2]{1,2,0:T(2,128)}, u32[]{:S(2)}) copy-start(s32[1,128,2]{1,2,0:T(2,128)} %param.24) | copy-start | bytes 3076
  57.9 7.3 %copy-start.2 = (bf16[1,64,1024]{2,1,0:T(8,128)(2,1)S(1)}, bf16[1,64,1024]{2,1,0:T(8,128)(2,1)}, u32[]{:S(2)}) copy-start(bf16[1,64,1024]{2,1,0:T(8,128)(2,1)} %param.27) | copy-start | bytes 393220
  57.9 7.3 %copy-start.3 = (bf16[1,1024,64]{1,2,0:T(8,128)(2,1)S(1)}, bf16[1,1024,64]{1,2,0:T(8,128)(2,1)}, u32[]{:S(2)}) copy-start(bf16[1,1024,64]{1,2,0:T(8,128)(2,1)} %param.26) | copy-start | bytes 393220
  144.7 66.1 %copy-start.8 = (f32[1,128,2]{1,2,0:T(2,128)S(1)}, f32[1,128,2]{1,2,0:T(2,128)}, u32[]{:S(2)}) copy-start(f32[1,128,2]{1,2,0:T(2,128)} %param.25) | copy-start | bytes 3076

commit v7 on v5

--- a/solution.py
+++ b/solution.py
@@ -82,49 +82,71 @@
 
 def dispatch_kernel(
     expert_n, tm_n, slots_ref, own_ref, arrived_ref, gathered_ref,
-    send_sems, recv_sems, weight_send_sems, weight_recv_sems, local_sems,
+    send_sems, recv_sems, weight_send_sems, weight_recv_sems, sibling_sems, local_sems,
 ):
     mesh_ids = pl.DeviceIdType.MESH
+    half = tm_n // 2
     me_e = lax.axis_index("expert")
     me_t = lax.axis_index("tm")
+    parity = me_t % 2
+    rank = me_t // 2
+    sibling = me_t + 1 - 2 * parity
     barrier = pltpu.get_barrier_semaphore()
     for k in range(1, expert_n):
         pl.semaphore_signal(barrier, inc=1, device_id={"expert": lax.rem(me_e + k, expert_n)}, device_id_type=mesh_ids)
-    for k in range(1, tm_n):
-        pl.semaphore_signal(barrier, inc=1, device_id={"tm": lax.rem(me_t + k, tm_n)}, device_id_type=mesh_ids)
-    pl.semaphore_wait(barrier, expert_n - 1 + tm_n - 1)
+    for k in range(1, half):
+        pl.semaphore_signal(barrier, inc=1, device_id={"tm": 2 * lax.rem(rank + k, half) + parity}, device_id_type=mesh_ids)
+    pl.semaphore_signal(barrier, inc=1, device_id={"tm": sibling}, device_id_type=mesh_ids)
+    pl.semaphore_wait(barrier, expert_n - 1 + half)
     local_slots = pltpu.make_async_copy(slots_ref.at[me_e], arrived_ref.at[me_e], local_sems.at[0])
-    local_weights = pltpu.make_async_copy(own_ref, gathered_ref.at[me_t], local_sems.at[1])
+    local_weights = pltpu.make_async_copy(own_ref, gathered_ref.at[parity, rank], local_sems.at[1])
+    local_weights.start()
     local_slots.start()
-    local_weights.start()
     copies = []
-    for k in range(1, max(expert_n, tm_n)):
-        if k < tm_n:
-            peer = lax.rem(me_t + k, tm_n)
-            copy = pltpu.make_async_remote_copy(
-                src_ref=own_ref,
-                dst_ref=gathered_ref.at[me_t],
-                send_sem=weight_send_sems.at[k],
-                recv_sem=weight_recv_sems.at[k],
-                device_id={"tm": peer},
-                device_id_type=mesh_ids,
-            )
-            copy.start()
-            copies.append(copy)
-        if k < expert_n:
-            peer = lax.rem(me_e + k, expert_n)
-            copy = pltpu.make_async_remote_copy(
-                src_ref=slots_ref.at[peer],
-                dst_ref=arrived_ref.at[me_e],
-                send_sem=send_sems.at[k],
-                recv_sem=recv_sems.at[k],
-                device_id={"expert": peer},
-                device_id_type=mesh_ids,
-            )
-            copy.start()
-            copies.append(copy)
+    for k in range(1, half):
+        copy = pltpu.make_async_remote_copy(
+            src_ref=own_ref,
+            dst_ref=gathered_ref.at[parity, rank],
+            send_sem=weight_send_sems.at[k],
+            recv_sem=weight_recv_sems.at[k],
+            device_id={"tm": 2 * lax.rem(rank + k, half) + parity},
+            device_id_type=mesh_ids,
+        )
+        copy.start()
+        copies.append(copy)
+    for k in range(1, expert_n):
+        peer = lax.rem(me_e + k, expert_n)
+        copy = pltpu.make_async_remote_copy(
+            src_ref=slots_ref.at[peer],
+            dst_ref=arrived_ref.at[me_e],
+            send_sem=send_sems.at[k],
+            recv_sem=recv_sems.at[k],
+            device_id={"expert": peer},
+            device_id_type=mesh_ids,
+        )
+        copy.start()
+        copies.append(copy)
+    local_weights.wait()
+    for k in range(1, half):
+        source = lax.rem(rank + half - k, half)
+        pltpu.make_async_remote_copy(
+            src_ref=own_ref,
+            dst_ref=gathered_ref.at[parity, source],
+            send_sem=weight_send_sems.at[k],
+            recv_sem=weight_recv_sems.at[k],
+            device_id={"tm": 2 * source + parity},
+            device_id_type=mesh_ids,
+        ).wait_recv()
+    forward = pltpu.make_async_remote_copy(
+        src_ref=gathered_ref.at[parity],
+        dst_ref=gathered_ref.at[parity],
+        send_sem=sibling_sems.at[0],
+        recv_sem=sibling_sems.at[1],
+        device_id={"tm": sibling},
+        device_id_type=mesh_ids,
+    )
+    forward.start()
     local_slots.wait()
-    local_weights.wait()
     for copy in copies:
         copy.wait_send()
     for k in range(1, expert_n):
@@ -137,16 +159,15 @@
             device_id={"expert": source},
             device_id_type=mesh_ids,
         ).wait_recv()
-    for k in range(1, tm_n):
-        source = lax.rem(me_t + tm_n - k, tm_n)
-        pltpu.make_async_remote_copy(
-            src_ref=own_ref,
-            dst_ref=gathered_ref.at[source],
-            send_sem=weight_send_sems.at[k],
-            recv_sem=weight_recv_sems.at[k],
-            device_id={"tm": source},
-            device_id_type=mesh_ids,
-        ).wait_recv()
+    forward.wait_send()
+    pltpu.make_async_remote_copy(
+        src_ref=gathered_ref.at[1 - parity],
+        dst_ref=gathered_ref.at[1 - parity],
+        send_sem=sibling_sems.at[0],
+        recv_sem=sibling_sems.at[1],
+        device_id={"tm": sibling},
+        device_id_type=mesh_ids,
+    ).wait_recv()
 
 
 def dispatch(slots, own_slices, tm_n, collective_id):
@@ -155,20 +176,20 @@
         functools.partial(dispatch_kernel, expert_n, tm_n),
         out_shape=(
             jax.ShapeDtypeStruct(slots.shape, slots.dtype),
-            jax.ShapeDtypeStruct((tm_n,) + own_slices.shape, own_slices.dtype),
+            jax.ShapeDtypeStruct((2, tm_n // 2) + own_slices.shape, own_slices.dtype),
         ),
         in_specs=[pl.BlockSpec(memory_space=pl.ANY)] * 2,
         out_specs=(pl.BlockSpec(memory_space=pl.ANY), pl.BlockSpec(memory_space=pl.ANY)),
         scratch_shapes=[
             pltpu.SemaphoreType.DMA((expert_n,)),
             pltpu.SemaphoreType.DMA((expert_n,)),
-            pltpu.SemaphoreType.DMA((tm_n,)),
-            pltpu.SemaphoreType.DMA((tm_n,)),
+            pltpu.SemaphoreType.DMA((tm_n // 2,)),
+            pltpu.SemaphoreType.DMA((tm_n // 2,)),
+            pltpu.SemaphoreType.DMA((2,)),
             pltpu.SemaphoreType.DMA((2,)),
         ],
         compiler_params=pltpu.CompilerParams(collective_id=collective_id, has_side_effects=True),
     )(slots, own_slices)
-
 
 def layer_norm(mixed, shift_row, scale_row):
     center = jnp.mean(mixed, axis=-1, keepdims=True)
@@ -250,8 +271,8 @@
     slots = slots.reshape(expert_count, capacity, model_width)
     own_slices = jnp.stack([jnp.transpose(up_weight[0]), down_weight[0]])
     arrived, gathered_slices = dispatch(slots, own_slices, lax.axis_size("tm"), 2)
-    up_rows = gathered_slices[:, 0].reshape(-1, model_width)
-    down_rows = gathered_slices[:, 1].reshape(-1, model_width)
+    up_rows = gathered_slices[:, :, 0].reshape(-1, model_width)
+    down_rows = gathered_slices[:, :, 1].reshape(-1, model_width)
     grouped = arrived.reshape(source_count * local_experts * capacity, model_width)
     hidden = jax.nn.gelu(
         jnp.einsum("rd,fd->rf", grouped, up_rows, preferred_element_type=jnp.float32),

time: 208 us -> 193 us (0.928)
  the two profiles are of different devices: /device:TPU:8 before, /device:TPU:40 now
where the time goes in v7:
time: 193 us
  Pallas kernels  123 us (64%)
  matrix products  20 us (10%)
  waiting for transfers between devices  16.4 us (8%)
  local copies, waits for them, and re-layouts  11.9 us (6%)
  starting transfers between devices  11.9 us (6%)
  other arithmetic  9.81 us (5%)
    pallas_call x1, Pallas kernels, dispatch(): pl.pallas_call(functools.partial(dispatch_kernel, expert_n, tm_n), out_sh...  64.4 us
    pallas_call x1, Pallas kernels, exchange(): pl.pallas_call(functools.partial(exchange_kernel, axis, n), out_shape=jax...  58.2 us
    all_to_all x1, waiting for transfers between devices, on_device(): lax.all_to_all(packed, 'tm', split_axis=0, concat_axis=0, tiled=True)  12.5 us
    all_to_all x1, starting transfers between devices, on_device(): lax.all_to_all(head_out, 'tm', split_axis=0, concat_axis=0, tiled=True)  6.08 us
    dot_general x1, matrix products, on_device(): jnp.dot(hidden, down_rows, preferred_element_type=jnp.float32)  6 us
    all_to_all x1, starting transfers between devices, on_device(): lax.all_to_all(packed, 'tm', split_axis=0, concat_axis=0, tiled=True)  5.86 us
    slice x1, local copies, waits for them, and re-layouts, on_device(): up_rows = gathered_slices[:, :, 0].reshape(-1, model_width)  4.92 us
    dot_general x4, matrix products, head_attention(): jnp.dot(block, key_rows.T, preferred_element_type=jnp.float32)  4.52 us
  transfers between devices with their start and end apart: 2, of which 2 were waited for; matrix products, arithmetic and copies ran while one was open for 2% of the time, Pallas kernels for 0%

profile of v7, /device:TPU:40, one launch (start us, length us, event | category | flops | bytes accessed | tf_op | source)
XLA Modules:
  0.0 192.9 jit_solution(8666959618178213925)
XLA Ops:
  0.0 1.3 copy.15
  1.3 1.1 copy.16
  2.4 1.1 copy.17
  3.6 0.7 compare_bitcast_fusion
  4.2 0.7 broadcast_select_fusion
  5.0 1.2 fusion.53
  6.1 5.9 %all-to-all-start = ((bf16[16,128,256]{1,2,0:T(8,128)(2,1)}), bf16[16,128,256]{1,2,0:T(8,128)(2,1)}, u32[]{:S(2)}, u32[]{:S(2)}) async-start(bf16[16,128,256]{1,2,0:T(8,128)(2,1)} %fusion.53), calls=%async_computation | async-start | bytes 2097152 | tf_op jit(solution)/shard_map/all_to_all | solution.py:236
  13.5 12.5 %all-to-all-done = bf16[16,128,256]{1,2,0:T(8,128)(2,1)} async-done(((bf16[16,128,256]{1,2,0:T(8,128)(2,1)}), bf16[16,128,256]{1,2,0:T(8,128)(2,1)}, u32[]{:S(2)}, u32[]{:S(2)}) %all-to-all-start) | async-done | bytes 1048608 | tf_op jit(solution)/shard_map/all_to_all | solution.py:236
  26.1 1.5 copy.18
  27.9 0.8 fusion.64
  28.7 0.8 fusion.66
  29.5 0.9 add_reduce_fusion.3
  30.4 2.1 %fusion = (f32[512]{0:T(512)S(1)}, f32[512]{0:T(512)S(1)}, f32[512]{0:T(512)S(1)}, f32[512]{0:T(512)S(1)}, f32[512,2048]{1,0:T(8,128)S(1)}) fusion(f32[512,2048]{1,0:T(8,128)S(1)} %get-tuple-element.35, f32[512]{0:T(512)S(1)} %get-tuple-element.34, f32[2048]{0:T(1024)S(1)} %convert_reduce_fusion, f32[512,2048]{1,0:T(8,128)S(1)} %fusion.66, ...), kind=kOutput, calls=%fused_computation.8 | convolution fusion | flops 143652864 | bytes 17451008 | tf_op jit(solution)/shard_map/dot_general | solution.py:18
  32.5 1.0 fusion.31
  33.4 2.5 %fusion.2 = (f32[512]{0:T(512)S(1)}, f32[512]{0:T(512)S(1)}, f32[512]{0:T(512)S(1)}) fusion(f32[512,2048]{1,0:T(8,128)S(1)} %get-tuple-element.36, f32[512]{0:T(512)S(1)} %get-tuple-element.22, f32[2048]{0:T(1024)S(1)} %convert_reduce_fusion, f32[512]{0:T(512)S(1)} %get-tuple-element.23, f32[512,2048]{1,0:T(8,128)S(1)} %fusion.66, ...), kind=kLoop, calls=%fused_computation.10 | loop fusion | flops 9435648 | bytes 12603392 | tf_op jit(solution)/shard_map/reduce_sum | solution.py:21
  35.9 1.0 fusion.37
  36.9 1.0 fusion.43
  37.9 1.0 fusion.49
  38.8 0.8 copy_bitcast_fusion
  39.6 6.1 %all-to-all-start.1 = ((bf16[16,128,64]{1,2,0:T(8,128)(2,1)}), bf16[16,128,64]{1,2,0:T(8,128)(2,1)S(1)}, u32[]{:S(2)}, u32[]{:S(2)}) async-start(bf16[16,128,64]{1,2,0:T(8,128)(2,1)} %copy_bitcast_fusion), calls=%async_computation.1 | async-start | bytes 524288 | tf_op jit(solution)/shard_map/all_to_all | solution.py:245
  45.7 0.7 pad_maximum_fusion.own_ref
  46.6 0.8 slice_add_fusion
  47.4 3.8 %all-to-all-done.1 = bf16[16,128,64]{1,2,0:T(8,128)(2,1)S(1)} async-done(((bf16[16,128,64]{1,2,0:T(8,128)(2,1)}), bf16[16,128,64]{1,2,0:T(8,128)(2,1)S(1)}, u32[]{:S(2)}, u32[]{:S(2)}) %all-to-all-start.1) | async-done | bytes 262176 | tf_op jit(solution)/shard_map/all_to_all | solution.py:245
  51.2 1.5 fusion.87
  53.4 1.0 reshape.198
  54.4 2.5 %convolution_convert_fusion.1 = bf16[512,1024]{1,0:T(8,128)(2,1)} fusion(bf16[256,1024]{1,0:T(8,128)(2,1)} %reshape.198, s32[256]{0:T(256)S(1)} %multiply_add_fusion), kind=kOutput, calls=%fused_computation.32 | convolution fusion | flops 269090816 | bytes 1573888 | tf_op jit(solution)/shard_map/dot_general | solution.py:270
  56.8 64.4 %shard_map.127 = (bf16[32,16,1024]{2,1,0:T(8,128)(2,1)}, bf16[2,8,2,64,1024]{4,3,2,1,0:T(8,128)(2,1)}) custom-call(bf16[32,16,1024]{2,1,0:T(8,128)(2,1)} %bitcast.75, bf16[2,64,1024]{2,1,0:T(8,128)(2,1)} %pad_maximum_fusion.own_ref), custom_call_target="tpu_custom_call" | custom-call | tf_op jit(solution)/shard_map/pallas_call | solution.py:175
  121.3 4.9 %fusion.85 = (bf16[2,8,1,64,1024]{4,3,2,1,0:T(8,128)(2,1)}, bf16[2,8,1,64,1024]{4,3,2,1,0:T(8,128)(2,1)}) fusion(bf16[2,8,2,64,1024]{4,3,2,1,0:T(8,128)(2,1)} %get-tuple-element.20), kind=kLoop, calls=%fused_computation.99 | loop fusion | bytes 8388608 | tf_op jit(solution)/shard_map/slice | solution.py:274
  126.2 6.0 %convolution_convert_fusion = bf16[512,1024]{1,0:T(8,128)(2,1)} fusion(bf16[1024,1024]{1,0:T(8,128)(2,1)} %bitcast.77, bf16[512,1024]{1,0:T(8,128)(2,1)} %bitcast.88, bf16[1024,1024]{1,0:T(8,128)(2,1)} %bitcast.76), kind=kOutput, calls=%fused_computation.31 | convolution fusion | flops 2152726528 | bytes 6291456 | tf_op jit(solution)/shard_map/dot_general | solution.py:281
  132.2 58.2 %shard_map.128 = bf16[32,16,1024]{2,1,0:T(8,128)(2,1)} custom-call(bf16[32,16,1024]{2,1,0:T(8,128)(2,1)} %bitcast.81), custom_call_target="tpu_custom_call" | custom-call | tf_op jit(solution)/shard_map/pallas_call | solution.py:69
  190.4 1.7 fusion.25
  192.1 0.8 fusion.72
  (32 shorter events, 2.7 us)
Async XLA Ops:
  0.0 51.2 %copy-start = (bf16[1024,1024]{1,0:T(8,128)(2,1)S(1)}, bf16[1024,1024]{1,0:T(8,128)(2,1)}, u32[]{:S(2)}) copy-start(bf16[1024,1024]{1,0:T(8,128)(2,1)} %param.21) | copy-start | bytes 6291460
  0.0 12.0 %copy-start.4 = (s32[1,128,2]{1,2,0:T(2,128)S(1)}, s32[1,128,2]{1,2,0:T(2,128)}, u32[]{:S(2)}) copy-start(s32[1,128,2]{1,2,0:T(2,128)} %param.24) | copy-start | bytes 3076
  0.0 13.4 %copy-start.3 = (f32[1,2,1024]{2,1,0:T(2,128)S(1)}, f32[1,2,1024]{2,1,0:T(2,128)}, u32[]{:S(2)}) copy-start(f32[1,2,1024]{2,1,0:T(2,128)} %param.23) | copy-start | bytes 24580
  6.1 19.9 %all-to-all-start = ((bf16[16,128,256]{1,2,0:T(8,128)(2,1)}), bf16[16,128,256]{1,2,0:T(8,128)(2,1)}, u32[]{:S(2)}, u32[]{:S(2)}) async-start(bf16[16,128,256]{1,2,0:T(8,128)(2,1)} %fusion.53), calls=%async_computation | async-start | bytes 2097152 | tf_op jit(solution)/shard_map/all_to_all | solution.py:236
  37.9 7.8 %copy-start.1 = (bf16[1,64,1024]{2,1,0:T(8,128)(2,1)S(1)}, bf16[1,64,1024]{2,1,0:T(8,128)(2,1)}, u32[]{:S(2)}) copy-start(bf16[1,64,1024]{2,1,0:T(8,128)(2,1)} %param.27) | copy-start | bytes 393220
  37.9 7.8 %copy-start.2 = (bf16[1,1024,64]{1,2,0:T(8,128)(2,1)S(1)}, bf16[1,1024,64]{1,2,0:T(8,128)(2,1)}, u32[]{:S(2)}) copy-start(bf16[1,1024,64]{1,2,0:T(8,128)(2,1)} %param.26) | copy-start | bytes 393220
  39.6 11.6 %all-to-all-start.1 = ((bf16[16,128,64]{1,2,0:T(8,128)(2,1)}), bf16[16,128,64]{1,2,0:T(8,128)(2,1)S(1)}, u32[]{:S(2)}, u32[]{:S(2)}) async-start(bf16[16,128,64]{1,2,0:T(8,128)(2,1)} %copy_bitcast_fusion), calls=%async_computation.1 | async-start | bytes 524288 | tf_op jit(solution)/shard_map/all_to_all | solution.py:245
  126.2 64.2 %copy-start.5 = (f32[1,128,2]{1,2,0:T(2,128)S(1)}, f32[1,128,2]{1,2,0:T(2,128)}, u32[]{:S(2)}) copy-start(f32[1,128,2]{1,2,0:T(2,128)} %param.25) | copy-start | bytes 3076

commit v8 on v7

--- a/solution.py
+++ b/solution.py
@@ -81,7 +81,7 @@
 
 
 def dispatch_kernel(
-    expert_n, tm_n, slots_ref, own_ref, arrived_ref, gathered_ref,
+    expert_n, tm_n, slots_ref, own_up_ref, own_down_ref, arrived_ref, up_ref, down_ref,
     send_sems, recv_sems, weight_send_sems, weight_recv_sems, sibling_sems, local_sems,
 ):
     mesh_ids = pl.DeviceIdType.MESH
@@ -91,6 +91,8 @@
     parity = me_t % 2
     rank = me_t // 2
     sibling = me_t + 1 - 2 * parity
+    owned = (own_up_ref, own_down_ref)
+    gathered = (up_ref, down_ref)
     barrier = pltpu.get_barrier_semaphore()
     for k in range(1, expert_n):
         pl.semaphore_signal(barrier, inc=1, device_id={"expert": lax.rem(me_e + k, expert_n)}, device_id_type=mesh_ids)
@@ -98,22 +100,26 @@
         pl.semaphore_signal(barrier, inc=1, device_id={"tm": 2 * lax.rem(rank + k, half) + parity}, device_id_type=mesh_ids)
     pl.semaphore_signal(barrier, inc=1, device_id={"tm": sibling}, device_id_type=mesh_ids)
     pl.semaphore_wait(barrier, expert_n - 1 + half)
-    local_slots = pltpu.make_async_copy(slots_ref.at[me_e], arrived_ref.at[me_e], local_sems.at[0])
-    local_weights = pltpu.make_async_copy(own_ref, gathered_ref.at[parity, rank], local_sems.at[1])
-    local_weights.start()
-    local_slots.start()
+    local_copies = [pltpu.make_async_copy(slots_ref.at[me_e], arrived_ref.at[me_e], local_sems.at[0])]
+    for w in range(2):
+        local_copies.append(
+            pltpu.make_async_copy(owned[w], gathered[w].at[parity, rank], local_sems.at[1 + w])
+        )
+    for copy in local_copies:
+        copy.start()
     copies = []
     for k in range(1, half):
-        copy = pltpu.make_async_remote_copy(
-            src_ref=own_ref,
-            dst_ref=gathered_ref.at[parity, rank],
-            send_sem=weight_send_sems.at[k],
-            recv_sem=weight_recv_sems.at[k],
-            device_id={"tm": 2 * lax.rem(rank + k, half) + parity},
-            device_id_type=mesh_ids,
-        )
-        copy.start()
-        copies.append(copy)
+        for w in range(2):
+            copy = pltpu.make_async_remote_copy(
+                src_ref=owned[w],
+                dst_ref=gathered[w].at[parity, rank],
+                send_sem=weight_send_sems.at[w, k],
+                recv_sem=weight_recv_sems.at[w, k],
+                device_id={"tm": 2 * lax.rem(rank + k, half) + parity},
+                device_id_type=mesh_ids,
+            )
+            copy.start()
+            copies.append(copy)
     for k in range(1, expert_n):
         peer = lax.rem(me_e + k, expert_n)
         copy = pltpu.make_async_remote_copy(
@@ -126,27 +132,30 @@
         )
         copy.start()
         copies.append(copy)
-    local_weights.wait()
-    for k in range(1, half):
-        source = lax.rem(rank + half - k, half)
-        pltpu.make_async_remote_copy(
-            src_ref=own_ref,
-            dst_ref=gathered_ref.at[parity, source],
-            send_sem=weight_send_sems.at[k],
-            recv_sem=weight_recv_sems.at[k],
-            device_id={"tm": 2 * source + parity},
+    for copy in local_copies:
+        copy.wait()
+    forwards = []
+    for w in range(2):
+        for k in range(1, half):
+            source = lax.rem(rank + half - k, half)
+            pltpu.make_async_remote_copy(
+                src_ref=owned[w],
+                dst_ref=gathered[w].at[parity, source],
+                send_sem=weight_send_sems.at[w, k],
+                recv_sem=weight_recv_sems.at[w, k],
+                device_id={"tm": 2 * source + parity},
+                device_id_type=mesh_ids,
+            ).wait_recv()
+        forward = pltpu.make_async_remote_copy(
+            src_ref=gathered[w].at[parity],
+            dst_ref=gathered[w].at[parity],
+            send_sem=sibling_sems.at[0, w],
+            recv_sem=sibling_sems.at[1, w],
+            device_id={"tm": sibling},
             device_id_type=mesh_ids,
-        ).wait_recv()
-    forward = pltpu.make_async_remote_copy(
-        src_ref=gathered_ref.at[parity],
-        dst_ref=gathered_ref.at[parity],
-        send_sem=sibling_sems.at[0],
-        recv_sem=sibling_sems.at[1],
-        device_id={"tm": sibling},
-        device_id_type=mesh_ids,
-    )
-    forward.start()
-    local_slots.wait()
+        )
+        forward.start()
+        forwards.append(forward)
     for copy in copies:
         copy.wait_send()
     for k in range(1, expert_n):
@@ -159,37 +168,36 @@
             device_id={"expert": source},
             device_id_type=mesh_ids,
         ).wait_recv()
-    forward.wait_send()
-    pltpu.make_async_remote_copy(
-        src_ref=gathered_ref.at[1 - parity],
-        dst_ref=gathered_ref.at[1 - parity],
-        send_sem=sibling_sems.at[0],
-        recv_sem=sibling_sems.at[1],
-        device_id={"tm": sibling},
-        device_id_type=mesh_ids,
-    ).wait_recv()
-
-
-def dispatch(slots, own_slices, tm_n, collective_id):
+    for w in range(2):
+        forwards[w].wait_send()
+        pltpu.make_async_remote_copy(
+            src_ref=gathered[w].at[1 - parity],
+            dst_ref=gathered[w].at[1 - parity],
+            send_sem=sibling_sems.at[0, w],
+            recv_sem=sibling_sems.at[1, w],
+            device_id={"tm": sibling},
+            device_id_type=mesh_ids,
+        ).wait_recv()
+
+
+def dispatch(slots, own_up, own_down, tm_n, collective_id):
     expert_n = slots.shape[0]
+    gathered_shape = jax.ShapeDtypeStruct((2, tm_n // 2) + own_up.shape, own_up.dtype)
     return pl.pallas_call(
         functools.partial(dispatch_kernel, expert_n, tm_n),
-        out_shape=(
-            jax.ShapeDtypeStruct(slots.shape, slots.dtype),
-            jax.ShapeDtypeStruct((2, tm_n // 2) + own_slices.shape, own_slices.dtype),
-        ),
-        in_specs=[pl.BlockSpec(memory_space=pl.ANY)] * 2,
-        out_specs=(pl.BlockSpec(memory_space=pl.ANY), pl.BlockSpec(memory_space=pl.ANY)),
+        out_shape=(jax.ShapeDtypeStruct(slots.shape, slots.dtype), gathered_shape, gathered_shape),
+        in_specs=[pl.BlockSpec(memory_space=pl.ANY)] * 3,
+        out_specs=tuple(pl.BlockSpec(memory_space=pl.ANY) for _ in range(3)),
         scratch_shapes=[
             pltpu.SemaphoreType.DMA((expert_n,)),
             pltpu.SemaphoreType.DMA((expert_n,)),
-            pltpu.SemaphoreType.DMA((tm_n // 2,)),
-            pltpu.SemaphoreType.DMA((tm_n // 2,)),
-            pltpu.SemaphoreType.DMA((2,)),
-            pltpu.SemaphoreType.DMA((2,)),
+            pltpu.SemaphoreType.DMA((2, tm_n // 2)),
+            pltpu.SemaphoreType.DMA((2, tm_n // 2)),
+            pltpu.SemaphoreType.DMA((2, 2)),
+            pltpu.SemaphoreType.DMA((3,)),
         ],
         compiler_params=pltpu.CompilerParams(collective_id=collective_id, has_side_effects=True),
-    )(slots, own_slices)
+    )(slots, own_up, own_down)
 
 def layer_norm(mixed, shift_row, scale_row):
     center = jnp.mean(mixed, axis=-1, keepdims=True)
@@ -269,10 +277,11 @@
     doubled = jnp.repeat(normed, 2, axis=0)
     slots = jnp.dot(placing, doubled, preferred_element_type=jnp.float32).astype(jnp.bfloat16)
     slots = slots.reshape(expert_count, capacity, model_width)
-    own_slices = jnp.stack([jnp.transpose(up_weight[0]), down_weight[0]])
-    arrived, gathered_slices = dispatch(slots, own_slices, lax.axis_size("tm"), 2)
-    up_rows = gathered_slices[:, :, 0].reshape(-1, model_width)
-    down_rows = gathered_slices[:, :, 1].reshape(-1, model_width)
+    arrived, gathered_up, gathered_down = dispatch(
+        slots, jnp.transpose(up_weight[0]), down_weight[0], lax.axis_size("tm"), 2
+    )
+    up_rows = gathered_up.reshape(-1, model_width)
+    down_rows = gathered_down.reshape(-1, model_width)
     grouped = arrived.reshape(source_count * local_experts * capacity, model_width)
     hidden = jax.nn.gelu(
         jnp.einsum("rd,fd->rf", grouped, up_rows, preferred_element_type=jnp.float32),

time: 193 us -> 189 us (0.979)
  local copies, waits for them, and re-layouts: 11.9 us -> 7.05 us
    slice x1 -> x0, local copies, waits for them, and re-layouts: 4.92 us -> none  [on_device(): up_rows = gathered_slices[:, :, 0].reshape(-1, model_width)]
  transfers between devices with their start and end apart: 2 -> 2, of which waited for: 2 -> 2; matrix products, arithmetic and copies ran while one was open for 2% -> 1% of each run, Pallas kernels for 0% -> 0%
where the time goes in v8:
time: 189 us; the launch traced here: 188 us
  Pallas kernels  123 us (65%)
  matrix products  20.1 us (11%)
  waiting for transfers between devices  17.9 us (9%)
  starting transfers between devices  12 us (6%)
  other arithmetic  8.36 us (4%)
  local copies, waits for them, and re-layouts  7.05 us (4%)
    pallas_call x1, Pallas kernels, dispatch(): pl.pallas_call(functools.partial(dispatch_kernel, expert_n, tm_n), out_sh...  64.6 us
    pallas_call x1, Pallas kernels, exchange(): pl.pallas_call(functools.partial(exchange_kernel, axis, n), out_shape=jax...  58.2 us
    all_to_all x1, waiting for transfers between devices, on_device(): lax.all_to_all(packed, 'tm', split_axis=0, concat_axis=0, tiled=True)  12.6 us
    all_to_all x1, starting transfers between devices, on_device(): lax.all_to_all(head_out, 'tm', split_axis=0, concat_axis=0, tiled=True)  6.09 us
    dot_general x1, matrix products, on_device(): jnp.dot(hidden, down_rows, preferred_element_type=jnp.float32)  5.98 us
    all_to_all x1, starting transfers between devices, on_device(): lax.all_to_all(packed, 'tm', split_axis=0, concat_axis=0, tiled=True)  5.86 us
    all_to_all x1, waiting for transfers between devices, on_device(): lax.all_to_all(head_out, 'tm', split_axis=0, concat_axis=0, tiled=True)  5.31 us
    dot_general x4, matrix products, head_attention(): jnp.dot(block, key_rows.T, preferred_element_type=jnp.float32)  4.57 us
  transfers between devices with their start and end apart: 2, of which 2 were waited for; matrix products, arithmetic and copies ran while one was open for 1% of the time, Pallas kernels for 0%

profile of v8, /device:TPU:40, one launch (start us, length us, event | category | flops | bytes accessed | tf_op | source)
XLA Modules:
  0.0 188.3 jit_solution(437115171279291841)
XLA Ops:
  0.0 1.3 copy.15
  1.3 1.1 copy.16
  2.5 1.1 copy.17
  3.6 0.7 compare_bitcast_fusion
  4.3 0.7 broadcast_select_fusion
  5.0 1.2 fusion.53
  6.2 5.9 %all-to-all-start = ((bf16[16,128,256]{1,2,0:T(8,128)(2,1)}), bf16[16,128,256]{1,2,0:T(8,128)(2,1)}, u32[]{:S(2)}, u32[]{:S(2)}) async-start(bf16[16,128,256]{1,2,0:T(8,128)(2,1)} %fusion.53), calls=%async_computation | async-start | bytes 2097152 | tf_op jit(solution)/shard_map/all_to_all | solution.py:244
  12.5 0.6 reduce-window.6
  13.5 12.6 %all-to-all-done = bf16[16,128,256]{1,2,0:T(8,128)(2,1)} async-done(((bf16[16,128,256]{1,2,0:T(8,128)(2,1)}), bf16[16,128,256]{1,2,0:T(8,128)(2,1)}, u32[]{:S(2)}, u32[]{:S(2)}) %all-to-all-start) | async-done | bytes 1048608 | tf_op jit(solution)/shard_map/all_to_all | solution.py:244
  26.1 1.5 copy.18
  27.6 0.4 convert_reduce_fusion
  28.0 0.8 fusion.64
  28.8 0.8 fusion.66
  29.6 0.9 add_reduce_fusion.3
  30.4 2.1 %fusion = (f32[512]{0:T(512)S(1)}, f32[512]{0:T(512)S(1)}, f32[512]{0:T(512)S(1)}, f32[512]{0:T(512)S(1)}, f32[512,2048]{1,0:T(8,128)S(1)}) fusion(f32[512,2048]{1,0:T(8,128)S(1)} %get-tuple-element.35, f32[512]{0:T(512)S(1)} %get-tuple-element.34, f32[2048]{0:T(1024)S(1)} %convert_reduce_fusion, f32[512,2048]{1,0:T(8,128)S(1)} %fusion.66, ...), kind=kOutput, calls=%fused_computation.8 | convolution fusion | flops 143652864 | bytes 17451008 | tf_op jit(solution)/shard_map/dot_general | solution.py:18
  32.6 1.0 fusion.31
  33.5 2.5 %fusion.2 = (f32[512]{0:T(512)S(1)}, f32[512]{0:T(512)S(1)}, f32[512]{0:T(512)S(1)}) fusion(f32[512,2048]{1,0:T(8,128)S(1)} %get-tuple-element.36, f32[512]{0:T(512)S(1)} %get-tuple-element.24, f32[2048]{0:T(1024)S(1)} %convert_reduce_fusion, f32[512]{0:T(512)S(1)} %get-tuple-element.25, f32[512,2048]{1,0:T(8,128)S(1)} %fusion.66, ...), kind=kLoop, calls=%fused_computation.10 | loop fusion | flops 9435648 | bytes 12603392 | tf_op jit(solution)/shard_map/reduce_sum | solution.py:21
  36.1 1.0 fusion.37
  37.1 1.0 fusion.43
  38.1 1.0 fusion.49
  39.0 0.8 copy_bitcast_fusion
  39.8 6.1 %all-to-all-start.1 = ((bf16[16,128,64]{1,2,0:T(8,128)(2,1)}), bf16[16,128,64]{1,2,0:T(8,128)(2,1)S(1)}, u32[]{:S(2)}, u32[]{:S(2)}) async-start(bf16[16,128,64]{1,2,0:T(8,128)(2,1)} %copy_bitcast_fusion), calls=%async_computation.1 | async-start | bytes 524288 | tf_op jit(solution)/shard_map/all_to_all | solution.py:253
  46.1 5.3 %all-to-all-done.1 = bf16[16,128,64]{1,2,0:T(8,128)(2,1)S(1)} async-done(((bf16[16,128,64]{1,2,0:T(8,128)(2,1)}), bf16[16,128,64]{1,2,0:T(8,128)(2,1)S(1)}, u32[]{:S(2)}, u32[]{:S(2)}) %all-to-all-start.1) | async-done | bytes 262176 | tf_op jit(solution)/shard_map/all_to_all | solution.py:253
  51.4 1.5 fusion.86
  53.3 0.3 broadcast_in_dim.27
  53.6 1.0 reshape.204
  54.6 2.5 %convolution_convert_fusion.1 = bf16[512,1024]{1,0:T(8,128)(2,1)} fusion(bf16[256,1024]{1,0:T(8,128)(2,1)} %reshape.204, s32[256]{0:T(256)S(1)} %multiply_add_fusion), kind=kOutput, calls=%fused_computation.32 | convolution fusion | flops 269090816 | bytes 1573888 | tf_op jit(solution)/shard_map/dot_general | solution.py:278
  57.1 64.6 %shard_map.127 = (bf16[32,16,1024]{2,1,0:T(8,128)(2,1)}, bf16[2,8,64,1024]{3,2,1,0:T(8,128)(2,1)}, bf16[2,8,64,1024]{3,2,1,0:T(8,128)(2,1)}) custom-call(bf16[32,16,1024]{2,1,0:T(8,128)(2,1)} %bitcast.74, bf16[64,1024]{1,0:T(8,128)(2,1)} %bitcast.80, bf16[64,1024]{1,0:T(8,128)(2,1)} %bitcast.81), custom_call_target="tpu_custom_call" | custom-call | tf_op jit(solution)/shard_map/pallas_call | solution.py:186
  121.7 6.0 %convolution_convert_fusion = bf16[512,1024]{1,0:T(8,128)(2,1)} fusion(bf16[1024,1024]{1,0:T(8,128)(2,1)} %bitcast.87, bf16[512,1024]{1,0:T(8,128)(2,1)} %bitcast.88, bf16[1024,1024]{1,0:T(8,128)(2,1)} %bitcast.86), kind=kOutput, calls=%fused_computation.31 | convolution fusion | flops 2152726528 | bytes 6291456 | tf_op jit(solution)/shard_map/dot_general | solution.py:290
  127.7 58.2 %shard_map.128 = bf16[32,16,1024]{2,1,0:T(8,128)(2,1)} custom-call(bf16[32,16,1024]{2,1,0:T(8,128)(2,1)} %bitcast.78), custom_call_target="tpu_custom_call" | custom-call | tf_op jit(solution)/shard_map/pallas_call | solution.py:69
  185.8 1.7 fusion.25
  187.6 0.8 fusion.72
  (28 shorter events, 1.5 us)
Async XLA Ops:
  0.0 51.4 %copy-start = (bf16[1024,1024]{1,0:T(8,128)(2,1)S(1)}, bf16[1024,1024]{1,0:T(8,128)(2,1)}, u32[]{:S(2)}) copy-start(bf16[1024,1024]{1,0:T(8,128)(2,1)} %param.21) | copy-start | bytes 6291460
  0.0 12.0 %copy-start.3 = (s32[1,128,2]{1,2,0:T(2,128)S(1)}, s32[1,128,2]{1,2,0:T(2,128)}, u32[]{:S(2)}) copy-start(s32[1,128,2]{1,2,0:T(2,128)} %param.24) | copy-start | bytes 3076
  6.2 19.9 %all-to-all-start = ((bf16[16,128,256]{1,2,0:T(8,128)(2,1)}), bf16[16,128,256]{1,2,0:T(8,128)(2,1)}, u32[]{:S(2)}, u32[]{:S(2)}) async-start(bf16[16,128,256]{1,2,0:T(8,128)(2,1)} %fusion.53), calls=%async_computation | async-start | bytes 2097152 | tf_op jit(solution)/shard_map/all_to_all | solution.py:244
  38.0 7.9 %copy-start.1 = (f32[1,2,1024]{2,1,0:T(2,128)S(1)}, f32[1,2,1024]{2,1,0:T(2,128)}, u32[]{:S(2)}) copy-start(f32[1,2,1024]{2,1,0:T(2,128)} %param.23) | copy-start | bytes 24580
  38.0 8.0 %copy-start.2 = (f32[1,2,1024]{2,1,0:T(2,128)S(1)}, f32[1,2,1024]{2,1,0:T(2,128)}, u32[]{:S(2)}) copy-start(f32[1,2,1024]{2,1,0:T(2,128)} %param.22) | copy-start | bytes 24580
  39.8 11.6 %all-to-all-start.1 = ((bf16[16,128,64]{1,2,0:T(8,128)(2,1)}), bf16[16,128,64]{1,2,0:T(8,128)(2,1)S(1)}, u32[]{:S(2)}, u32[]{:S(2)}) async-start(bf16[16,128,64]{1,2,0:T(8,128)(2,1)} %copy_bitcast_fusion), calls=%async_computation.1 | async-start | bytes 524288 | tf_op jit(solution)/shard_map/all_to_all | solution.py:253
  121.7 64.2 %copy-start.4 = (f32[1,128,2]{1,2,0:T(2,128)S(1)}, f32[1,128,2]{1,2,0:T(2,128)}, u32[]{:S(2)}) copy-start(f32[1,128,2]{1,2,0:T(2,128)} %param.25) | copy-start | bytes 3076

commit v9 on v8

--- a/solution.py
+++ b/solution.py
@@ -230,7 +230,7 @@
     offsets = jnp.where(
         inpaint_mask[0][:, None] == 1, key_bias[None, :], jnp.zeros((), jnp.bfloat16)
     )
-    offset_cols = jnp.zeros((tok_rows, head_count, head_width), jnp.bfloat16).at[:, :, 0].set(offsets)
+    offset_cols = jnp.zeros((tok_rows, head_count, 16), jnp.bfloat16).at[:, :, 0].set(offsets)
     packed = jnp.concatenate(
         [
             scaled_queries.reshape(tok_rows, head_count, head_width),
@@ -242,7 +242,7 @@
     )
     packed = jnp.transpose(packed, (1, 0, 2))
     gathered = lax.all_to_all(packed, "tm", split_axis=0, concat_axis=0, tiled=True)
-    clip_rows = gathered.reshape(-1, 4 * head_width)
+    clip_rows = gathered.reshape(-1, 3 * head_width + 16)
     head_out = head_attention(
         clip_rows[:, :head_width],
         clip_rows[:, head_width:2 * head_width],
@@ -274,8 +274,8 @@
     placing = (
         jnp.arange(capacity * expert_count, dtype=jnp.int32)[:, None] == target[None, :]
     ).astype(jnp.bfloat16)
-    doubled = jnp.repeat(normed, 2, axis=0)
-    slots = jnp.dot(placing, doubled, preferred_element_type=jnp.float32).astype(jnp.bfloat16)
+    token_placing = placing.reshape(capacity * expert_count, tok_rows, 2).sum(axis=2)
+    slots = jnp.dot(token_placing, normed, preferred_element_type=jnp.float32).astype(jnp.bfloat16)
     slots = slots.reshape(expert_count, capacity, model_width)
     arrived, gathered_up, gathered_down = dispatch(
         slots, jnp.transpose(up_weight[0]), down_weight[0], lax.axis_size("tm"), 2

time: 189 us -> 181 us (0.958)
  waiting for transfers between devices: 17.9 us -> 15.3 us
  local copies, waits for them, and re-layouts: 7.05 us -> 4.59 us
  matrix products: 20.1 us -> 17.8 us
    all_to_all x1, waiting for transfers between devices: 12.6 us -> 10.1 us  [on_device(): lax.all_to_all(packed, 'tm', split_axis=0, concat_axis=0, tiled=True)]
where the time goes in v9:
time: 181 us; the launch traced here: 180 us
  Pallas kernels  123 us (68%)
  matrix products  17.8 us (10%)
  waiting for transfers between devices  15.3 us (8%)
  starting transfers between devices  11.9 us (7%)
  other arithmetic  7.68 us (4%)
  local copies, waits for them, and re-layouts  4.59 us (3%)
    pallas_call x1, Pallas kernels, dispatch(): pl.pallas_call(functools.partial(dispatch_kernel, expert_n, tm_n), out_sh...  64.6 us
    pallas_call x1, Pallas kernels, exchange(): pl.pallas_call(functools.partial(exchange_kernel, axis, n), out_shape=jax...  58.1 us
    all_to_all x1, waiting for transfers between devices, on_device(): lax.all_to_all(packed, 'tm', split_axis=0, concat_axis=0, tiled=True)  10.1 us
    all_to_all x1, starting transfers between devices, on_device(): lax.all_to_all(head_out, 'tm', split_axis=0, concat_axis=0, tiled=True)  6.07 us
    dot_general x1, matrix products, on_device(): jnp.dot(hidden, down_rows, preferred_element_type=jnp.float32)  6.03 us
    all_to_all x1, starting transfers between devices, on_device(): lax.all_to_all(packed, 'tm', split_axis=0, concat_axis=0, tiled=True)  5.86 us
    all_to_all x1, waiting for transfers between devices, on_device(): lax.all_to_all(head_out, 'tm', split_axis=0, concat_axis=0, tiled=True)  5.26 us
    dot_general x4, matrix products, head_attention(): jnp.dot(block, key_rows.T, preferred_element_type=jnp.float32)  4.33 us
  transfers between devices with their start and end apart: 2, of which 2 were waited for; matrix products, arithmetic and copies ran while one was open for 1% of the time, Pallas kernels for 0%

profile of v9, /device:TPU:40, one launch (start us, length us, event | category | flops | bytes accessed | tf_op | source)
XLA Modules:
  0.0 180.3 jit_solution(9802103643040526644)
XLA Ops:
  0.0 1.3 copy.26
  1.3 1.1 copy.27
  2.4 1.1 copy.28
  3.6 0.7 compare_bitcast_fusion
  4.2 0.7 broadcast_select_fusion
  5.0 1.0 fusion.58
  6.0 5.9 %all-to-all-start = ((bf16[16,128,208]{1,2,0:T(8,128)(2,1)}), bf16[16,128,208]{1,2,0:T(8,128)(2,1)S(1)}, u32[]{:S(2)}, u32[]{:S(2)}) async-start(bf16[16,128,208]{1,2,0:T(8,128)(2,1)} %fusion.58), calls=%async_computation | async-start | bytes 1703936 | tf_op jit(solution)/shard_map/all_to_all | solution.py:244
  12.2 0.6 reduce-window.6
  12.8 0.2 slice_reduce_fusion
  13.2 0.1 reduce_sum.91
  13.6 10.1 %all-to-all-done = bf16[16,128,208]{1,2,0:T(8,128)(2,1)S(1)} async-done(((bf16[16,128,208]{1,2,0:T(8,128)(2,1)}), bf16[16,128,208]{1,2,0:T(8,128)(2,1)S(1)}, u32[]{:S(2)}, u32[]{:S(2)}) %all-to-all-start) | async-done | bytes 852000 | tf_op jit(solution)/shard_map/all_to_all | solution.py:244
  23.8 0.7 fusion.71
  24.5 0.7 fusion.73
  25.2 0.8 add_reduce_fusion.3
  26.0 2.1 %fusion = (f32[512]{0:T(512)S(1)}, f32[512]{0:T(512)S(1)}, f32[512]{0:T(512)S(1)}, f32[512]{0:T(512)S(1)}, f32[512,2048]{1,0:T(8,128)S(1)}) fusion(f32[512,2048]{1,0:T(8,128)S(1)} %get-tuple-element.35, f32[512]{0:T(512)S(1)} %get-tuple-element.34, f32[2048]{0:T(1024)S(1)} %bitcast.81, f32[512,2048]{1,0:T(8,128)S(1)} %fusion.73, ...), kind=kOutput, calls=%fused_computation.8 | convolution fusion | flops 143652864 | bytes 17123328 | tf_op jit(solution)/shard_map/dot_general | solution.py:18
  28.1 0.9 fusion.31
  29.0 2.5 %fusion.2 = (f32[512]{0:T(512)S(1)}, f32[512]{0:T(512)S(1)}, f32[512]{0:T(512)S(1)}) fusion(f32[512,2048]{1,0:T(8,128)S(1)} %get-tuple-element.36, f32[512]{0:T(512)S(1)} %get-tuple-element.24, f32[2048]{0:T(1024)S(1)} %bitcast.83, f32[512]{0:T(512)S(1)} %get-tuple-element.25, f32[512,2048]{1,0:T(8,128)S(1)} %fusion.73, f32[512]{0:T(512)S(1)} %get-tuple-element.26, ...), kind=kLoop, calls=%fused_computation.10 | loop fusion | flops 9435648 | bytes 12603392 | tf_op jit(solution)/shard_map/reduce_sum | solution.py:21
  31.5 0.9 fusion.37
  32.5 0.9 fusion.43
  33.4 0.9 fusion.49
  34.3 0.8 copy_bitcast_fusion.1
  35.1 6.1 %all-to-all-start.1 = ((bf16[16,128,64]{1,2,0:T(8,128)(2,1)}), bf16[16,128,64]{1,2,0:T(8,128)(2,1)S(1)}, u32[]{:S(2)}, u32[]{:S(2)}) async-start(bf16[16,128,64]{1,2,0:T(8,128)(2,1)} %copy_bitcast_fusion.1), calls=%async_computation.1 | async-start | bytes 524288 | tf_op jit(solution)/shard_map/all_to_all | solution.py:253
  41.2 0.2 eq.79
  41.4 5.3 %all-to-all-done.1 = bf16[16,128,64]{1,2,0:T(8,128)(2,1)S(1)} async-done(((bf16[16,128,64]{1,2,0:T(8,128)(2,1)}), bf16[16,128,64]{1,2,0:T(8,128)(2,1)S(1)}, u32[]{:S(2)}, u32[]{:S(2)}) %all-to-all-start.1) | async-done | bytes 262176 | tf_op jit(solution)/shard_map/all_to_all | solution.py:253
  46.7 0.5 fusion.91
  47.3 0.2 multiply_reduce_fusion
  47.5 1.6 convolution_convert_fusion
  49.0 64.6 %shard_map.127 = (bf16[32,16,1024]{2,1,0:T(8,128)(2,1)}, bf16[2,8,64,1024]{3,2,1,0:T(8,128)(2,1)}, bf16[2,8,64,1024]{3,2,1,0:T(8,128)(2,1)}) custom-call(bf16[32,16,1024]{2,1,0:T(8,128)(2,1)} %bitcast.72, bf16[64,1024]{1,0:T(8,128)(2,1)} %bitcast.78, bf16[64,1024]{1,0:T(8,128)(2,1)} %bitcast.79), custom_call_target="tpu_custom_call" | custom-call | tf_op jit(solution)/shard_map/pallas_call | solution.py:186
  113.6 6.0 %convolution_convert_fusion.1 = bf16[512,1024]{1,0:T(8,128)(2,1)} fusion(bf16[1024,1024]{1,0:T(8,128)(2,1)} %bitcast.92, bf16[512,1024]{1,0:T(8,128)(2,1)} %bitcast.93, bf16[1024,1024]{1,0:T(8,128)(2,1)} %bitcast.91), kind=kOutput, calls=%fused_computation.32 | convolution fusion | flops 2152726528 | bytes 6291456 | tf_op jit(solution)/shard_map/dot_general | solution.py:290
  119.6 58.1 %shard_map.128 = bf16[32,16,1024]{2,1,0:T(8,128)(2,1)} custom-call(bf16[32,16,1024]{2,1,0:T(8,128)(2,1)} %bitcast.76), custom_call_target="tpu_custom_call" | custom-call | tf_op jit(solution)/shard_map/pallas_call | solution.py:69
  177.8 1.7 fusion.25
  179.5 0.8 fusion.62
  (31 shorter events, 1.0 us)
Async XLA Ops:
  0.0 46.7 %copy-start = (bf16[1024,1024]{1,0:T(8,128)(2,1)S(1)}, bf16[1024,1024]{1,0:T(8,128)(2,1)}, u32[]{:S(2)}) copy-start(bf16[1024,1024]{1,0:T(8,128)(2,1)} %param.21) | copy-start | bytes 6291460
  0.0 11.8 %copy-start.4 = (s32[1,128,2]{1,2,0:T(2,128)S(1)}, s32[1,128,2]{1,2,0:T(2,128)}, u32[]{:S(2)}) copy-start(s32[1,128,2]{1,2,0:T(2,128)} %param.24) | copy-start | bytes 3076
  0.0 13.4 %copy-start.2 = (f32[1,2,1024]{2,1,0:T(2,128)S(1)}, f32[1,2,1024]{2,1,0:T(2,128)}, u32[]{:S(2)}) copy-start(f32[1,2,1024]{2,1,0:T(2,128)} %param.23) | copy-start | bytes 24580
  6.0 17.7 %all-to-all-start = ((bf16[16,128,208]{1,2,0:T(8,128)(2,1)}), bf16[16,128,208]{1,2,0:T(8,128)(2,1)S(1)}, u32[]{:S(2)}, u32[]{:S(2)}) async-start(bf16[16,128,208]{1,2,0:T(8,128)(2,1)} %fusion.58), calls=%async_computation | async-start | bytes 1703936 | tf_op jit(solution)/shard_map/all_to_all | solution.py:244
  33.4 8.0 %copy-start.3 = (f32[1,2,1024]{2,1,0:T(2,128)S(1)}, f32[1,2,1024]{2,1,0:T(2,128)}, u32[]{:S(2)}) copy-start(f32[1,2,1024]{2,1,0:T(2,128)} %param.22) | copy-start | bytes 24580
  33.4 13.3 %copy-start.1 = (bf16[1,128,1024]{2,1,0:T(8,128)(2,1)S(1)}, bf16[1,128,1024]{2,1,0:T(8,128)(2,1)}, u32[]{:S(2)}) copy-start(bf16[1,128,1024]{2,1,0:T(8,128)(2,1)} %param.15) | copy-start | bytes 786436
  35.1 11.6 %all-to-all-start.1 = ((bf16[16,128,64]{1,2,0:T(8,128)(2,1)}), bf16[16,128,64]{1,2,0:T(8,128)(2,1)S(1)}, u32[]{:S(2)}, u32[]{:S(2)}) async-start(bf16[16,128,64]{1,2,0:T(8,128)(2,1)} %copy_bitcast_fusion.1), calls=%async_computation.1 | async-start | bytes 524288 | tf_op jit(solution)/shard_map/all_to_all | solution.py:253
  113.6 64.2 %copy-start.5 = (f32[1,128,2]{1,2,0:T(2,128)S(1)}, f32[1,128,2]{1,2,0:T(2,128)}, u32[]{:S(2)}) copy-start(f32[1,128,2]{1,2,0:T(2,128)} %param.25) | copy-start | bytes 3076

commit v10 on v9

--- a/solution.py
+++ b/solution.py
@@ -26,6 +26,13 @@
     return jnp.concatenate(outputs, axis=0)
 
 
+def both_ways(n):
+    order = []
+    for k in range(1, n // 2 + 1):
+        order += [k] if 2 * k == n else [k, n - k]
+    return order
+
+
 def exchange_kernel(axis, n, x_ref, y_ref, send_sems, recv_sems, local_sem):
     me = lax.axis_index(axis)
     barrier = pltpu.get_barrier_semaphore()
@@ -37,7 +44,7 @@
     local = pltpu.make_async_copy(x_ref.at[me], y_ref.at[me], local_sem)
     local.start()
     copies = []
-    for k in range(1, n):
+    for k in both_ways(n):
         peer = lax.rem(me + k, n)
         copy = pltpu.make_async_remote_copy(
             src_ref=x_ref.at[peer],
@@ -120,7 +127,7 @@
             )
             copy.start()
             copies.append(copy)
-    for k in range(1, expert_n):
+    for k in both_ways(expert_n):
         peer = lax.rem(me_e + k, expert_n)
         copy = pltpu.make_async_remote_copy(
             src_ref=slots_ref.at[peer],

time: 181 us -> 180 us (level)
  the two profiles are of different devices: /device:TPU:40 before, /device:TPU:8 now
where the time goes in v10:
time: 180 us; the launch traced here: 179 us
  Pallas kernels  118 us (66%)
  matrix products  17.9 us (10%)
  starting transfers between devices  15.4 us (9%)
  waiting for transfers between devices  15.3 us (8%)
  other arithmetic  7.68 us (4%)
  local copies, waits for them, and re-layouts  4.59 us (3%)
    pallas_call x1, Pallas kernels, dispatch(): pl.pallas_call(functools.partial(dispatch_kernel, expert_n, tm_n), out_sh...  62.1 us
    pallas_call x1, Pallas kernels, exchange(): pl.pallas_call(functools.partial(exchange_kernel, axis, n), out_shape=jax...  56.1 us
    all_to_all x1, waiting for transfers between devices, on_device(): lax.all_to_all(packed, 'tm', split_axis=0, concat_axis=0, tiled=True)  10.1 us
    all_to_all x1, starting transfers between devices, on_device(): lax.all_to_all(packed, 'tm', split_axis=0, concat_axis=0, tiled=True)  9.25 us
    all_to_all x1, starting transfers between devices, on_device(): lax.all_to_all(head_out, 'tm', split_axis=0, concat_axis=0, tiled=True)  6.14 us
    dot_general x1, matrix products, on_device(): jnp.dot(hidden, down_rows, preferred_element_type=jnp.float32)  6.03 us
    all_to_all x1, waiting for transfers between devices, on_device(): lax.all_to_all(head_out, 'tm', split_axis=0, concat_axis=0, tiled=True)  5.26 us
    dot_general x4, matrix products, head_attention(): jnp.dot(block, key_rows.T, preferred_element_type=jnp.float32)  4.35 us
  transfers between devices with their start and end apart: 2, of which 2 were waited for; matrix products, arithmetic and copies ran while one was open for 1% of the time, Pallas kernels for 0%

profile of v10, /device:TPU:8, one launch (start us, length us, event | category | flops | bytes accessed | tf_op | source)
XLA Modules:
  0.0 179.2 jit_solution(15261565588007331116)
XLA Ops:
  0.0 1.3 copy.26
  1.3 1.1 copy.27
  2.4 1.1 copy.28
  3.6 0.7 compare_bitcast_fusion
  4.2 0.7 broadcast_select_fusion
  5.0 1.0 fusion.58
  6.0 9.3 %all-to-all-start = ((bf16[16,128,208]{1,2,0:T(8,128)(2,1)}), bf16[16,128,208]{1,2,0:T(8,128)(2,1)S(1)}, u32[]{:S(2)}, u32[]{:S(2)}) async-start(bf16[16,128,208]{1,2,0:T(8,128)(2,1)} %fusion.58), calls=%async_computation | async-start | bytes 1703936 | tf_op jit(solution)/shard_map/all_to_all | solution.py:251
  15.6 0.6 reduce-window.6
  16.2 0.2 slice_reduce_fusion
  16.5 0.1 reduce_sum.91
  17.0 10.1 %all-to-all-done = bf16[16,128,208]{1,2,0:T(8,128)(2,1)S(1)} async-done(((bf16[16,128,208]{1,2,0:T(8,128)(2,1)}), bf16[16,128,208]{1,2,0:T(8,128)(2,1)S(1)}, u32[]{:S(2)}, u32[]{:S(2)}) %all-to-all-start) | async-done | bytes 852000 | tf_op jit(solution)/shard_map/all_to_all | solution.py:251
  27.1 0.7 fusion.71
  27.9 0.7 fusion.73
  28.6 0.8 add_reduce_fusion.3
  29.4 2.1 %fusion = (f32[512]{0:T(512)S(1)}, f32[512]{0:T(512)S(1)}, f32[512]{0:T(512)S(1)}, f32[512]{0:T(512)S(1)}, f32[512,2048]{1,0:T(8,128)S(1)}) fusion(f32[512,2048]{1,0:T(8,128)S(1)} %get-tuple-element.35, f32[512]{0:T(512)S(1)} %get-tuple-element.34, f32[2048]{0:T(1024)S(1)} %bitcast.81, f32[512,2048]{1,0:T(8,128)S(1)} %fusion.73, ...), kind=kOutput, calls=%fused_computation.8 | convolution fusion | flops 143652864 | bytes 17123328 | tf_op jit(solution)/shard_map/dot_general | solution.py:18
  31.5 0.9 fusion.31
  32.4 2.5 %fusion.2 = (f32[512]{0:T(512)S(1)}, f32[512]{0:T(512)S(1)}, f32[512]{0:T(512)S(1)}) fusion(f32[512,2048]{1,0:T(8,128)S(1)} %get-tuple-element.36, f32[512]{0:T(512)S(1)} %get-tuple-element.24, f32[2048]{0:T(1024)S(1)} %bitcast.83, f32[512]{0:T(512)S(1)} %get-tuple-element.25, f32[512,2048]{1,0:T(8,128)S(1)} %fusion.73, f32[512]{0:T(512)S(1)} %get-tuple-element.26, ...), kind=kLoop, calls=%fused_computation.10 | loop fusion | flops 9435648 | bytes 12603392 | tf_op jit(solution)/shard_map/reduce_sum | solution.py:21
  34.9 0.9 fusion.37
  35.9 0.9 fusion.43
  36.8 0.9 fusion.49
  37.7 0.8 copy_bitcast_fusion.1
  38.5 6.1 %all-to-all-start.1 = ((bf16[16,128,64]{1,2,0:T(8,128)(2,1)}), bf16[16,128,64]{1,2,0:T(8,128)(2,1)S(1)}, u32[]{:S(2)}, u32[]{:S(2)}) async-start(bf16[16,128,64]{1,2,0:T(8,128)(2,1)} %copy_bitcast_fusion.1), calls=%async_computation.1 | async-start | bytes 524288 | tf_op jit(solution)/shard_map/all_to_all | solution.py:260
  44.7 0.2 eq.79
  44.9 5.3 %all-to-all-done.1 = bf16[16,128,64]{1,2,0:T(8,128)(2,1)S(1)} async-done(((bf16[16,128,64]{1,2,0:T(8,128)(2,1)}), bf16[16,128,64]{1,2,0:T(8,128)(2,1)S(1)}, u32[]{:S(2)}, u32[]{:S(2)}) %all-to-all-start.1) | async-done | bytes 262176 | tf_op jit(solution)/shard_map/all_to_all | solution.py:260
  50.2 0.5 fusion.91
  50.7 0.2 multiply_reduce_fusion
  50.9 1.6 convolution_convert_fusion
  52.5 62.1 %shard_map.127 = (bf16[32,16,1024]{2,1,0:T(8,128)(2,1)}, bf16[2,8,64,1024]{3,2,1,0:T(8,128)(2,1)}, bf16[2,8,64,1024]{3,2,1,0:T(8,128)(2,1)}) custom-call(bf16[32,16,1024]{2,1,0:T(8,128)(2,1)} %bitcast.72, bf16[64,1024]{1,0:T(8,128)(2,1)} %bitcast.78, bf16[64,1024]{1,0:T(8,128)(2,1)} %bitcast.79), custom_call_target="tpu_custom_call" | custom-call | tf_op jit(solution)/shard_map/pallas_call | solution.py:193
  114.6 6.0 %convolution_convert_fusion.1 = bf16[512,1024]{1,0:T(8,128)(2,1)} fusion(bf16[1024,1024]{1,0:T(8,128)(2,1)} %bitcast.92, bf16[512,1024]{1,0:T(8,128)(2,1)} %bitcast.93, bf16[1024,1024]{1,0:T(8,128)(2,1)} %bitcast.91), kind=kOutput, calls=%fused_computation.32 | convolution fusion | flops 2152726528 | bytes 6291456 | tf_op jit(solution)/shard_map/dot_general | solution.py:297
  120.6 56.1 %shard_map.128 = bf16[32,16,1024]{2,1,0:T(8,128)(2,1)} custom-call(bf16[32,16,1024]{2,1,0:T(8,128)(2,1)} %bitcast.76), custom_call_target="tpu_custom_call" | custom-call | tf_op jit(solution)/shard_map/pallas_call | solution.py:76
  176.7 1.7 fusion.25
  178.5 0.8 fusion.62
  (31 shorter events, 1.0 us)
Async XLA Ops:
  0.0 50.2 %copy-start = (bf16[1024,1024]{1,0:T(8,128)(2,1)S(1)}, bf16[1024,1024]{1,0:T(8,128)(2,1)}, u32[]{:S(2)}) copy-start(bf16[1024,1024]{1,0:T(8,128)(2,1)} %param.21) | copy-start | bytes 6291460
  0.0 15.2 %copy-start.4 = (s32[1,128,2]{1,2,0:T(2,128)S(1)}, s32[1,128,2]{1,2,0:T(2,128)}, u32[]{:S(2)}) copy-start(s32[1,128,2]{1,2,0:T(2,128)} %param.24) | copy-start | bytes 3076
  0.0 16.8 %copy-start.2 = (f32[1,2,1024]{2,1,0:T(2,128)S(1)}, f32[1,2,1024]{2,1,0:T(2,128)}, u32[]{:S(2)}) copy-start(f32[1,2,1024]{2,1,0:T(2,128)} %param.23) | copy-start | bytes 24580
  6.0 21.1 %all-to-all-start = ((bf16[16,128,208]{1,2,0:T(8,128)(2,1)}), bf16[16,128,208]{1,2,0:T(8,128)(2,1)S(1)}, u32[]{:S(2)}, u32[]{:S(2)}) async-start(bf16[16,128,208]{1,2,0:T(8,128)(2,1)} %fusion.58), calls=%async_computation | async-start | bytes 1703936 | tf_op jit(solution)/shard_map/all_to_all | solution.py:251
  36.8 8.1 %copy-start.3 = (f32[1,2,1024]{2,1,0:T(2,128)S(1)}, f32[1,2,1024]{2,1,0:T(2,128)}, u32[]{:S(2)}) copy-start(f32[1,2,1024]{2,1,0:T(2,128)} %param.22) | copy-start | bytes 24580
  36.8 13.4 %copy-start.1 = (bf16[1,128,1024]{2,1,0:T(8,128)(2,1)S(1)}, bf16[1,128,1024]{2,1,0:T(8,128)(2,1)}, u32[]{:S(2)}) copy-start(bf16[1,128,1024]{2,1,0:T(8,128)(2,1)} %param.15) | copy-start | bytes 786436
  38.5 11.7 %all-to-all-start.1 = ((bf16[16,128,64]{1,2,0:T(8,128)(2,1)}), bf16[16,128,64]{1,2,0:T(8,128)(2,1)S(1)}, u32[]{:S(2)}, u32[]{:S(2)}) async-start(bf16[16,128,64]{1,2,0:T(8,128)(2,1)} %copy_bitcast_fusion.1), calls=%async_computation.1 | async-start | bytes 524288 | tf_op jit(solution)/shard_map/all_to_all | solution.py:260
  114.6 62.1 %copy-start.5 = (f32[1,128,2]{1,2,0:T(2,128)S(1)}, f32[1,128,2]{1,2,0:T(2,128)}, u32[]{:S(2)}) copy-start(f32[1,128,2]{1,2,0:T(2,128)} %param.25) | copy-start | bytes 3076

commit v11 on v10

--- a/solution.py
+++ b/solution.py
@@ -8,7 +8,7 @@
 from jax.sharding import PartitionSpec as P
 
 eps = 1e-06
-query_block = 512
+query_block = 1024
 
 
 def head_attention(query_rows, key_rows, value_rows, offset_row):

time: 180 us -> 177 us (0.983)
  other arithmetic: 7.68 us -> 5.8 us
    dot_general x4 -> x2, matrix products: 3.64 us -> 3.32 us  [head_attention(): jnp.dot(unscaled.astype(jnp.bfloat16), value_rows, preferred_element_type...]
    dot_general x4 -> x2, matrix products: 4.35 us -> 4.14 us  [head_attention(): jnp.dot(block, key_rows.T, preferred_element_type=jnp.float32)]
    unnamed x16 -> x20, local copies, waits for them, and re-layouts: 3.65 us -> 3.66 us
where the time goes in v11:
time: 177 us
  Pallas kernels  118 us (67%)
  matrix products  17.3 us (10%)
  starting transfers between devices  15.4 us (9%)
  waiting for transfers between devices  15.3 us (9%)
  other arithmetic  5.8 us (3%)
  local copies, waits for them, and re-layouts  4.6 us (3%)
    pallas_call x1, Pallas kernels, dispatch(): pl.pallas_call(functools.partial(dispatch_kernel, expert_n, tm_n), out_sh...  62.1 us
    pallas_call x1, Pallas kernels, exchange(): pl.pallas_call(functools.partial(exchange_kernel, axis, n), out_shape=jax...  56.2 us
    all_to_all x1, waiting for transfers between devices, on_device(): lax.all_to_all(packed, 'tm', split_axis=0, concat_axis=0, tiled=True)  10.1 us
    all_to_all x1, starting transfers between devices, on_device(): lax.all_to_all(packed, 'tm', split_axis=0, concat_axis=0, tiled=True)  9.25 us
    all_to_all x1, starting transfers between devices, on_device(): lax.all_to_all(head_out, 'tm', split_axis=0, concat_axis=0, tiled=True)  6.14 us
    dot_general x1, matrix products, on_device(): jnp.dot(hidden, down_rows, preferred_element_type=jnp.float32)  6.02 us
    all_to_all x1, waiting for transfers between devices, on_device(): lax.all_to_all(head_out, 'tm', split_axis=0, concat_axis=0, tiled=True)  5.26 us
    dot_general x2, matrix products, head_attention(): jnp.dot(block, key_rows.T, preferred_element_type=jnp.float32)  4.14 us
  transfers between devices with their start and end apart: 2, of which 2 were waited for; matrix products, arithmetic and copies ran while one was open for 1% of the time, Pallas kernels for 0%

profile of v11, /device:TPU:8, one launch (start us, length us, event | category | flops | bytes accessed | tf_op | source)
XLA Modules:
  0.0 177.0 jit_solution(17788397644908537520)
XLA Ops:
  0.0 1.3 copy.26
  1.3 1.1 copy.27
  2.5 1.1 copy.28
  3.7 1.0 fusion.38
  4.7 9.3 %all-to-all-start = ((bf16[16,128,208]{1,2,0:T(8,128)(2,1)}), bf16[16,128,208]{1,2,0:T(8,128)(2,1)S(1)}, u32[]{:S(2)}, u32[]{:S(2)}) async-start(bf16[16,128,208]{1,2,0:T(8,128)(2,1)} %fusion.38), calls=%async_computation | async-start | bytes 1703936 | tf_op jit(solution)/shard_map/all_to_all | solution.py:251
  14.0 0.1 copy.31
  14.1 0.1 eq.73
  14.2 0.1 reshape_squeeze.11
  14.4 0.6 reduce-window.6
  15.0 0.2 slice_reduce_fusion
  15.2 0.1 fusion.56
  15.3 0.1 reduce_sum.71
  15.6 0.1 iota_compare_fusion.2
  15.7 10.1 %all-to-all-done = bf16[16,128,208]{1,2,0:T(8,128)(2,1)S(1)} async-done(((bf16[16,128,208]{1,2,0:T(8,128)(2,1)}), bf16[16,128,208]{1,2,0:T(8,128)(2,1)S(1)}, u32[]{:S(2)}, u32[]{:S(2)}) %all-to-all-start) | async-done | bytes 852000 | tf_op jit(solution)/shard_map/all_to_all | solution.py:251
  25.8 0.1 copy_bitcast_fusion
  25.9 1.4 add_reduce_fusion.1
  27.3 2.8 %fusion = (f32[1024]{0:T(1024)S(1)}, f32[1024]{0:T(1024)S(1)}, f32[1024,2048]{1,0:T(8,128)S(1)}) fusion(f32[1024,2048]{1,0:T(8,128)S(1)} %get-tuple-element.30, f32[1024]{0:T(1024)S(1)} %get-tuple-element.29, f32[2048]{0:T(1024)S(1)} %bitcast.79, bf16[2048,208]{0,1:T(8,128)(2,1)S(1)} %copy_bitcast_fusion), kind=kOutput, calls=%fused_computation.4 | convolution fusion | flops 278919168 | bytes 17190912 | tf_op jit(solution)/shard_map/dot_general | solution.py:18
  30.0 2.0 %fusion.2 = f32[1024]{0:T(1024)S(1)} fusion(f32[1024,2048]{1,0:T(8,128)S(1)} %get-tuple-element.31, f32[1024]{0:T(1024)S(1)} %get-tuple-element.24, f32[2048]{0:T(1024)S(1)} %bitcast.80), kind=kLoop, calls=%fused_computation.6 | loop fusion | flops 6290432 | bytes 8404992 | tf_op jit(solution)/shard_map/reduce_sum | solution.py:21
  32.0 1.7 fusion.29
  33.7 1.7 fusion.23
  35.3 0.8 copy_bitcast_fusion.1
  36.1 6.1 %all-to-all-start.1 = ((bf16[16,128,64]{1,2,0:T(8,128)(2,1)}), bf16[16,128,64]{1,2,0:T(8,128)(2,1)S(1)}, u32[]{:S(2)}, u32[]{:S(2)}) async-start(bf16[16,128,64]{1,2,0:T(8,128)(2,1)} %copy_bitcast_fusion.1), calls=%async_computation.1 | async-start | bytes 524288 | tf_op jit(solution)/shard_map/all_to_all | solution.py:260
  42.3 0.2 eq.79
  42.5 5.3 %all-to-all-done.1 = bf16[16,128,64]{1,2,0:T(8,128)(2,1)S(1)} async-done(((bf16[16,128,64]{1,2,0:T(8,128)(2,1)}), bf16[16,128,64]{1,2,0:T(8,128)(2,1)S(1)}, u32[]{:S(2)}, u32[]{:S(2)}) %all-to-all-start.1) | async-done | bytes 262176 | tf_op jit(solution)/shard_map/all_to_all | solution.py:260
  47.8 0.5 fusion.63
  48.3 0.2 multiply_reduce_fusion
  48.6 1.6 convolution_convert_fusion
  50.1 62.1 %shard_map.127 = (bf16[32,16,1024]{2,1,0:T(8,128)(2,1)}, bf16[2,8,64,1024]{3,2,1,0:T(8,128)(2,1)}, bf16[2,8,64,1024]{3,2,1,0:T(8,128)(2,1)}) custom-call(bf16[32,16,1024]{2,1,0:T(8,128)(2,1)} %bitcast.72, bf16[64,1024]{1,0:T(8,128)(2,1)} %bitcast.83, bf16[64,1024]{1,0:T(8,128)(2,1)} %bitcast.84), custom_call_target="tpu_custom_call" | custom-call | tf_op jit(solution)/shard_map/pallas_call | solution.py:193
  112.2 6.0 %convolution_convert_fusion.1 = bf16[512,1024]{1,0:T(8,128)(2,1)} fusion(bf16[1024,1024]{1,0:T(8,128)(2,1)} %bitcast.90, bf16[512,1024]{1,0:T(8,128)(2,1)} %bitcast.91, bf16[1024,1024]{1,0:T(8,128)(2,1)} %bitcast.89), kind=kOutput, calls=%fused_computation.22 | convolution fusion | flops 2152726528 | bytes 6291456 | tf_op jit(solution)/shard_map/dot_general | solution.py:297
  118.3 56.2 %shard_map.128 = bf16[32,16,1024]{2,1,0:T(8,128)(2,1)} custom-call(bf16[32,16,1024]{2,1,0:T(8,128)(2,1)} %bitcast.76), custom_call_target="tpu_custom_call" | custom-call | tf_op jit(solution)/shard_map/pallas_call | solution.py:76
  174.5 1.7 fusion.17
  176.2 0.8 fusion.42
  (31 shorter events, 0.4 us)
Async XLA Ops:
  0.0 47.8 %copy-start = (bf16[1024,1024]{1,0:T(8,128)(2,1)S(1)}, bf16[1024,1024]{1,0:T(8,128)(2,1)}, u32[]{:S(2)}) copy-start(bf16[1024,1024]{1,0:T(8,128)(2,1)} %param.21) | copy-start | bytes 6291460
  0.0 3.6 %copy-start.7 = (s32[1,128]{1,0:T(1,128)S(1)}, s32[1,128]{1,0:T(1,128)}, u32[]{:S(2)}) copy-start(s32[1,128]{1,0:T(1,128)} %param.19) | copy-start | bytes 1540
  0.0 3.6 %copy-start.5 = (bf16[16]{0:T(256)(128)(2,1)S(1)}, bf16[16]{0:T(256)(128)(2,1)}, u32[]{:S(2)}) copy-start(bf16[16]{0:T(256)(128)(2,1)} %param.20) | copy-start | bytes 100
  1.3 12.6 %copy-start.4 = (s32[1,128,2]{1,2,0:T(2,128)S(1)}, s32[1,128,2]{1,2,0:T(2,128)}, u32[]{:S(2)}) copy-start(s32[1,128,2]{1,2,0:T(2,128)} %param.24) | copy-start | bytes 3076
  3.6 11.9 %copy-start.2 = (f32[1,2,1024]{2,1,0:T(2,128)S(1)}, f32[1,2,1024]{2,1,0:T(2,128)}, u32[]{:S(2)}) copy-start(f32[1,2,1024]{2,1,0:T(2,128)} %param.23) | copy-start | bytes 24580
  4.7 21.1 %all-to-all-start = ((bf16[16,128,208]{1,2,0:T(8,128)(2,1)}), bf16[16,128,208]{1,2,0:T(8,128)(2,1)S(1)}, u32[]{:S(2)}, u32[]{:S(2)}) async-start(bf16[16,128,208]{1,2,0:T(8,128)(2,1)} %fusion.38), calls=%async_computation | async-start | bytes 1703936 | tf_op jit(solution)/shard_map/all_to_all | solution.py:251
  33.7 8.8 %copy-start.3 = (f32[1,2,1024]{2,1,0:T(2,128)S(1)}, f32[1,2,1024]{2,1,0:T(2,128)}, u32[]{:S(2)}) copy-start(f32[1,2,1024]{2,1,0:T(2,128)} %param.22) | copy-start | bytes 24580
  33.7 14.1 %copy-start.1 = (bf16[1,128,1024]{2,1,0:T(8,128)(2,1)S(1)}, bf16[1,128,1024]{2,1,0:T(8,128)(2,1)}, u32[]{:S(2)}) copy-start(bf16[1,128,1024]{2,1,0:T(8,128)(2,1)} %param.15) | copy-start | bytes 786436
  36.1 11.7 %all-to-all-start.1 = ((bf16[16,128,64]{1,2,0:T(8,128)(2,1)}), bf16[16,128,64]{1,2,0:T(8,128)(2,1)S(1)}, u32[]{:S(2)}, u32[]{:S(2)}) async-start(bf16[16,128,64]{1,2,0:T(8,128)(2,1)} %copy_bitcast_fusion.1), calls=%async_computation.1 | async-start | bytes 524288 | tf_op jit(solution)/shard_map/all_to_all | solution.py:260
  118.3 56.2 %copy-start.6 = (f32[1,128,2]{1,2,0:T(2,128)S(1)}, f32[1,128,2]{1,2,0:T(2,128)}, u32[]{:S(2)}) copy-start(f32[1,128,2]{1,2,0:T(2,128)} %param.25) | copy-start | bytes 3076

commit v12 on v11

--- a/solution.py
+++ b/solution.py
@@ -8,7 +8,7 @@
 from jax.sharding import PartitionSpec as P
 
 eps = 1e-06
-query_block = 1024
+query_block = 2048
 
 
 def head_attention(query_rows, key_rows, value_rows, offset_row):

time: 177 us -> 178 us (level)
    dot_general x2 -> x1, matrix products: 4.14 us -> 2.44 us  [head_attention(): jnp.dot(block, key_rows.T, preferred_element_type=jnp.float32)]
    unnamed x20 -> x18, local copies, waits for them, and re-layouts: 3.66 us -> 3.66 us
where the time goes in v12:
time: 178 us
  Pallas kernels  118 us (66%)
  matrix products  16.3 us (9%)
  starting transfers between devices  15.4 us (9%)
  waiting for transfers between devices  15.3 us (9%)
  other arithmetic  6.73 us (4%)
  local copies, waits for them, and re-layouts  5.37 us (3%)
    pallas_call x1, Pallas kernels, dispatch(): pl.pallas_call(functools.partial(dispatch_kernel, expert_n, tm_n), out_sh...  62.1 us
    pallas_call x1, Pallas kernels, exchange(): pl.pallas_call(functools.partial(exchange_kernel, axis, n), out_shape=jax...  56.2 us
    all_to_all x1, waiting for transfers between devices, on_device(): lax.all_to_all(packed, 'tm', split_axis=0, concat_axis=0, tiled=True)  10.1 us
    all_to_all x1, starting transfers between devices, on_device(): lax.all_to_all(packed, 'tm', split_axis=0, concat_axis=0, tiled=True)  9.25 us
    all_to_all x1, starting transfers between devices, on_device(): lax.all_to_all(head_out, 'tm', split_axis=0, concat_axis=0, tiled=True)  6.14 us
    dot_general x1, matrix products, on_device(): jnp.dot(hidden, down_rows, preferred_element_type=jnp.float32)  6.03 us
    all_to_all x1, waiting for transfers between devices, on_device(): lax.all_to_all(head_out, 'tm', split_axis=0, concat_axis=0, tiled=True)  5.26 us
    reduce_sum x1, other arithmetic, head_attention(): total = jnp.sum(unscaled, axis=1, keepdims=True)  3.68 us
  transfers between devices with their start and end apart: 2, of which 2 were waited for; matrix products, arithmetic and copies ran while one was open for 1% of the time, Pallas kernels for 0%

profile of v12, /device:TPU:8, one launch (start us, length us, event | category | flops | bytes accessed | tf_op | source)
XLA Modules:
  0.0 177.7 jit_solution(8162651757881869292)
XLA Ops:
  0.0 1.3 copy.26
  1.3 1.1 copy.27
  2.5 1.1 copy.28
  3.6 0.1 broadcast_select_fusion
  3.7 1.0 fusion.31
  4.7 9.3 %all-to-all-start = ((bf16[16,128,208]{1,2,0:T(8,128)(2,1)}), bf16[16,128,208]{1,2,0:T(8,128)(2,1)S(1)}, u32[]{:S(2)}, u32[]{:S(2)}) async-start(bf16[16,128,208]{1,2,0:T(8,128)(2,1)} %fusion.31), calls=%async_computation | async-start | bytes 1703936 | tf_op jit(solution)/shard_map/all_to_all | solution.py:251
  14.0 0.1 copy.31
  14.1 0.1 eq.73
  14.2 0.1 reshape_squeeze.11
  14.4 0.6 reduce-window.6
  15.0 0.2 slice_reduce_fusion
  15.2 0.1 fusion.45
  15.3 0.1 reduce_sum.61
  15.6 0.1 iota_compare_fusion.2
  15.7 10.1 %all-to-all-done = bf16[16,128,208]{1,2,0:T(8,128)(2,1)S(1)} async-done(((bf16[16,128,208]{1,2,0:T(8,128)(2,1)}), bf16[16,128,208]{1,2,0:T(8,128)(2,1)S(1)}, u32[]{:S(2)}, u32[]{:S(2)}) %all-to-all-start) | async-done | bytes 852000 | tf_op jit(solution)/shard_map/all_to_all | solution.py:251
  25.8 0.1 copy_bitcast_fusion
  25.9 2.4 %add_reduce_fusion = (f32[2048]{0:T(1024)S(1)}, f32[2048,2048]{0,1:T(8,128)S(1)}) fusion(f32[2048]{0:T(1024)S(1)} %bitcast.78, bf16[2048,208]{0,1:T(8,128)(2,1)S(1)} %copy_bitcast_fusion), kind=kOutput, calls=%fused_computation.1 | convolution fusion | flops 545257472 | bytes 17317888 | tf_op jit(solution)/shard_map/dot_general | solution.py:18
  28.3 3.7 %fusion = f32[2048]{0:T(1024)S(1)} fusion(f32[2048,2048]{0,1:T(8,128)S(1)} %get-tuple-element.28, f32[2048]{0:T(1024)S(1)} %get-tuple-element.27, f32[2048]{0:T(1024)S(1)} %bitcast.79), kind=kLoop, calls=%fused_computation.2 | loop fusion | flops 12580864 | bytes 16801792 | tf_op jit(solution)/shard_map/reduce_sum | solution.py:21
  32.0 3.1 %fusion.22 = bf16[8,16,8,128]{3,2,1,0:T(8,128)(2,1)S(1)} fusion(f32[2048,2048]{0,1:T(8,128)S(1)} %get-tuple-element.28, f32[2048]{0:T(1024)S(1)} %get-tuple-element.27, f32[2048]{0:T(1024)S(1)} %bitcast.80, bf16[2048,208]{0,1:T(8,128)(2,1)S(1)} %copy_bitcast_fusion, f32[2048]{0:T(1024)S(1)} %fusion), kind=kOutput, calls=%fused_computation.25 | convolution fusion | flops 549715968 | bytes 17326080 | tf_op jit(solution)/shard_map/dot_general | solution.py:22
  35.1 0.8 copy.45
  35.9 6.1 %all-to-all-start.1 = ((bf16[16,128,64]{1,2,0:T(8,128)(2,1)}), bf16[16,128,64]{1,2,0:T(8,128)(2,1)S(1)}, u32[]{:S(2)}, u32[]{:S(2)}) async-start(bf16[16,128,64]{1,2,0:T(8,128)(2,1)} %bitcast.70), calls=%async_computation.1 | async-start | bytes 524288 | tf_op jit(solution)/shard_map/all_to_all | solution.py:260
  42.1 0.1 fusion.34
  42.1 0.2 eq.79
  42.3 5.3 %all-to-all-done.1 = bf16[16,128,64]{1,2,0:T(8,128)(2,1)S(1)} async-done(((bf16[16,128,64]{1,2,0:T(8,128)(2,1)}), bf16[16,128,64]{1,2,0:T(8,128)(2,1)S(1)}, u32[]{:S(2)}, u32[]{:S(2)}) %all-to-all-start.1) | async-done | bytes 262176 | tf_op jit(solution)/shard_map/all_to_all | solution.py:260
  47.6 1.5 fusion.52
  49.1 0.2 multiply_reduce_fusion
  49.3 1.6 convolution_convert_fusion
  50.9 62.1 %shard_map.127 = (bf16[32,16,1024]{2,1,0:T(8,128)(2,1)}, bf16[2,8,64,1024]{3,2,1,0:T(8,128)(2,1)}, bf16[2,8,64,1024]{3,2,1,0:T(8,128)(2,1)}) custom-call(bf16[32,16,1024]{2,1,0:T(8,128)(2,1)} %bitcast.72, bf16[64,1024]{1,0:T(8,128)(2,1)} %bitcast.81, bf16[64,1024]{1,0:T(8,128)(2,1)} %bitcast.82), custom_call_target="tpu_custom_call" | custom-call | tf_op jit(solution)/shard_map/pallas_call | solution.py:193
  113.0 6.0 %convolution_convert_fusion.1 = bf16[512,1024]{1,0:T(8,128)(2,1)} fusion(bf16[1024,1024]{1,0:T(8,128)(2,1)} %bitcast.88, bf16[512,1024]{1,0:T(8,128)(2,1)} %bitcast.89, bf16[1024,1024]{1,0:T(8,128)(2,1)} %bitcast.87), kind=kOutput, calls=%fused_computation.19 | convolution fusion | flops 2152726528 | bytes 6291456 | tf_op jit(solution)/shard_map/dot_general | solution.py:297
  119.0 56.2 %shard_map.128 = bf16[32,16,1024]{2,1,0:T(8,128)(2,1)} custom-call(bf16[32,16,1024]{2,1,0:T(8,128)(2,1)} %bitcast.76), custom_call_target="tpu_custom_call" | custom-call | tf_op jit(solution)/shard_map/pallas_call | solution.py:76
  175.2 1.7 fusion.19
  176.9 0.8 fusion.35
  (27 shorter events, 0.2 us)
Async XLA Ops:
  0.0 47.6 %copy-start = (bf16[1024,1024]{1,0:T(8,128)(2,1)S(1)}, bf16[1024,1024]{1,0:T(8,128)(2,1)}, u32[]{:S(2)}) copy-start(bf16[1024,1024]{1,0:T(8,128)(2,1)} %param.21) | copy-start | bytes 6291460
  0.0 3.6 %copy-start.6 = (s32[1,128]{1,0:T(1,128)S(1)}, s32[1,128]{1,0:T(1,128)}, u32[]{:S(2)}) copy-start(s32[1,128]{1,0:T(1,128)} %param.19) | copy-start | bytes 1540
  0.0 3.6 %copy-start.4 = (bf16[16]{0:T(256)(128)(2,1)S(1)}, bf16[16]{0:T(256)(128)(2,1)}, u32[]{:S(2)}) copy-start(bf16[16]{0:T(256)(128)(2,1)} %param.20) | copy-start | bytes 100
  1.3 12.6 %copy-start.3 = (s32[1,128,2]{1,2,0:T(2,128)S(1)}, s32[1,128,2]{1,2,0:T(2,128)}, u32[]{:S(2)}) copy-start(s32[1,128,2]{1,2,0:T(2,128)} %param.24) | copy-start | bytes 3076
  3.6 11.9 %copy-start.1 = (f32[1,2,1024]{2,1,0:T(2,128)S(1)}, f32[1,2,1024]{2,1,0:T(2,128)}, u32[]{:S(2)}) copy-start(f32[1,2,1024]{2,1,0:T(2,128)} %param.23) | copy-start | bytes 24580
  4.7 21.1 %all-to-all-start = ((bf16[16,128,208]{1,2,0:T(8,128)(2,1)}), bf16[16,128,208]{1,2,0:T(8,128)(2,1)S(1)}, u32[]{:S(2)}, u32[]{:S(2)}) async-start(bf16[16,128,208]{1,2,0:T(8,128)(2,1)} %fusion.31), calls=%async_computation | async-start | bytes 1703936 | tf_op jit(solution)/shard_map/all_to_all | solution.py:251
  32.0 10.3 %copy-start.2 = (f32[1,2,1024]{2,1,0:T(2,128)S(1)}, f32[1,2,1024]{2,1,0:T(2,128)}, u32[]{:S(2)}) copy-start(f32[1,2,1024]{2,1,0:T(2,128)} %param.22) | copy-start | bytes 24580
  35.9 11.7 %all-to-all-start.1 = ((bf16[16,128,64]{1,2,0:T(8,128)(2,1)}), bf16[16,128,64]{1,2,0:T(8,128)(2,1)S(1)}, u32[]{:S(2)}, u32[]{:S(2)}) async-start(bf16[16,128,64]{1,2,0:T(8,128)(2,1)} %bitcast.70), calls=%async_computation.1 | async-start | bytes 524288 | tf_op jit(solution)/shard_map/all_to_all | solution.py:260
  119.0 56.2 %copy-start.5 = (f32[1,128,2]{1,2,0:T(2,128)S(1)}, f32[1,128,2]{1,2,0:T(2,128)}, u32[]{:S(2)}) copy-start(f32[1,128,2]{1,2,0:T(2,128)} %param.25) | copy-start | bytes 3076

commit v13 on v11

--- a/solution.py
+++ b/solution.py
@@ -206,6 +206,79 @@
         compiler_params=pltpu.CompilerParams(collective_id=collective_id, has_side_effects=True),
     )(slots, own_up, own_down)
 
+def ffn_return_kernel(
+    n, group, arrived_ref, up_ref, down_ref, out_ref, rows_buf, out_buf, send_sems, recv_sems, local_sem
+):
+    mesh_ids = pl.DeviceIdType.MESH
+    me = lax.axis_index("expert")
+    cap = arrived_ref.shape[1]
+    barrier = pltpu.get_barrier_semaphore()
+    for k in range(1, n):
+        pl.semaphore_signal(barrier, inc=1, device_id={"expert": lax.rem(me + k, n)}, device_id_type=mesh_ids)
+    pl.semaphore_wait(barrier, n - 1)
+    copies = []
+    local = None
+    for c in range(n // group):
+        for j in range(group):
+            peer = lax.rem(me + c * group + j, n)
+            rows_buf[pl.ds(j * cap, cap), :] = arrived_ref[peer]
+        hidden = lax.dot_general(
+            rows_buf[...], up_ref[...], (((1,), (1,)), ((), ())), preferred_element_type=jnp.float32
+        )
+        hidden = jax.nn.gelu(hidden, approximate=True).astype(jnp.bfloat16)
+        produced = jnp.dot(hidden, down_ref[...], preferred_element_type=jnp.float32)
+        out_buf[pl.ds(c * group * cap, group * cap), :] = produced.astype(jnp.bfloat16)
+        for j in range(group):
+            k = c * group + j
+            block = out_buf.at[pl.ds(k * cap, cap)]
+            if k == 0:
+                local = pltpu.make_async_copy(block, out_ref.at[me], local_sem)
+                local.start()
+                continue
+            copy = pltpu.make_async_remote_copy(
+                src_ref=block,
+                dst_ref=out_ref.at[me],
+                send_sem=send_sems.at[k],
+                recv_sem=recv_sems.at[k],
+                device_id={"expert": lax.rem(me + k, n)},
+                device_id_type=mesh_ids,
+            )
+            copy.start()
+            copies.append(copy)
+    local.wait()
+    for copy in copies:
+        copy.wait_send()
+    for k in range(1, n):
+        source = lax.rem(me + n - k, n)
+        pltpu.make_async_remote_copy(
+            src_ref=out_buf.at[pl.ds(k * cap, cap)],
+            dst_ref=out_ref.at[source],
+            send_sem=send_sems.at[k],
+            recv_sem=recv_sems.at[k],
+            device_id={"expert": source},
+            device_id_type=mesh_ids,
+        ).wait_recv()
+
+
+def ffn_return(arrived, up_rows, down_rows, collective_id, group=8):
+    n, cap, width = arrived.shape
+    vmem = pl.BlockSpec(memory_space=pltpu.VMEM)
+    return pl.pallas_call(
+        functools.partial(ffn_return_kernel, n, group),
+        out_shape=jax.ShapeDtypeStruct(arrived.shape, arrived.dtype),
+        in_specs=[vmem, vmem, vmem],
+        out_specs=pl.BlockSpec(memory_space=pl.ANY),
+        scratch_shapes=[
+            pltpu.VMEM((group * cap, width), arrived.dtype),
+            pltpu.VMEM((n * cap, width), arrived.dtype),
+            pltpu.SemaphoreType.DMA((n,)),
+            pltpu.SemaphoreType.DMA((n,)),
+            pltpu.SemaphoreType.DMA,
+        ],
+        compiler_params=pltpu.CompilerParams(collective_id=collective_id, has_side_effects=True),
+    )(arrived, up_rows, down_rows)
+
+
 def layer_norm(mixed, shift_row, scale_row):
     center = jnp.mean(mixed, axis=-1, keepdims=True)
     deviation = mixed - center
@@ -289,14 +362,7 @@
     )
     up_rows = gathered_up.reshape(-1, model_width)
     down_rows = gathered_down.reshape(-1, model_width)
-    grouped = arrived.reshape(source_count * local_experts * capacity, model_width)
-    hidden = jax.nn.gelu(
-        jnp.einsum("rd,fd->rf", grouped, up_rows, preferred_element_type=jnp.float32),
-        approximate=True,
-    ).astype(jnp.bfloat16)
-    produced = jnp.dot(hidden, down_rows, preferred_element_type=jnp.float32).astype(jnp.bfloat16)
-    produced = produced.reshape(source_count * local_experts, capacity, model_width)
-    returned = exchange(produced, "expert", 3)
+    returned = ffn_return(arrived, up_rows, down_rows, 3)
     picked = jnp.einsum(
         "sa,sd->ad",
         placing,

time: 177 us -> 180 us (1.017)
  Pallas kernels: 118 us -> 126 us
  matrix products: 17.3 us -> 11.3 us
    pallas_call x1, Pallas kernels: 56.2 us -> 63.4 us  [ffn_return(): pl.pallas_call(functools.partial(ffn_return_kernel, n, group), out_shape=...]
    dot_general x1 -> x0, matrix products: 6.02 us -> none  [on_device(): jnp.dot(hidden, down_rows, preferred_element_type=jnp.float32)]
    unnamed x20 -> x10, local copies, waits for them, and re-layouts: 3.66 us -> 4.31 us
  transfers between devices with their start and end apart: 2 -> 2, of which waited for: 2 -> 2; matrix products, arithmetic and copies ran while one was open for 1% -> 2% of each run, Pallas kernels for 0% -> 0%
where the time goes in v13:
time: 180 us; the launch traced here: 179 us
  Pallas kernels  126 us (70%)
  starting transfers between devices  15.4 us (9%)
  waiting for transfers between devices  13.9 us (8%)
  matrix products  11.3 us (6%)
  other arithmetic  7.12 us (4%)
  local copies, waits for them, and re-layouts  6.02 us (3%)
    pallas_call x1, Pallas kernels, ffn_return(): pl.pallas_call(functools.partial(ffn_return_kernel, n, group), out_shape=...  63.4 us
    pallas_call x1, Pallas kernels, dispatch(): pl.pallas_call(functools.partial(dispatch_kernel, expert_n, tm_n), out_sh...  62.1 us
    all_to_all x1, starting transfers between devices, on_device(): lax.all_to_all(packed, 'tm', split_axis=0, concat_axis=0, tiled=True)  9.25 us
    all_to_all x1, waiting for transfers between devices, on_device(): lax.all_to_all(packed, 'tm', split_axis=0, concat_axis=0, tiled=True)  8.63 us
    all_to_all x1, starting transfers between devices, on_device(): lax.all_to_all(head_out, 'tm', split_axis=0, concat_axis=0, tiled=True)  6.14 us
    all_to_all x1, waiting for transfers between devices, on_device(): lax.all_to_all(head_out, 'tm', split_axis=0, concat_axis=0, tiled=True)  5.26 us
    unnamed x10, local copies, waits for them, and re-layouts  4.31 us
    dot_general x2, matrix products, head_attention(): jnp.dot(block, key_rows.T, preferred_element_type=jnp.float32)  4.15 us
  transfers between devices with their start and end apart: 2, of which 2 were waited for; matrix products, arithmetic and copies ran while one was open for 2% of the time, Pallas kernels for 0%

profile of v13, /device:TPU:8, one launch (start us, length us, event | category | flops | bytes accessed | tf_op | source)
XLA Modules:
  0.0 179.4 jit_solution(8024250709447032485)
XLA Ops:
  0.0 1.3 copy.26
  1.3 1.1 copy.27
  2.4 1.1 copy.28
  3.6 0.7 compare_bitcast_fusion
  4.2 0.7 broadcast_select_fusion
  5.0 1.0 fusion.25
  5.9 9.3 %all-to-all-start = ((bf16[16,128,208]{1,2,0:T(8,128)(2,1)}), bf16[16,128,208]{1,2,0:T(8,128)(2,1)S(1)}, u32[]{:S(2)}, u32[]{:S(2)}) async-start(bf16[16,128,208]{1,2,0:T(8,128)(2,1)} %fusion.25), calls=%async_computation | async-start | bytes 1703936 | tf_op jit(solution)/shard_map/all_to_all | solution.py:324
  15.2 0.8 copy.31
  16.0 0.1 eq.73
  16.1 0.1 reshape_squeeze.11
  16.3 0.6 reduce-window.6
  16.9 0.2 slice_reduce_fusion
  17.2 0.1 reduce_sum.71
  17.4 0.8 fusion.45
  18.2 0.1 iota_compare_fusion.2
  18.4 8.6 %all-to-all-done = bf16[16,128,208]{1,2,0:T(8,128)(2,1)S(1)} async-done(((bf16[16,128,208]{1,2,0:T(8,128)(2,1)}), bf16[16,128,208]{1,2,0:T(8,128)(2,1)S(1)}, u32[]{:S(2)}, u32[]{:S(2)}) %all-to-all-start) | async-done | bytes 852000 | tf_op jit(solution)/shard_map/all_to_all | solution.py:324
  27.1 1.4 add_reduce_fusion.1
  28.5 2.8 %fusion = (f32[1024]{0:T(1024)S(1)}, f32[1024]{0:T(1024)S(1)}, f32[1024,2048]{1,0:T(8,128)S(1)}) fusion(f32[1024,2048]{1,0:T(8,128)S(1)} %get-tuple-element.30, f32[1024]{0:T(1024)S(1)} %get-tuple-element.29, f32[2048]{0:T(1024)S(1)} %bitcast.75, bf16[2048,208]{0,1:T(8,128)(2,1)S(1)} %copy_bitcast_fusion), kind=kOutput, calls=%fused_computation.4 | convolution fusion | flops 278919168 | bytes 17190912 | tf_op jit(solution)/shard_map/dot_general | solution.py:18
  31.3 2.0 %fusion.2 = f32[1024]{0:T(1024)S(1)} fusion(f32[1024,2048]{1,0:T(8,128)S(1)} %get-tuple-element.31, f32[1024]{0:T(1024)S(1)} %get-tuple-element.24, f32[2048]{0:T(1024)S(1)} %bitcast.76), kind=kLoop, calls=%fused_computation.6 | loop fusion | flops 6290432 | bytes 8404992 | tf_op jit(solution)/shard_map/reduce_sum | solution.py:21
  33.3 1.7 fusion.21
  34.9 1.7 fusion.15
  36.6 0.8 copy_bitcast_fusion.1
  37.4 6.1 %all-to-all-start.1 = ((bf16[16,128,64]{1,2,0:T(8,128)(2,1)}), bf16[16,128,64]{1,2,0:T(8,128)(2,1)S(1)}, u32[]{:S(2)}, u32[]{:S(2)}) async-start(bf16[16,128,64]{1,2,0:T(8,128)(2,1)} %copy_bitcast_fusion.1), calls=%async_computation.1 | async-start | bytes 524288 | tf_op jit(solution)/shard_map/all_to_all | solution.py:333
  43.6 0.2 eq.79
  43.8 5.3 %all-to-all-done.1 = bf16[16,128,64]{1,2,0:T(8,128)(2,1)S(1)} async-done(((bf16[16,128,64]{1,2,0:T(8,128)(2,1)}), bf16[16,128,64]{1,2,0:T(8,128)(2,1)S(1)}, u32[]{:S(2)}, u32[]{:S(2)}) %all-to-all-start.1) | async-done | bytes 262176 | tf_op jit(solution)/shard_map/all_to_all | solution.py:333
  49.1 0.5 fusion.46
  49.6 0.2 multiply_reduce_fusion
  49.8 1.6 convolution_convert_fusion
  51.4 62.1 %shard_map.127 = (bf16[32,16,1024]{2,1,0:T(8,128)(2,1)}, bf16[2,8,64,1024]{3,2,1,0:T(8,128)(2,1)}, bf16[2,8,64,1024]{3,2,1,0:T(8,128)(2,1)}) custom-call(bf16[32,16,1024]{2,1,0:T(8,128)(2,1)} %bitcast.67, bf16[64,1024]{1,0:T(8,128)(2,1)} %bitcast.79, bf16[64,1024]{1,0:T(8,128)(2,1)} %bitcast.80), custom_call_target="tpu_custom_call" | custom-call | tf_op jit(solution)/shard_map/pallas_call | solution.py:193
  113.5 63.4 %shard_map.128 = bf16[32,16,1024]{2,1,0:T(8,128)(2,1)} custom-call(bf16[32,16,1024]{2,1,0:T(8,128)(2,1)} %get-tuple-element.20.arrived_ref, bf16[1024,1024]{1,0:T(8,128)(2,1)} %bitcast.68, bf16[1024,1024]{1,0:T(8,128)(2,1)} %bitcast.69), custom_call_target="tpu_custom_call" | custom-call | tf_op jit(solution)/shard_map/pallas_call | solution.py:266
  176.9 1.7 fusion.9
  178.6 0.8 fusion.29
  (20 shorter events, 0.4 us)
Async XLA Ops:
  0.0 49.0 %copy-start = (bf16[1024,1024]{1,0:T(8,128)(2,1)S(1)}, bf16[1024,1024]{1,0:T(8,128)(2,1)}, u32[]{:S(2)}) copy-start(bf16[1024,1024]{1,0:T(8,128)(2,1)} %param.21) | copy-start | bytes 6291460
  5.9 21.1 %all-to-all-start = ((bf16[16,128,208]{1,2,0:T(8,128)(2,1)}), bf16[16,128,208]{1,2,0:T(8,128)(2,1)S(1)}, u32[]{:S(2)}, u32[]{:S(2)}) async-start(bf16[16,128,208]{1,2,0:T(8,128)(2,1)} %fusion.25), calls=%async_computation | async-start | bytes 1703936 | tf_op jit(solution)/shard_map/all_to_all | solution.py:324
  33.3 10.5 %copy-start.2 = (f32[1,2,1024]{2,1,0:T(2,128)S(1)}, f32[1,2,1024]{2,1,0:T(2,128)}, u32[]{:S(2)}) copy-start(f32[1,2,1024]{2,1,0:T(2,128)} %param.22) | copy-start | bytes 24580
  33.3 15.8 %copy-start.1 = (bf16[1,128,1024]{2,1,0:T(8,128)(2,1)S(1)}, bf16[1,128,1024]{2,1,0:T(8,128)(2,1)}, u32[]{:S(2)}) copy-start(bf16[1,128,1024]{2,1,0:T(8,128)(2,1)} %param.15) | copy-start | bytes 786436
  37.4 11.7 %all-to-all-start.1 = ((bf16[16,128,64]{1,2,0:T(8,128)(2,1)}), bf16[16,128,64]{1,2,0:T(8,128)(2,1)S(1)}, u32[]{:S(2)}, u32[]{:S(2)}) async-start(bf16[16,128,64]{1,2,0:T(8,128)(2,1)} %copy_bitcast_fusion.1), calls=%async_computation.1 | async-start | bytes 524288 | tf_op jit(solution)/shard_map/all_to_all | solution.py:333

commit v14 on v13

--- a/solution.py
+++ b/solution.py
@@ -362,7 +362,7 @@
     )
     up_rows = gathered_up.reshape(-1, model_width)
     down_rows = gathered_down.reshape(-1, model_width)
-    returned = ffn_return(arrived, up_rows, down_rows, 3)
+    returned = ffn_return(arrived, up_rows, down_rows, 3, group=4)
     picked = jnp.einsum(
         "sa,sd->ad",
         placing,

time: 180 us -> 180 us (level)
  no operation moved by 1% of the time
where the time goes in v14:
time: 180 us; the launch traced here: 179 us
  Pallas kernels  125 us (69%)
  starting transfers between devices  15.4 us (9%)
  waiting for transfers between devices  13.9 us (8%)
  matrix products  11.3 us (6%)
  other arithmetic  7.12 us (4%)
  local copies, waits for them, and re-layouts  6.02 us (3%)
    pallas_call x1, Pallas kernels, ffn_return(): pl.pallas_call(functools.partial(ffn_return_kernel, n, group), out_shape=...  63.2 us
    pallas_call x1, Pallas kernels, dispatch(): pl.pallas_call(functools.partial(dispatch_kernel, expert_n, tm_n), out_sh...  62.1 us
    all_to_all x1, starting transfers between devices, on_device(): lax.all_to_all(packed, 'tm', split_axis=0, concat_axis=0, tiled=True)  9.25 us
    all_to_all x1, waiting for transfers between devices, on_device(): lax.all_to_all(packed, 'tm', split_axis=0, concat_axis=0, tiled=True)  8.63 us
    all_to_all x1, starting transfers between devices, on_device(): lax.all_to_all(head_out, 'tm', split_axis=0, concat_axis=0, tiled=True)  6.14 us
    all_to_all x1, waiting for transfers between devices, on_device(): lax.all_to_all(head_out, 'tm', split_axis=0, concat_axis=0, tiled=True)  5.26 us
    unnamed x10, local copies, waits for them, and re-layouts  4.31 us
    dot_general x2, matrix products, head_attention(): jnp.dot(block, key_rows.T, preferred_element_type=jnp.float32)  4.15 us
  transfers between devices with their start and end apart: 2, of which 2 were waited for; matrix products, arithmetic and copies ran while one was open for 2% of the time, Pallas kernels for 0%

profile of v14, /device:TPU:8, one launch (start us, length us, event | category | flops | bytes accessed | tf_op | source)
XLA Modules:
  0.0 179.2 jit_solution(16674446950772269009)
XLA Ops:
  0.0 1.3 copy.26
  1.3 1.1 copy.27
  2.4 1.1 copy.28
  3.6 0.7 compare_bitcast_fusion
  4.2 0.7 broadcast_select_fusion
  5.0 1.0 fusion.25
  5.9 9.3 %all-to-all-start = ((bf16[16,128,208]{1,2,0:T(8,128)(2,1)}), bf16[16,128,208]{1,2,0:T(8,128)(2,1)S(1)}, u32[]{:S(2)}, u32[]{:S(2)}) async-start(bf16[16,128,208]{1,2,0:T(8,128)(2,1)} %fusion.25), calls=%async_computation | async-start | bytes 1703936 | tf_op jit(solution)/shard_map/all_to_all | solution.py:324
  15.2 0.8 copy.31
  16.0 0.1 eq.73
  16.1 0.1 reshape_squeeze.11
  16.3 0.6 reduce-window.6
  16.9 0.2 slice_reduce_fusion
  17.2 0.1 reduce_sum.71
  17.4 0.8 fusion.45
  18.2 0.1 iota_compare_fusion.2
  18.4 8.6 %all-to-all-done = bf16[16,128,208]{1,2,0:T(8,128)(2,1)S(1)} async-done(((bf16[16,128,208]{1,2,0:T(8,128)(2,1)}), bf16[16,128,208]{1,2,0:T(8,128)(2,1)S(1)}, u32[]{:S(2)}, u32[]{:S(2)}) %all-to-all-start) | async-done | bytes 852000 | tf_op jit(solution)/shard_map/all_to_all | solution.py:324
  27.1 1.4 add_reduce_fusion.1
  28.5 2.8 %fusion = (f32[1024]{0:T(1024)S(1)}, f32[1024]{0:T(1024)S(1)}, f32[1024,2048]{1,0:T(8,128)S(1)}) fusion(f32[1024,2048]{1,0:T(8,128)S(1)} %get-tuple-element.30, f32[1024]{0:T(1024)S(1)} %get-tuple-element.29, f32[2048]{0:T(1024)S(1)} %bitcast.75, bf16[2048,208]{0,1:T(8,128)(2,1)S(1)} %copy_bitcast_fusion), kind=kOutput, calls=%fused_computation.4 | convolution fusion | flops 278919168 | bytes 17190912 | tf_op jit(solution)/shard_map/dot_general | solution.py:18
  31.3 2.0 %fusion.2 = f32[1024]{0:T(1024)S(1)} fusion(f32[1024,2048]{1,0:T(8,128)S(1)} %get-tuple-element.31, f32[1024]{0:T(1024)S(1)} %get-tuple-element.24, f32[2048]{0:T(1024)S(1)} %bitcast.76), kind=kLoop, calls=%fused_computation.6 | loop fusion | flops 6290432 | bytes 8404992 | tf_op jit(solution)/shard_map/reduce_sum | solution.py:21
  33.3 1.7 fusion.21
  34.9 1.7 fusion.15
  36.6 0.8 copy_bitcast_fusion.1
  37.4 6.1 %all-to-all-start.1 = ((bf16[16,128,64]{1,2,0:T(8,128)(2,1)}), bf16[16,128,64]{1,2,0:T(8,128)(2,1)S(1)}, u32[]{:S(2)}, u32[]{:S(2)}) async-start(bf16[16,128,64]{1,2,0:T(8,128)(2,1)} %copy_bitcast_fusion.1), calls=%async_computation.1 | async-start | bytes 524288 | tf_op jit(solution)/shard_map/all_to_all | solution.py:333
  43.6 0.2 eq.79
  43.8 5.3 %all-to-all-done.1 = bf16[16,128,64]{1,2,0:T(8,128)(2,1)S(1)} async-done(((bf16[16,128,64]{1,2,0:T(8,128)(2,1)}), bf16[16,128,64]{1,2,0:T(8,128)(2,1)S(1)}, u32[]{:S(2)}, u32[]{:S(2)}) %all-to-all-start.1) | async-done | bytes 262176 | tf_op jit(solution)/shard_map/all_to_all | solution.py:333
  49.1 0.5 fusion.46
  49.6 0.2 multiply_reduce_fusion
  49.8 1.6 convolution_convert_fusion
  51.4 62.1 %shard_map.127 = (bf16[32,16,1024]{2,1,0:T(8,128)(2,1)}, bf16[2,8,64,1024]{3,2,1,0:T(8,128)(2,1)}, bf16[2,8,64,1024]{3,2,1,0:T(8,128)(2,1)}) custom-call(bf16[32,16,1024]{2,1,0:T(8,128)(2,1)} %bitcast.67, bf16[64,1024]{1,0:T(8,128)(2,1)} %bitcast.79, bf16[64,1024]{1,0:T(8,128)(2,1)} %bitcast.80), custom_call_target="tpu_custom_call" | custom-call | tf_op jit(solution)/shard_map/pallas_call | solution.py:193
  113.5 63.2 %shard_map.128 = bf16[32,16,1024]{2,1,0:T(8,128)(2,1)} custom-call(bf16[32,16,1024]{2,1,0:T(8,128)(2,1)} %get-tuple-element.20.arrived_ref, bf16[1024,1024]{1,0:T(8,128)(2,1)} %bitcast.68, bf16[1024,1024]{1,0:T(8,128)(2,1)} %bitcast.69), custom_call_target="tpu_custom_call" | custom-call | tf_op jit(solution)/shard_map/pallas_call | solution.py:266
  176.7 1.7 fusion.9
  178.4 0.8 fusion.29
  (20 shorter events, 0.4 us)
Async XLA Ops:
  0.0 49.0 %copy-start = (bf16[1024,1024]{1,0:T(8,128)(2,1)S(1)}, bf16[1024,1024]{1,0:T(8,128)(2,1)}, u32[]{:S(2)}) copy-start(bf16[1024,1024]{1,0:T(8,128)(2,1)} %param.21) | copy-start | bytes 6291460
  5.9 21.1 %all-to-all-start = ((bf16[16,128,208]{1,2,0:T(8,128)(2,1)}), bf16[16,128,208]{1,2,0:T(8,128)(2,1)S(1)}, u32[]{:S(2)}, u32[]{:S(2)}) async-start(bf16[16,128,208]{1,2,0:T(8,128)(2,1)} %fusion.25), calls=%async_computation | async-start | bytes 1703936 | tf_op jit(solution)/shard_map/all_to_all | solution.py:324
  33.3 10.5 %copy-start.2 = (f32[1,2,1024]{2,1,0:T(2,128)S(1)}, f32[1,2,1024]{2,1,0:T(2,128)}, u32[]{:S(2)}) copy-start(f32[1,2,1024]{2,1,0:T(2,128)} %param.22) | copy-start | bytes 24580
  33.3 15.8 %copy-start.1 = (bf16[1,128,1024]{2,1,0:T(8,128)(2,1)S(1)}, bf16[1,128,1024]{2,1,0:T(8,128)(2,1)}, u32[]{:S(2)}) copy-start(bf16[1,128,1024]{2,1,0:T(8,128)(2,1)} %param.15) | copy-start | bytes 786436
  37.4 11.7 %all-to-all-start.1 = ((bf16[16,128,64]{1,2,0:T(8,128)(2,1)}), bf16[16,128,64]{1,2,0:T(8,128)(2,1)S(1)}, u32[]{:S(2)}, u32[]{:S(2)}) async-start(bf16[16,128,64]{1,2,0:T(8,128)(2,1)} %copy_bitcast_fusion.1), calls=%async_computation.1 | async-start | bytes 524288 | tf_op jit(solution)/shard_map/all_to_all | solution.py:333

commit v15 on v11

--- a/solution.py
+++ b/solution.py
@@ -115,6 +115,18 @@
     for copy in local_copies:
         copy.start()
     copies = []
+    for k in both_ways(expert_n):
+        peer = lax.rem(me_e + k, expert_n)
+        copy = pltpu.make_async_remote_copy(
+            src_ref=slots_ref.at[peer],
+            dst_ref=arrived_ref.at[me_e],
+            send_sem=send_sems.at[k],
+            recv_sem=recv_sems.at[k],
+            device_id={"expert": peer},
+            device_id_type=mesh_ids,
+        )
+        copy.start()
+        copies.append(copy)
     for k in range(1, half):
         for w in range(2):
             copy = pltpu.make_async_remote_copy(
@@ -127,18 +139,6 @@
             )
             copy.start()
             copies.append(copy)
-    for k in both_ways(expert_n):
-        peer = lax.rem(me_e + k, expert_n)
-        copy = pltpu.make_async_remote_copy(
-            src_ref=slots_ref.at[peer],
-            dst_ref=arrived_ref.at[me_e],
-            send_sem=send_sems.at[k],
-            recv_sem=recv_sems.at[k],
-            device_id={"expert": peer},
-            device_id_type=mesh_ids,
-        )
-        copy.start()
-        copies.append(copy)
     for copy in local_copies:
         copy.wait()
     forwards = []

time: 177 us -> 177 us (level)
  no operation moved by 1% of the time
where the time goes in v15:
time: 177 us
  Pallas kernels  118 us (67%)
  matrix products  17.3 us (10%)
  starting transfers between devices  15.4 us (9%)
  waiting for transfers between devices  15.3 us (9%)
  other arithmetic  5.8 us (3%)
  local copies, waits for them, and re-layouts  4.6 us (3%)
    pallas_call x1, Pallas kernels, dispatch(): pl.pallas_call(functools.partial(dispatch_kernel, expert_n, tm_n), out_sh...  62.1 us
    pallas_call x1, Pallas kernels, exchange(): pl.pallas_call(functools.partial(exchange_kernel, axis, n), out_shape=jax...  56.2 us
    all_to_all x1, waiting for transfers between devices, on_device(): lax.all_to_all(packed, 'tm', split_axis=0, concat_axis=0, tiled=True)  10.1 us
    all_to_all x1, starting transfers between devices, on_device(): lax.all_to_all(packed, 'tm', split_axis=0, concat_axis=0, tiled=True)  9.25 us
    all_to_all x1, starting transfers between devices, on_device(): lax.all_to_all(head_out, 'tm', split_axis=0, concat_axis=0, tiled=True)  6.14 us
    dot_general x1, matrix products, on_device(): jnp.dot(hidden, down_rows, preferred_element_type=jnp.float32)  6.02 us
    all_to_all x1, waiting for transfers between devices, on_device(): lax.all_to_all(head_out, 'tm', split_axis=0, concat_axis=0, tiled=True)  5.26 us
    dot_general x2, matrix products, head_attention(): jnp.dot(block, key_rows.T, preferred_element_type=jnp.float32)  4.14 us
  transfers between devices with their start and end apart: 2, of which 2 were waited for; matrix products, arithmetic and copies ran while one was open for 1% of the time, Pallas kernels for 0%

profile of v15, /device:TPU:8, one launch (start us, length us, event | category | flops | bytes accessed | tf_op | source)
XLA Modules:
  0.0 177.0 jit_solution(9624427070187045793)
XLA Ops:
  0.0 1.3 copy.26
  1.3 1.1 copy.27
  2.5 1.1 copy.28
  3.7 1.0 fusion.38
  4.7 9.3 %all-to-all-start = ((bf16[16,128,208]{1,2,0:T(8,128)(2,1)}), bf16[16,128,208]{1,2,0:T(8,128)(2,1)S(1)}, u32[]{:S(2)}, u32[]{:S(2)}) async-start(bf16[16,128,208]{1,2,0:T(8,128)(2,1)} %fusion.38), calls=%async_computation | async-start | bytes 1703936 | tf_op jit(solution)/shard_map/all_to_all | solution.py:251
  14.0 0.1 copy.31
  14.1 0.1 eq.73
  14.2 0.1 reshape_squeeze.11
  14.4 0.6 reduce-window.6
  15.0 0.2 slice_reduce_fusion
  15.2 0.1 fusion.56
  15.3 0.1 reduce_sum.71
  15.6 0.1 iota_compare_fusion.2
  15.7 10.1 %all-to-all-done = bf16[16,128,208]{1,2,0:T(8,128)(2,1)S(1)} async-done(((bf16[16,128,208]{1,2,0:T(8,128)(2,1)}), bf16[16,128,208]{1,2,0:T(8,128)(2,1)S(1)}, u32[]{:S(2)}, u32[]{:S(2)}) %all-to-all-start) | async-done | bytes 852000 | tf_op jit(solution)/shard_map/all_to_all | solution.py:251
  25.8 0.1 copy_bitcast_fusion
  25.9 1.4 add_reduce_fusion.1
  27.3 2.8 %fusion = (f32[1024]{0:T(1024)S(1)}, f32[1024]{0:T(1024)S(1)}, f32[1024,2048]{1,0:T(8,128)S(1)}) fusion(f32[1024,2048]{1,0:T(8,128)S(1)} %get-tuple-element.30, f32[1024]{0:T(1024)S(1)} %get-tuple-element.29, f32[2048]{0:T(1024)S(1)} %bitcast.79, bf16[2048,208]{0,1:T(8,128)(2,1)S(1)} %copy_bitcast_fusion), kind=kOutput, calls=%fused_computation.4 | convolution fusion | flops 278919168 | bytes 17190912 | tf_op jit(solution)/shard_map/dot_general | solution.py:18
  30.0 2.0 %fusion.2 = f32[1024]{0:T(1024)S(1)} fusion(f32[1024,2048]{1,0:T(8,128)S(1)} %get-tuple-element.31, f32[1024]{0:T(1024)S(1)} %get-tuple-element.24, f32[2048]{0:T(1024)S(1)} %bitcast.80), kind=kLoop, calls=%fused_computation.6 | loop fusion | flops 6290432 | bytes 8404992 | tf_op jit(solution)/shard_map/reduce_sum | solution.py:21
  32.0 1.7 fusion.29
  33.7 1.7 fusion.23
  35.3 0.8 copy_bitcast_fusion.1
  36.1 6.1 %all-to-all-start.1 = ((bf16[16,128,64]{1,2,0:T(8,128)(2,1)}), bf16[16,128,64]{1,2,0:T(8,128)(2,1)S(1)}, u32[]{:S(2)}, u32[]{:S(2)}) async-start(bf16[16,128,64]{1,2,0:T(8,128)(2,1)} %copy_bitcast_fusion.1), calls=%async_computation.1 | async-start | bytes 524288 | tf_op jit(solution)/shard_map/all_to_all | solution.py:260
  42.3 0.2 eq.79
  42.5 5.3 %all-to-all-done.1 = bf16[16,128,64]{1,2,0:T(8,128)(2,1)S(1)} async-done(((bf16[16,128,64]{1,2,0:T(8,128)(2,1)}), bf16[16,128,64]{1,2,0:T(8,128)(2,1)S(1)}, u32[]{:S(2)}, u32[]{:S(2)}) %all-to-all-start.1) | async-done | bytes 262176 | tf_op jit(solution)/shard_map/all_to_all | solution.py:260
  47.8 0.5 fusion.63
  48.3 0.2 multiply_reduce_fusion
  48.6 1.6 convolution_convert_fusion
  50.1 62.1 %shard_map.127 = (bf16[32,16,1024]{2,1,0:T(8,128)(2,1)}, bf16[2,8,64,1024]{3,2,1,0:T(8,128)(2,1)}, bf16[2,8,64,1024]{3,2,1,0:T(8,128)(2,1)}) custom-call(bf16[32,16,1024]{2,1,0:T(8,128)(2,1)} %bitcast.72, bf16[64,1024]{1,0:T(8,128)(2,1)} %bitcast.83, bf16[64,1024]{1,0:T(8,128)(2,1)} %bitcast.84), custom_call_target="tpu_custom_call" | custom-call | tf_op jit(solution)/shard_map/pallas_call | solution.py:193
  112.2 6.0 %convolution_convert_fusion.1 = bf16[512,1024]{1,0:T(8,128)(2,1)} fusion(bf16[1024,1024]{1,0:T(8,128)(2,1)} %bitcast.90, bf16[512,1024]{1,0:T(8,128)(2,1)} %bitcast.91, bf16[1024,1024]{1,0:T(8,128)(2,1)} %bitcast.89), kind=kOutput, calls=%fused_computation.22 | convolution fusion | flops 2152726528 | bytes 6291456 | tf_op jit(solution)/shard_map/dot_general | solution.py:297
  118.2 56.2 %shard_map.128 = bf16[32,16,1024]{2,1,0:T(8,128)(2,1)} custom-call(bf16[32,16,1024]{2,1,0:T(8,128)(2,1)} %bitcast.76), custom_call_target="tpu_custom_call" | custom-call | tf_op jit(solution)/shard_map/pallas_call | solution.py:76
  174.5 1.7 fusion.17
  176.2 0.8 fusion.42
  (31 shorter events, 0.4 us)
Async XLA Ops:
  0.0 47.8 %copy-start = (bf16[1024,1024]{1,0:T(8,128)(2,1)S(1)}, bf16[1024,1024]{1,0:T(8,128)(2,1)}, u32[]{:S(2)}) copy-start(bf16[1024,1024]{1,0:T(8,128)(2,1)} %param.21) | copy-start | bytes 6291460
  0.0 3.6 %copy-start.7 = (s32[1,128]{1,0:T(1,128)S(1)}, s32[1,128]{1,0:T(1,128)}, u32[]{:S(2)}) copy-start(s32[1,128]{1,0:T(1,128)} %param.19) | copy-start | bytes 1540
  0.0 3.6 %copy-start.5 = (bf16[16]{0:T(256)(128)(2,1)S(1)}, bf16[16]{0:T(256)(128)(2,1)}, u32[]{:S(2)}) copy-start(bf16[16]{0:T(256)(128)(2,1)} %param.20) | copy-start | bytes 100
  1.3 12.6 %copy-start.4 = (s32[1,128,2]{1,2,0:T(2,128)S(1)}, s32[1,128,2]{1,2,0:T(2,128)}, u32[]{:S(2)}) copy-start(s32[1,128,2]{1,2,0:T(2,128)} %param.24) | copy-start | bytes 3076
  3.6 11.9 %copy-start.2 = (f32[1,2,1024]{2,1,0:T(2,128)S(1)}, f32[1,2,1024]{2,1,0:T(2,128)}, u32[]{:S(2)}) copy-start(f32[1,2,1024]{2,1,0:T(2,128)} %param.23) | copy-start | bytes 24580
  4.7 21.1 %all-to-all-start = ((bf16[16,128,208]{1,2,0:T(8,128)(2,1)}), bf16[16,128,208]{1,2,0:T(8,128)(2,1)S(1)}, u32[]{:S(2)}, u32[]{:S(2)}) async-start(bf16[16,128,208]{1,2,0:T(8,128)(2,1)} %fusion.38), calls=%async_computation | async-start | bytes 1703936 | tf_op jit(solution)/shard_map/all_to_all | solution.py:251
  33.7 8.8 %copy-start.3 = (f32[1,2,1024]{2,1,0:T(2,128)S(1)}, f32[1,2,1024]{2,1,0:T(2,128)}, u32[]{:S(2)}) copy-start(f32[1,2,1024]{2,1,0:T(2,128)} %param.22) | copy-start | bytes 24580
  33.7 14.1 %copy-start.1 = (bf16[1,128,1024]{2,1,0:T(8,128)(2,1)S(1)}, bf16[1,128,1024]{2,1,0:T(8,128)(2,1)}, u32[]{:S(2)}) copy-start(bf16[1,128,1024]{2,1,0:T(8,128)(2,1)} %param.15) | copy-start | bytes 786436
  36.1 11.7 %all-to-all-start.1 = ((bf16[16,128,64]{1,2,0:T(8,128)(2,1)}), bf16[16,128,64]{1,2,0:T(8,128)(2,1)S(1)}, u32[]{:S(2)}, u32[]{:S(2)}) async-start(bf16[16,128,64]{1,2,0:T(8,128)(2,1)} %copy_bitcast_fusion.1), calls=%async_computation.1 | async-start | bytes 524288 | tf_op jit(solution)/shard_map/all_to_all | solution.py:260
  118.2 56.2 %copy-start.6 = (f32[1,128,2]{1,2,0:T(2,128)S(1)}, f32[1,128,2]{1,2,0:T(2,128)}, u32[]{:S(2)}) copy-start(f32[1,128,2]{1,2,0:T(2,128)} %param.25) | copy-start | bytes 3076

commit v16 on v11

--- a/solution.py
+++ b/solution.py
@@ -278,11 +278,12 @@
     )
     ranks = jnp.sum((jnp.cumsum(hits, axis=0) - 1) * hits, axis=1)
     target = choice_list * capacity + ranks
-    placing = (
-        jnp.arange(capacity * expert_count, dtype=jnp.int32)[:, None] == target[None, :]
-    ).astype(jnp.bfloat16)
-    token_placing = placing.reshape(capacity * expert_count, tok_rows, 2).sum(axis=2)
-    slots = jnp.dot(token_placing, normed, preferred_element_type=jnp.float32).astype(jnp.bfloat16)
+    slot_token = (
+        jnp.full((capacity * expert_count,), tok_rows, jnp.int32)
+        .at[target]
+        .set(jnp.arange(2 * tok_rows, dtype=jnp.int32) // 2)
+    )
+    slots = jnp.take(normed, slot_token, axis=0, mode="fill", fill_value=0)
     slots = slots.reshape(expert_count, capacity, model_width)
     arrived, gathered_up, gathered_down = dispatch(
         slots, jnp.transpose(up_weight[0]), down_weight[0], lax.axis_size("tm"), 2
@@ -297,12 +298,9 @@
     produced = jnp.dot(hidden, down_rows, preferred_element_type=jnp.float32).astype(jnp.bfloat16)
     produced = produced.reshape(source_count * local_experts, capacity, model_width)
     returned = exchange(produced, "expert", 3)
-    picked = jnp.einsum(
-        "sa,sd->ad",
-        placing,
-        returned.reshape(expert_count * capacity, model_width),
-        preferred_element_type=jnp.float32,
-    )
+    picked = jnp.take(
+        returned.reshape(expert_count * capacity, model_width), target, axis=0
+    ).astype(jnp.float32)
     picked = picked.reshape(tok_rows, 2, model_width)
     combined = jnp.sum(gate_values[0][:, :, None] * picked, axis=1)
     layer_out = (mixed + branch_gates[0, 1][None, :] * combined).astype(jnp.bfloat16)

time: 177 us -> 187 us (1.056)
  local copies, waits for them, and re-layouts: 4.6 us -> 13.1 us
  other arithmetic: 5.8 us -> 12.2 us
  matrix products: 17.3 us -> 14 us
    gather x0 -> x3, local copies, waits for them, and re-layouts: none -> 6.7 us  [the longest x2 3.91 us: on_device(): jnp.take(returned.reshape(expert_count * capacity, model_width), target,...]
    dot_general x2 -> x0, matrix products: 3.26 us -> none  [the longest x1 1.71 us: on_device(): jnp.einsum('sa,sd->ad', placing, returned.reshape(expert_count * capacity...]
    reduce_sum x1, other arithmetic: 0.06 us -> 2.72 us  [on_device(): combined = jnp.sum(gate_values[0][:, :, None] * picked, axis=1)]
    select_n x0 -> x4, other arithmetic: none -> 2.36 us  [the longest x2 2.35 us: on_device(): slots = jnp.take(normed, slot_token, axis=0, mode='fill', fill_value=0)]
  transfers between devices with their start and end apart: 2 -> 2, of which waited for: 2 -> 2; matrix products, arithmetic and copies ran while one was open for 1% -> 2% of each run, Pallas kernels for 0% -> 0%
where the time goes in v16:
time: 187 us
  Pallas kernels  118 us (63%)
  starting transfers between devices  15.4 us (8%)
  matrix products  14 us (7%)
  waiting for transfers between devices  13.6 us (7%)
  local copies, waits for them, and re-layouts  13.1 us (7%)
  other arithmetic  12.2 us (7%)
    pallas_call x1, Pallas kernels, dispatch(): pl.pallas_call(functools.partial(dispatch_kernel, expert_n, tm_n), out_sh...  62.1 us
    pallas_call x1, Pallas kernels, exchange(): pl.pallas_call(functools.partial(exchange_kernel, axis, n), out_shape=jax...  56.1 us
    all_to_all x1, starting transfers between devices, on_device(): lax.all_to_all(packed, 'tm', split_axis=0, concat_axis=0, tiled=True)  9.25 us
    all_to_all x1, waiting for transfers between devices, on_device(): lax.all_to_all(packed, 'tm', split_axis=0, concat_axis=0, tiled=True)  8.5 us
    all_to_all x1, starting transfers between devices, on_device(): lax.all_to_all(head_out, 'tm', split_axis=0, concat_axis=0, tiled=True)  6.14 us
    dot_general x1, matrix products, on_device(): jnp.dot(hidden, down_rows, preferred_element_type=jnp.float32)  5.98 us
    all_to_all x1, waiting for transfers between devices, on_device(): lax.all_to_all(head_out, 'tm', split_axis=0, concat_axis=0, tiled=True)  5.14 us
    dot_general x2, matrix products, head_attention(): jnp.dot(block, key_rows.T, preferred_element_type=jnp.float32)  4.12 us
  transfers between devices with their start and end apart: 2, of which 2 were waited for; matrix products, arithmetic and copies ran while one was open for 2% of the time, Pallas kernels for 0%

profile of v16, /device:TPU:8, one launch (start us, length us, event | category | flops | bytes accessed | tf_op | source)
XLA Modules:
  0.0 186.7 jit_solution(11304220801008108912)
XLA Ops:
  0.0 1.3 copy.27
  1.3 1.1 copy.28
  2.4 1.1 copy.29
  3.6 0.7 compare_bitcast_fusion
  4.2 0.7 broadcast_select_fusion.2
  5.0 1.0 fusion.37
  6.0 9.3 %all-to-all-start = ((bf16[16,128,208]{1,2,0:T(8,128)(2,1)}), bf16[16,128,208]{1,2,0:T(8,128)(2,1)S(1)}, u32[]{:S(2)}, u32[]{:S(2)}) async-start(bf16[16,128,208]{1,2,0:T(8,128)(2,1)} %fusion.37), calls=%async_computation | async-start | bytes 1703936 | tf_op jit(solution)/shard_map/all_to_all | solution.py:251
  15.6 0.6 reduce-window.6
  16.2 0.2 slice_reduce_fusion
  16.6 0.1 mul.119
  16.8 1.4 scatter_custom_fusion
  18.5 8.5 %all-to-all-done = bf16[16,128,208]{1,2,0:T(8,128)(2,1)S(1)} async-done(((bf16[16,128,208]{1,2,0:T(8,128)(2,1)}), bf16[16,128,208]{1,2,0:T(8,128)(2,1)S(1)}, u32[]{:S(2)}, u32[]{:S(2)}) %all-to-all-start) | async-done | bytes 852000 | tf_op jit(solution)/shard_map/all_to_all | solution.py:251
  27.1 1.4 add_reduce_fusion.1
  28.5 2.7 %fusion = (f32[1024]{0:T(1024)S(1)}, f32[1024]{0:T(1024)S(1)}, f32[1024,2048]{1,0:T(8,128)S(1)}) fusion(f32[1024,2048]{1,0:T(8,128)S(1)} %get-tuple-element.30, f32[1024]{0:T(1024)S(1)} %get-tuple-element.29, f32[2048]{0:T(1024)S(1)} %bitcast.79, bf16[2048,208]{0,1:T(8,128)(2,1)S(1)} %copy_bitcast_fusion), kind=kOutput, calls=%fused_computation.7 | convolution fusion | flops 278919168 | bytes 17190912 | tf_op jit(solution)/shard_map/dot_general | solution.py:18
  31.3 1.9 %fusion.2 = f32[1024]{0:T(1024)S(1)} fusion(f32[1024,2048]{1,0:T(8,128)S(1)} %get-tuple-element.31, f32[1024]{0:T(1024)S(1)} %get-tuple-element.24, f32[2048]{0:T(1024)S(1)} %bitcast.80), kind=kLoop, calls=%fused_computation.9 | loop fusion | flops 6290432 | bytes 8404992 | tf_op jit(solution)/shard_map/reduce_sum | solution.py:21
  33.2 1.7 fusion.28
  34.9 1.7 fusion.22
  36.6 0.8 copy_bitcast_fusion.1
  37.3 6.1 %all-to-all-start.1 = ((bf16[16,128,64]{1,2,0:T(8,128)(2,1)}), bf16[16,128,64]{1,2,0:T(8,128)(2,1)S(1)}, u32[]{:S(2)}, u32[]{:S(2)}) async-start(bf16[16,128,64]{1,2,0:T(8,128)(2,1)} %copy_bitcast_fusion.1), calls=%async_computation.1 | async-start | bytes 524288 | tf_op jit(solution)/shard_map/all_to_all | solution.py:260
  43.9 5.1 %all-to-all-done.1 = bf16[16,128,64]{1,2,0:T(8,128)(2,1)S(1)} async-done(((bf16[16,128,64]{1,2,0:T(8,128)(2,1)}), bf16[16,128,64]{1,2,0:T(8,128)(2,1)S(1)}, u32[]{:S(2)}, u32[]{:S(2)}) %all-to-all-start.1) | async-done | bytes 262176 | tf_op jit(solution)/shard_map/all_to_all | solution.py:260
  49.0 0.6 fusion.57
  49.6 0.2 multiply_reduce_fusion.1
  49.8 0.2 add_convert_fusion.1
  50.0 2.8 %gather_fusion = bf16[512,1024]{1,0:T(8,128)(2,1)} fusion(bf16[128,1024]{1,0:T(8,128)(2,1)S(1)} %add_convert_fusion.1, s32[1024]{0:T(1024)S(1)} %pad_clamp_fusion.1), kind=kCustom, calls=%fused_computation | custom fusion | bytes 2099200 | tf_op jit(solution)/shard_map/jit(_take)/gather | solution.py:286
  52.7 2.3 %broadcast_select_fusion.slots_ref = bf16[32,16,1024]{2,1,0:T(8,128)(2,1)} fusion(bf16[32,16,1024]{2,1,0:T(8,128)(2,1)} %bitcast.73, pred[32,16]{1,0:T(8,128)(4,1)S(1)} %broadcast_in_dim.67), kind=kLoop, calls=%fused_computation.37 | loop fusion | flops 524288 | bytes 2097664 | tf_op jit(solution)/shard_map/jit(_take)/select_n | solution.py:286
  55.1 62.1 %shard_map.127 = (bf16[32,16,1024]{2,1,0:T(8,128)(2,1)}, bf16[2,8,64,1024]{3,2,1,0:T(8,128)(2,1)}, bf16[2,8,64,1024]{3,2,1,0:T(8,128)(2,1)}) custom-call(bf16[32,16,1024]{2,1,0:T(8,128)(2,1)} %broadcast_select_fusion.slots_ref, bf16[64,1024]{1,0:T(8,128)(2,1)} %bitcast.83, bf16[64,1024]{1,0:T(8,128)(2,1)} %bitcast.84), custom_call_target="tpu_custom_call" | custom-call | tf_op jit(solution)/shard_map/pallas_call | solution.py:193
  117.2 6.0 %convolution_convert_fusion = bf16[512,1024]{1,0:T(8,128)(2,1)} fusion(bf16[1024,1024]{1,0:T(8,128)(2,1)} %bitcast.94, bf16[512,1024]{1,0:T(8,128)(2,1)} %bitcast.95, bf16[1024,1024]{1,0:T(8,128)(2,1)} %bitcast.93), kind=kOutput, calls=%fused_computation.24 | convolution fusion | flops 2152726528 | bytes 6291456 | tf_op jit(solution)/shard_map/dot_general | solution.py:298
  123.2 56.1 %shard_map.128 = bf16[32,16,1024]{2,1,0:T(8,128)(2,1)} custom-call(bf16[32,16,1024]{2,1,0:T(8,128)(2,1)} %bitcast.77), custom_call_target="tpu_custom_call" | custom-call | tf_op jit(solution)/shard_map/pallas_call | solution.py:76
  179.3 2.9 %gather_fusion.1 = bf16[256,1024]{1,0:T(8,128)(2,1)S(1)} fusion(bf16[512,1024]{1,0:T(8,128)(2,1)} %bitcast.72, s32[1024]{0:T(1024)S(1)} %pad_clamp_fusion), kind=kCustom, calls=%fused_computation.1 | custom fusion | bytes 1049600 | tf_op jit(solution)/shard_map/jit(_take)/gather | solution.py:301
  182.2 1.0 gather.15
  183.2 2.7 %multiply_reduce_fusion = f32[128,1024]{1,0:T(8,128)S(1)} fusion(bf16[128,2,1024]{2,1,0:T(2,128)(2,1)} %gather.15, pred[128,2]{1,0:T(8,128)(4,1)S(1)} %copy.37, f32[128,2]{1,0:T(8,128)S(1)} %copy.32), kind=kLoop, calls=%fused_computation.32 | loop fusion | flops 917504 | bytes 1049856 | tf_op jit(solution)/shard_map/reduce_sum | solution.py:305
  185.9 0.8 fusion.38
  (40 shorter events, 1.4 us)
Async XLA Ops:
  0.0 49.0 %copy-start = (bf16[1024,1024]{1,0:T(8,128)(2,1)S(1)}, bf16[1024,1024]{1,0:T(8,128)(2,1)}, u32[]{:S(2)}) copy-start(bf16[1024,1024]{1,0:T(8,128)(2,1)} %param.21) | copy-start | bytes 6291460
  0.0 15.2 %copy-start.2 = (s32[1,128,2]{1,2,0:T(2,128)S(1)}, s32[1,128,2]{1,2,0:T(2,128)}, u32[]{:S(2)}) copy-start(s32[1,128,2]{1,2,0:T(2,128)} %param.24) | copy-start | bytes 3076
  0.0 18.5 %copy-start.3 = (f32[1,2,1024]{2,1,0:T(2,128)S(1)}, f32[1,2,1024]{2,1,0:T(2,128)}, u32[]{:S(2)}) copy-start(f32[1,2,1024]{2,1,0:T(2,128)} %param.23) | copy-start | bytes 24580
  6.0 21.1 %all-to-all-start = ((bf16[16,128,208]{1,2,0:T(8,128)(2,1)}), bf16[16,128,208]{1,2,0:T(8,128)(2,1)S(1)}, u32[]{:S(2)}, u32[]{:S(2)}) async-start(bf16[16,128,208]{1,2,0:T(8,128)(2,1)} %fusion.37), calls=%async_computation | async-start | bytes 1703936 | tf_op jit(solution)/shard_map/all_to_all | solution.py:251
  34.9 8.8 %copy-start.5 = (f32[1,128,2]{1,2,0:T(2,128)S(1)}, f32[1,128,2]{1,2,0:T(2,128)}, u32[]{:S(2)}) copy-start(f32[1,128,2]{1,2,0:T(2,128)} %param.25) | copy-start | bytes 3076
  34.9 9.0 %copy-start.4 = (f32[1,2,1024]{2,1,0:T(2,128)S(1)}, f32[1,2,1024]{2,1,0:T(2,128)}, u32[]{:S(2)}) copy-start(f32[1,2,1024]{2,1,0:T(2,128)} %param.22) | copy-start | bytes 24580
  34.9 14.1 %copy-start.1 = (bf16[1,128,1024]{2,1,0:T(8,128)(2,1)S(1)}, bf16[1,128,1024]{2,1,0:T(8,128)(2,1)}, u32[]{:S(2)}) copy-start(bf16[1,128,1024]{2,1,0:T(8,128)(2,1)} %param.15) | copy-start | bytes 786436
  37.3 11.7 %all-to-all-start.1 = ((bf16[16,128,64]{1,2,0:T(8,128)(2,1)}), bf16[16,128,64]{1,2,0:T(8,128)(2,1)S(1)}, u32[]{:S(2)}, u32[]{:S(2)}) async-start(bf16[16,128,64]{1,2,0:T(8,128)(2,1)} %copy_bitcast_fusion.1), calls=%async_computation.1 | async-start | bytes 524288 | tf_op jit(solution)/shard_map/all_to_all | solution.py:260

commit v17 on v11

--- a/solution.py
+++ b/solution.py
@@ -233,14 +233,13 @@
     head_count = key_bias.shape[0]
     head_width = model_width // head_count
     score_scale = head_width ** (-0.5)
-    scaled_queries = queries[0] * jnp.asarray(score_scale, jnp.bfloat16)
     offsets = jnp.where(
         inpaint_mask[0][:, None] == 1, key_bias[None, :], jnp.zeros((), jnp.bfloat16)
     )
     offset_cols = jnp.zeros((tok_rows, head_count, 16), jnp.bfloat16).at[:, :, 0].set(offsets)
     packed = jnp.concatenate(
         [
-            scaled_queries.reshape(tok_rows, head_count, head_width),
+            queries[0].reshape(tok_rows, head_count, head_width),
             keys[0].reshape(tok_rows, head_count, head_width),
             values[0].reshape(tok_rows, head_count, head_width),
             offset_cols,
@@ -251,7 +250,7 @@
     gathered = lax.all_to_all(packed, "tm", split_axis=0, concat_axis=0, tiled=True)
     clip_rows = gathered.reshape(-1, 3 * head_width + 16)
     head_out = head_attention(
-        clip_rows[:, :head_width],
+        clip_rows[:, :head_width] * jnp.asarray(score_scale, jnp.bfloat16),
         clip_rows[:, head_width:2 * head_width],
         clip_rows[:, 2 * head_width:3 * head_width],
         clip_rows[:, 3 * head_width].astype(jnp.float32),

time: 177 us -> 179 us (1.011)
    unnamed x20 -> x16, local copies, waits for them, and re-layouts: 3.66 us -> 3.66 us
where the time goes in v17:
time: 179 us; the launch traced here: 178 us
  Pallas kernels  118 us (66%)
  matrix products  17.3 us (10%)
  starting transfers between devices  15.4 us (9%)
  waiting for transfers between devices  15.3 us (9%)
  other arithmetic  7.11 us (4%)
  local copies, waits for them, and re-layouts  4.6 us (3%)
    pallas_call x1, Pallas kernels, dispatch(): pl.pallas_call(functools.partial(dispatch_kernel, expert_n, tm_n), out_sh...  62.1 us
    pallas_call x1, Pallas kernels, exchange(): pl.pallas_call(functools.partial(exchange_kernel, axis, n), out_shape=jax...  56.3 us
    all_to_all x1, waiting for transfers between devices, on_device(): lax.all_to_all(packed, 'tm', split_axis=0, concat_axis=0, tiled=True)  10.1 us
    all_to_all x1, starting transfers between devices, on_device(): lax.all_to_all(packed, 'tm', split_axis=0, concat_axis=0, tiled=True)  9.25 us
    all_to_all x1, starting transfers between devices, on_device(): lax.all_to_all(head_out, 'tm', split_axis=0, concat_axis=0, tiled=True)  6.14 us
    dot_general x1, matrix products, on_device(): jnp.dot(hidden, down_rows, preferred_element_type=jnp.float32)  6.02 us
    all_to_all x1, waiting for transfers between devices, on_device(): lax.all_to_all(head_out, 'tm', split_axis=0, concat_axis=0, tiled=True)  5.26 us
    dot_general x2, matrix products, head_attention(): jnp.dot(block, key_rows.T, preferred_element_type=jnp.float32)  4.15 us
  transfers between devices with their start and end apart: 2, of which 2 were waited for; matrix products, arithmetic and copies ran while one was open for 1% of the time, Pallas kernels for 0%

profile of v17, /device:TPU:8, one launch (start us, length us, event | category | flops | bytes accessed | tf_op | source)
XLA Modules:
  0.0 178.3 jit_solution(15943057248992851206)
XLA Ops:
  0.0 1.3 copy.26
  1.3 1.1 copy.27
  2.4 1.1 copy.28
  3.6 0.7 compare_bitcast_fusion
  4.2 0.7 broadcast_select_fusion
  5.0 1.0 fusion.38
  5.9 9.3 %all-to-all-start = ((bf16[16,128,208]{1,2,0:T(8,128)(2,1)}), bf16[16,128,208]{1,2,0:T(8,128)(2,1)S(1)}, u32[]{:S(2)}, u32[]{:S(2)}) async-start(bf16[16,128,208]{1,2,0:T(8,128)(2,1)} %fusion.38), calls=%async_computation | async-start | bytes 1703936 | tf_op jit(solution)/shard_map/all_to_all | solution.py:250
  15.2 0.1 copy.31
  15.3 0.1 eq.73
  15.5 0.1 reshape_squeeze.15
  15.6 0.6 reduce-window.6
  16.2 0.2 slice_reduce_fusion
  16.5 0.1 reduce_sum.71
  16.8 0.1 iota_compare_fusion.2
  17.0 10.1 %all-to-all-done = bf16[16,128,208]{1,2,0:T(8,128)(2,1)S(1)} async-done(((bf16[16,128,208]{1,2,0:T(8,128)(2,1)}), bf16[16,128,208]{1,2,0:T(8,128)(2,1)S(1)}, u32[]{:S(2)}, u32[]{:S(2)}) %all-to-all-start) | async-done | bytes 852000 | tf_op jit(solution)/shard_map/all_to_all | solution.py:250
  27.2 1.4 add_reduce_fusion.1
  28.6 2.8 %fusion = (f32[1024]{0:T(1024)S(1)}, f32[1024]{0:T(1024)S(1)}, f32[1024,2048]{1,0:T(8,128)S(1)}) fusion(f32[1024,2048]{1,0:T(8,128)S(1)} %get-tuple-element.30, f32[1024]{0:T(1024)S(1)} %get-tuple-element.29, f32[2048]{0:T(1024)S(1)} %bitcast.79, bf16[2048,208]{0,1:T(8,128)(2,1)S(1)} %copy_bitcast_fusion, bf16[2048,64]{0,1:T(8,128)(2,1)S(1)} %slice_multiply_fusion), kind=kOutput, calls=%fused_computation.4 | convolution fusion | flops 278919168 | bytes 17190912 | tf_op jit(solution)/shard_map/dot_general | solution.py:18
  31.3 1.7 fusion.23
  33.0 2.0 %fusion.2 = f32[1024]{0:T(1024)S(1)} fusion(f32[1024,2048]{1,0:T(8,128)S(1)} %get-tuple-element.31, f32[1024]{0:T(1024)S(1)} %get-tuple-element.24, f32[2048]{0:T(1024)S(1)} %bitcast.81), kind=kLoop, calls=%fused_computation.6 | loop fusion | flops 6290432 | bytes 8404992 | tf_op jit(solution)/shard_map/reduce_sum | solution.py:21
  35.0 1.7 fusion.29
  36.6 0.8 copy_bitcast_fusion.1
  37.4 6.1 %all-to-all-start.1 = ((bf16[16,128,64]{1,2,0:T(8,128)(2,1)}), bf16[16,128,64]{1,2,0:T(8,128)(2,1)S(1)}, u32[]{:S(2)}, u32[]{:S(2)}) async-start(bf16[16,128,64]{1,2,0:T(8,128)(2,1)} %copy_bitcast_fusion.1), calls=%async_computation.1 | async-start | bytes 524288 | tf_op jit(solution)/shard_map/all_to_all | solution.py:259
  43.6 0.2 eq.79
  43.8 5.3 %all-to-all-done.1 = bf16[16,128,64]{1,2,0:T(8,128)(2,1)S(1)} async-done(((bf16[16,128,64]{1,2,0:T(8,128)(2,1)}), bf16[16,128,64]{1,2,0:T(8,128)(2,1)S(1)}, u32[]{:S(2)}, u32[]{:S(2)}) %all-to-all-start.1) | async-done | bytes 262176 | tf_op jit(solution)/shard_map/all_to_all | solution.py:259
  49.1 0.5 fusion.63
  49.6 0.2 multiply_reduce_fusion
  49.9 1.6 convolution_convert_fusion
  51.4 62.1 %shard_map.127 = (bf16[32,16,1024]{2,1,0:T(8,128)(2,1)}, bf16[2,8,64,1024]{3,2,1,0:T(8,128)(2,1)}, bf16[2,8,64,1024]{3,2,1,0:T(8,128)(2,1)}) custom-call(bf16[32,16,1024]{2,1,0:T(8,128)(2,1)} %bitcast.72, bf16[64,1024]{1,0:T(8,128)(2,1)} %bitcast.83, bf16[64,1024]{1,0:T(8,128)(2,1)} %bitcast.84), custom_call_target="tpu_custom_call" | custom-call | tf_op jit(solution)/shard_map/pallas_call | solution.py:193
  113.5 6.0 %convolution_convert_fusion.1 = bf16[512,1024]{1,0:T(8,128)(2,1)} fusion(bf16[1024,1024]{1,0:T(8,128)(2,1)} %bitcast.90, bf16[512,1024]{1,0:T(8,128)(2,1)} %bitcast.91, bf16[1024,1024]{1,0:T(8,128)(2,1)} %bitcast.89), kind=kOutput, calls=%fused_computation.22 | convolution fusion | flops 2152726528 | bytes 6291456 | tf_op jit(solution)/shard_map/dot_general | solution.py:296
  119.5 56.3 %shard_map.128 = bf16[32,16,1024]{2,1,0:T(8,128)(2,1)} custom-call(bf16[32,16,1024]{2,1,0:T(8,128)(2,1)} %bitcast.76), custom_call_target="tpu_custom_call" | custom-call | tf_op jit(solution)/shard_map/pallas_call | solution.py:76
  175.8 1.7 fusion.17
  177.5 0.8 fusion.42
  (27 shorter events, 0.5 us)
Async XLA Ops:
  0.0 49.1 %copy-start = (bf16[1024,1024]{1,0:T(8,128)(2,1)S(1)}, bf16[1024,1024]{1,0:T(8,128)(2,1)}, u32[]{:S(2)}) copy-start(bf16[1024,1024]{1,0:T(8,128)(2,1)} %param.21) | copy-start | bytes 6291460
  1.3 13.9 %copy-start.4 = (s32[1,128,2]{1,2,0:T(2,128)S(1)}, s32[1,128,2]{1,2,0:T(2,128)}, u32[]{:S(2)}) copy-start(s32[1,128,2]{1,2,0:T(2,128)} %param.24) | copy-start | bytes 3076
  3.5 13.2 %copy-start.2 = (f32[1,2,1024]{2,1,0:T(2,128)S(1)}, f32[1,2,1024]{2,1,0:T(2,128)}, u32[]{:S(2)}) copy-start(f32[1,2,1024]{2,1,0:T(2,128)} %param.23) | copy-start | bytes 24580
  5.9 21.1 %all-to-all-start = ((bf16[16,128,208]{1,2,0:T(8,128)(2,1)}), bf16[16,128,208]{1,2,0:T(8,128)(2,1)S(1)}, u32[]{:S(2)}, u32[]{:S(2)}) async-start(bf16[16,128,208]{1,2,0:T(8,128)(2,1)} %fusion.38), calls=%async_computation | async-start | bytes 1703936 | tf_op jit(solution)/shard_map/all_to_all | solution.py:250
  35.0 8.8 %copy-start.3 = (f32[1,2,1024]{2,1,0:T(2,128)S(1)}, f32[1,2,1024]{2,1,0:T(2,128)}, u32[]{:S(2)}) copy-start(f32[1,2,1024]{2,1,0:T(2,128)} %param.22) | copy-start | bytes 24580
  35.0 14.1 %copy-start.1 = (bf16[1,128,1024]{2,1,0:T(8,128)(2,1)S(1)}, bf16[1,128,1024]{2,1,0:T(8,128)(2,1)}, u32[]{:S(2)}) copy-start(bf16[1,128,1024]{2,1,0:T(8,128)(2,1)} %param.15) | copy-start | bytes 786436
  37.4 11.7 %all-to-all-start.1 = ((bf16[16,128,64]{1,2,0:T(8,128)(2,1)}), bf16[16,128,64]{1,2,0:T(8,128)(2,1)S(1)}, u32[]{:S(2)}, u32[]{:S(2)}) async-start(bf16[16,128,64]{1,2,0:T(8,128)(2,1)} %copy_bitcast_fusion.1), calls=%async_computation.1 | async-start | bytes 524288 | tf_op jit(solution)/shard_map/all_to_all | solution.py:259
  119.5 56.3 %copy-start.5 = (f32[1,128,2]{1,2,0:T(2,128)S(1)}, f32[1,128,2]{1,2,0:T(2,128)}, u32[]{:S(2)}) copy-start(f32[1,128,2]{1,2,0:T(2,128)} %param.25) | copy-start | bytes 3076
